TPU v7x, 128 devices: a whole 4x4x4 slice. The times are simulated.
128 devices in a mesh: row: 8 (over y, z_hi), col: 16 (over z_lo, x, core).
Axes of the slice: x: 4, y: 4, z: 4 (z_hi: 2, z_lo: 2; z = z_hi * 2 + z_lo), core: 2. Of those that a mesh axis runs over, the one named last changes fastest.
Arguments:
- measurement_tiling_settings: bfloat16 [65536, 40], P(('row', 'col')), may hold values from -4.875 to 4.875
- dest: int32 [65536], P(('row', 'col')), may hold values from 0 to 65535, as said below
- column_tiling_settings: bfloat16 [32768, 40], P('col'), may hold values from -4.875 to 4.875
- entry_layer_weight: bfloat16 [40, 2048], replicated, may hold values from -1 to 1
- entry_layer_bias: float32 [2048], replicated, may hold values from -3 to 3
- middle_layer_weight: bfloat16 [2048, 2048], replicated, may hold values from -0.1875 to 0.1875
- middle_layer_bias: float32 [2048], replicated, may hold values from -3 to 3
- output_layer_weight: bfloat16 [2048, 256], replicated, may hold values from -0.1875 to 0.1875
- relevance_weight_vector: float32 [256], replicated, may hold values from 0.015625 to 0.03125
- probes: float32 [32768, 64], P('col'), may hold values from -1.3258252 to 1.3258252
Outputs:
- product: float32 [65536, 64], P(('row', 'col'))
Inputs may be any that keep to these rules, and one draw needn't show every extreme that they name: dest is a permutation of 0 to 65535, and the measurements held by one device go in equal numbers to the row positions of every device, 4 to each.
All inputs are finite; a program needn't handle non-finite values.
Results may differ from a plain program's by a relative error of at most 0.0088.
Values may be sent and summed in bfloat16 or wider, within the bound.
No kernel may reach another device: no remote copies, remote signals or barrier semaphores. Data moves between devices by JAX's collectives and lax.ppermute only.
A program may use at most 64 MiB of HBM per device.

v0:
```python
import functools

import jax
import jax.numpy as jnp
from jax import lax
from jax.experimental import pallas as pl
from jax.experimental.pallas import tpu as pltpu
from jax.sharding import Mesh, PartitionSpec as P


f32 = jnp.float32
bf16 = jnp.bfloat16
NT = (((1,), (1,)), ((), ()))
TN = (((0,), (0,)), ((), ()))
ALL = ("y", "zh", "zl", "x", "core")
COL = ("zl", "x", "core")
LOG2E = 1.4426950408889634
ROWS = 512
FEAT = 256
UNIT = 512
PAIR = 2560


def dot(a, b):
    return jnp.dot(a, b, preferred_element_type=f32)


def send_kernel(dest_ref, xt_ref, o_ref):
    d_row = dest_ref[...]
    d_f = d_row.astype(f32)
    d_col = jnp.transpose(jnp.broadcast_to(d_f, (128, ROWS)))
    before = jnp.concatenate([d_col] * (ROWS // 128), axis=1) < d_f
    rank = jnp.sum(jnp.where(before, 1.0, 0.0), axis=0, keepdims=True)
    place = lax.broadcasted_iota(jnp.int32, (ROWS, ROWS), 0).astype(f32) == rank
    place = jnp.where(place, 1.0, 0.0).astype(bf16)
    pos = jnp.bitwise_and(d_row, ROWS - 1)
    high = jnp.right_shift(pos, 4).astype(f32)
    low = jnp.bitwise_and(pos, 15).astype(f32)
    line = lax.broadcasted_iota(jnp.int32, (88, ROWS), 0)
    extra = jnp.where(line == 0, high, jnp.where(line == 1, low, 0.0))
    ext = jnp.concatenate([xt_ref[...].astype(f32), extra], axis=0).astype(bf16)
    o_ref[...] = lax.dot_general(place, ext, NT, preferred_element_type=f32).astype(bf16)


def send_rows(dest, x_t):
    return pl.pallas_call(
        send_kernel,
        out_shape=jax.ShapeDtypeStruct((ROWS, 128), bf16),
        name="send_rows",
    )(dest.reshape(1, ROWS), x_t)


def mlp_tail(h1, w2_ref, b2_ref, w3_ref, o_ref, acc, steps):
    i = pl.program_id(0)
    h2 = jnp.maximum(dot(h1[...], w2_ref[...]) + b2_ref[...], 0.0).astype(bf16)
    part = dot(h2, w3_ref[...])

    @pl.when(i == 0)
    def _():
        acc[...] = part

    @pl.when(i > 0)
    def _():
        acc[...] += part

    @pl.when(i == steps - 1)
    def _():
        o_ref[...] = acc[...].astype(bf16)


def col_kernel(y_ref, xt_ref, p_ref, w1_ref, b1_ref, w2_ref, b2_ref, w3_ref, o_ref, q_ref, h1, acc, *, steps):
    @pl.when(pl.program_id(0) == 0)
    def _():
        x = lax.dot_general(xt_ref[...], w1_ref[...], TN, preferred_element_type=f32)
        h1[...] = jnp.maximum(x + b1_ref[...], 0.0).astype(bf16)
        for j in range(8):
            q_ref[j * 64 : (j + 1) * 64, :] = p_ref[:, j * 256 : (j + 1) * 256].astype(bf16)

    mlp_tail(h1, w2_ref, b2_ref, w3_ref, o_ref, acc, steps)


def row_kernel(r_ref, w1_ref, b1_ref, w2_ref, b2_ref, w3_ref, o_ref, h1, acc, *, steps):
    @pl.when(pl.program_id(0) == 0)
    def _():
        got = r_ref[...]
        lane = lax.broadcasted_iota(jnp.int32, (8, 128), 1)
        pick = jnp.where(lane == 40, 16.0, jnp.where(lane == 41, 1.0, 0.0)).astype(bf16)
        pos = lax.dot_general(pick, got, NT, preferred_element_type=f32)[0:1, :]
        place = lax.broadcasted_iota(jnp.int32, (ROWS, ROWS), 0).astype(f32) == pos
        place = jnp.where(place, 1.0, 0.0).astype(bf16)
        x = dot(place, got).astype(bf16)[:, :40]
        h1[...] = jnp.maximum(dot(x, w1_ref[...]) + b1_ref[...], 0.0).astype(bf16)

    mlp_tail(h1, w2_ref, b2_ref, w3_ref, o_ref, acc, steps)


def weight_specs(w1, hid, bn, ft):
    return [
        pl.BlockSpec(w1.shape, lambda i, *_: (0, 0)),
        pl.BlockSpec((1, hid), lambda i, *_: (0, 0)),
        pl.BlockSpec((hid, bn), lambda i, *_: (0, i)),
        pl.BlockSpec((1, bn), lambda i, *_: (0, i)),
        pl.BlockSpec((bn, ft), lambda i, *_: (i, 0)),
    ]


def col_net(y, x_t, p_t, w1, b1, w2, b2, w3, bn=512):
    hid, ft = w2.shape[0], w3.shape[1]
    steps = hid // bn
    spec = pltpu.PrefetchScalarGridSpec(
        num_scalar_prefetch=1,
        grid=(steps,),
        in_specs=[
            pl.BlockSpec((40, UNIT), lambda i, y: (0, y[0])),
            pl.BlockSpec((64, 2048), lambda i, y: (0, 0)),
            *weight_specs(w1, hid, bn, ft),
        ],
        out_specs=[
            pl.BlockSpec((UNIT, ft), lambda i, y: (0, 0)),
            pl.BlockSpec((UNIT, ft), lambda i, y: (0, 0)),
        ],
        scratch_shapes=[pltpu.VMEM((UNIT, hid), bf16), pltpu.VMEM((UNIT, ft), f32)],
    )
    return pl.pallas_call(
        functools.partial(col_kernel, steps=steps),
        grid_spec=spec,
        out_shape=[jax.ShapeDtypeStruct((UNIT, ft), bf16)] * 2,
        name="col_net",
    )(y, x_t, p_t, w1, b1.reshape(1, -1), w2, b2.reshape(1, -1), w3)


def row_net(got, w1, b1, w2, b2, w3, bn=512):
    hid, ft = w2.shape[0], w3.shape[1]
    steps = hid // bn
    return pl.pallas_call(
        functools.partial(row_kernel, steps=steps),
        grid=(steps,),
        in_specs=[pl.BlockSpec((ROWS, 128), lambda i: (0, 0)), *weight_specs(w1, hid, bn, ft)],
        out_specs=pl.BlockSpec((ROWS, ft), lambda i: (0, 0)),
        out_shape=jax.ShapeDtypeStruct((ROWS, ft), bf16),
        scratch_shapes=[pltpu.VMEM((ROWS, hid), bf16), pltpu.VMEM((ROWS, ft), f32)],
        name="row_net",
    )(got, w1, b1.reshape(1, -1), w2, b2.reshape(1, -1), w3)


def rbf_kernel(off_ref,rel_ref,*refs,nr,pairs,with_init,bm,cs,ug):
    rows=refs[:nr]; refs=refs[nr:]
    cols=refs[:2*pairs]; refs=refs[2*pairs:]
    if with_init: init_ref,refs=refs[0],refs[1:]
    outs=refs[:nr]; refs=refs[nr:]
    sc,sqr,cv,sv,kv,acc,sem=refs
    m=nr*ROWS

    def copies(p,a,b):
        return (pltpu.make_async_copy(a,cv.at[pl.ds(pl.multiple_of(p*PAIR,PAIR),1536)],sem.at[2*p]),
                pltpu.make_async_copy(b,cv.at[pl.ds(pl.multiple_of(p*PAIR+1536,512),1024)],sem.at[2*p+1]))

    for p in range(pairs):
        for c in copies(p,cols[2*p],cols[2*p+1]): c.start()
    rel=rel_ref[...]
    ones=jnp.ones((8,FEAT),bf16)
    for j in range(nr):
        at=slice(j*ROWS,(j+1)*ROWS)
        rf=rows[j][...].astype(f32)
        sc[at,:]=(rf*(rel*LOG2E)).astype(bf16)
        w=rel*rf*rf
        hi=w.astype(bf16); lo=(w-hi.astype(f32)).astype(bf16)
        sqr[:,at]=(-0.5*LOG2E)*(lax.dot_general(ones,hi,NT,preferred_element_type=f32)+lax.dot_general(ones,lo,NT,preferred_element_type=f32))
        acc[:,at]=init_ref[...] if with_init else jnp.zeros((64,ROWS),f32)

    def body(p,_):
        for c in copies(p,cols[0],cols[1]): c.wait()
        starts=[pl.multiple_of(p*PAIR+(0 if u==0 else 512+u*512),512) for u in range(4)]
        for u0 in range(0,4,ug):
            us=range(u0,u0+ug)
            for u in us:
                c=cv[pl.ds(starts[u],UNIT),:].astype(f32)
                sv[u*UNIT:(u+1)*UNIT,:]=jnp.broadcast_to((-0.5*LOG2E)*jnp.sum(rel*c*c,axis=1,keepdims=True),(UNIT,128))
            prs=[]
            for u in us:
                st=pl.multiple_of(p*PAIR+512+off_ref[u]*128,128)
                prs+=[cv[pl.ds(st,64),:],cv[pl.ds(st+64,64),:]]
            pr=jnp.concatenate(prs,axis=1)
            for r in range(0,m,bm):
                for u in us:
                    for b in range(0,UNIT,cs):
                        s=lax.dot_general(cv[pl.ds(starts[u]+b,cs),:],sc[r:r+bm,:],NT,preferred_element_type=f32)
                        q=sv[u*UNIT+b:u*UNIT+b+cs,:]
                        q=jnp.concatenate([q]*(bm//128),axis=1)
                        kv[u*UNIT+b:u*UNIT+b+cs,r:r+bm]=jnp.exp2(s+(q+sqr[0:1,r:r+bm])).astype(bf16)
                acc[:,r:r+bm]+=jnp.dot(pr,kv[u0*UNIT:(u0+ug)*UNIT,r:r+bm],preferred_element_type=f32)
        return 0

    lax.fori_loop(0,pairs,body,0)
    for j in range(nr): outs[j][...]=acc[:,j*ROWS:(j+1)*ROWS].astype(outs[j].dtype)


def rbf(off,rel,rows,pairs,init=None,out=f32,bm=256,cs=512,ug=4):
    nr=len(rows)
    args=list(rows)+[x for p in pairs for x in p]+([init] if init is not None else [])
    V=pl.BlockSpec(memory_space=pltpu.VMEM); A=pl.BlockSpec(memory_space=pl.ANY)
    npairs=len(pairs); m=nr*ROWS
    return pl.pallas_call(functools.partial(rbf_kernel,nr=nr,pairs=npairs,with_init=init is not None,bm=bm,cs=cs,ug=ug),
        in_specs=[pl.BlockSpec(memory_space=pltpu.SMEM),V]+[V]*nr+[A]*(2*npairs)+([V] if init is not None else []),
        out_specs=[V]*nr,out_shape=[jax.ShapeDtypeStruct((64,ROWS),out)]*nr,
        scratch_shapes=[pltpu.VMEM((m,FEAT),bf16),pltpu.VMEM((8,m),f32),pltpu.VMEM((npairs*PAIR,FEAT),bf16),pltpu.VMEM((2048,128),f32),
          pltpu.VMEM((2048,m),bf16),pltpu.VMEM((64,m),f32),pltpu.SemaphoreType.DMA((2*npairs,))])(off,rel,*args)


def ring(shift):
    return [(i, (i + shift) % 4) for i in range(4)]


Z = ("zh", "zl")
SWAP = [(0, 1), (1, 0)]


def steps(x_m, dest, x_c, w1, b1, w2, b2, w3, rel, probes):
    rel = rel.reshape(1, FEAT)
    y = lax.axis_index("y").astype(jnp.int32)
    off = jnp.stack([y, (y + 3) % 4, (y + 1) % 4, (y + 2) % 4]).astype(jnp.int32)
    sent = send_rows(dest, x_m.T)
    own, probe = col_net(y.reshape(1), x_c.T, probes.T, w1, b1, w2, b2, w3)
    sent, own = lax.optimization_barrier((sent, own))
    u1 = lax.ppermute(own, "y", ring(1))
    u3 = lax.ppermute(own, "y", ring(3))
    u2 = lax.ppermute(own, "y", ring(2))
    got = lax.all_to_all(sent, ALL, 0, 0, tiled=True)
    u1, u3, u2, got = lax.optimization_barrier((u1, u3, u2, got))
    feats = row_net(got, w1, b1, w2, b2, w3)
    ca = jnp.concatenate([own, probe, u1], 0)
    cb = jnp.concatenate([u3, u2], 0)
    za = lax.ppermute(ca, Z, ring(1))
    zb = lax.ppermute(cb, Z, ring(3))
    pa = lax.ppermute(ca, "core", SWAP)
    pb = lax.ppermute(cb, "core", SWAP)
    f1 = lax.ppermute(feats, "x", ring(1))
    f3 = lax.ppermute(feats, "x", ring(3))
    f2 = lax.ppermute(feats, "x", ring(2))
    near = [(ca, cb), (pa, pb)]
    (first,) = rbf(off, rel, [feats], near, bm=512)
    za, zb, first = lax.optimization_barrier((za, zb, first))
    pza = lax.ppermute(za, "core", SWAP)
    pzb = lax.ppermute(zb, "core", SWAP)
    far = [(za, zb), (pza, pzb)]
    t1, t3 = rbf(off, rel, [f1, f3], near + far, out=bf16)
    r1 = lax.ppermute(t1, "x", ring(3))
    r3 = lax.ppermute(t3, "x", ring(1))
    (t2,) = rbf(off, rel, [f2], near + far, out=bf16, bm=512)
    r2 = lax.ppermute(t2, "x", ring(2))
    (mine,) = rbf(off, rel, [feats], far, first, bm=512)
    total = mine + r1.astype(f32) + r3.astype(f32) + r2.astype(f32)
    return total.T


def solution(mesh):
    fine = Mesh(mesh.devices.reshape(4, 2, 2, 4, 2), ALL)
    placed = (P(ALL, None), P(ALL), P(COL, None), P(), P(), P(), P(), P(), P(), P(COL, None))
    return jax.shard_map(steps, mesh=fine, in_specs=placed, out_specs=P(ALL, None), check_vma=False)
```

profile of v0, /device:TPU:0, one launch (start us, length us, event | category | flops | bytes accessed | tf_op | source)
XLA Modules:
  0.0 107.7 jit_solution(7111946154181711945)
XLA Ops:
  0.0 1.9 %send_rows.1 = bf16[512,128]{1,0:T(8,128)(2,1)} custom-call(s32[1,512]{1,0:T(1,128)} %bitcast.27, bf16[40,512]{1,0:T(8,128)(2,1)} %bitcast.18), custom_call_target="tpu_custom_call" | custom-call | tf_op jit(solution)/shard_map/send_rows/pallas_call | solution.py:46
  1.9 10.4 %col_net.1 = (bf16[512,256]{1,0:T(8,128)(2,1)}, bf16[512,256]{1,0:T(8,128)(2,1)}) custom-call(s32[1]{0:T(128)} %bitcast.y_ref, bf16[40,2048]{1,0:T(8,128)(2,1)} %bitcast.17, f32[64,2048]{1,0:T(8,128)} %bitcast.16, bf16[40,2048]{1,0:T(8,128)(2,1)} %w1_ref.3, f32[1,2048]{1,0:T(1,128)} %bitcast.19, bf16[2048,2048]{1,0:T(8,128)(2,1)} %w2_ref.3, ...), custom_call_target="tpu_custom_call" | custom-call | tf_op jit(solution)/shard_map/col_net/pallas_call | solution.py:124
  12.3 1.7 %collective-permute-start = (bf16[512,256]{1,0:T(8,128)(2,1)}, bf16[512,256]{1,0:T(8,128)(2,1)S(1)}, u32[]{:S(2)}, u32[]{:S(2)}) collective-permute-start(bf16[512,256]{1,0:T(8,128)(2,1)} %get-tuple-element.19), channel_id=1, source_target_pairs={{0,32},{32,64},{64,96},{96,0},{1,33},{33,65},{65,97},{97,1},{2,34}... | collective-permute-start | bytes 786440 | tf_op jit(solution)/shard_map/ppermute | solution.py:225
  14.0 1.5 %collective-permute-start.1 = (bf16[512,256]{1,0:T(8,128)(2,1)}, bf16[512,256]{1,0:T(8,128)(2,1)S(1)}, u32[]{:S(2)}, u32[]{:S(2)}) collective-permute-start(bf16[512,256]{1,0:T(8,128)(2,1)} %get-tuple-element.19), channel_id=1, source_target_pairs={{0,96},{32,0},{64,32},{96,64},{1,97},{33,1},{65,33},{97,65},{2,98}... | collective-permute-start | bytes 786440 | tf_op jit(solution)/shard_map/ppermute | solution.py:226
  15.6 2.1 %collective-permute-start.2 = (bf16[512,256]{1,0:T(8,128)(2,1)}, bf16[512,256]{1,0:T(8,128)(2,1)S(1)}, u32[]{:S(2)}, u32[]{:S(2)}) collective-permute-start(bf16[512,256]{1,0:T(8,128)(2,1)} %get-tuple-element.19), channel_id=1, source_target_pairs={{0,64},{32,96},{64,0},{96,32},{1,65},{33,97},{65,1},{97,33},{2,66}... | collective-permute-start | bytes 786440 | tf_op jit(solution)/shard_map/ppermute | solution.py:227
  17.7 9.4 %all-to-all-start = ((bf16[128,4,128]{2,1,0:T(4,128)(2,1)}), bf16[128,4,128]{2,1,0:T(4,128)(2,1)S(1)}, u32[]{:S(2)}, u32[]{:S(2)}) async-start(bf16[128,4,128]{2,1,0:T(4,128)(2,1)} %bitcast.11), calls=%async_computation | async-start | bytes 262144 | tf_op jit(solution)/shard_map/all_to_all | solution.py:228
  27.1 1.0 constant_dynamic-update-slice_fusion.2
  28.0 1.0 constant_dynamic-update-slice_fusion.1
  29.0 7.4 %all-to-all-done = bf16[128,4,128]{2,1,0:T(4,128)(2,1)S(1)} async-done(((bf16[128,4,128]{2,1,0:T(4,128)(2,1)}), bf16[128,4,128]{2,1,0:T(4,128)(2,1)S(1)}, u32[]{:S(2)}, u32[]{:S(2)}) %all-to-all-start) | async-done | bytes 131104 | tf_op jit(solution)/shard_map/all_to_all | solution.py:228
  36.6 0.8 collective-permute-start.3
  37.5 0.2 collective-permute-start.6
  37.7 2.5 %collective-permute-start.4 = (bf16[1024,256]{1,0:T(8,128)(2,1)S(1)}, bf16[1024,256]{1,0:T(8,128)(2,1)S(1)}, u32[]{:S(2)}, u32[]{:S(2)}) collective-permute-start(bf16[1024,256]{1,0:T(8,128)(2,1)S(1)} %constant_dynamic-update-slice_fusion.3.refs_2_.refs_3_), channel_id=1, source_target_pairs={{0,24},{8,0},{16,8},{24,16},{1,25},{9,1},{17,9},{25,17},{2,26},{10... | collective-permute-start | bytes 1572872 | tf_op jit(solution)/shard_map/ppermute | solution.py:234
  40.2 0.6 pad_add_fusion.off_ref
  40.8 10.0 %row_net.1.refs_0_ = bf16[512,256]{1,0:T(8,128)(2,1)} custom-call(bf16[512,128]{1,0:T(8,128)(2,1)} %bitcast.15, bf16[40,2048]{1,0:T(8,128)(2,1)} %w1_ref.3, f32[1,2048]{1,0:T(1,128)} %bitcast.20, bf16[2048,2048]{1,0:T(8,128)(2,1)} %w2_ref.3, f32[1,2048]{1,0:T(1,128)} %bitcast.22, bf16[2048,256]{1,0:T(8,128)(2,1)} %w3_ref.3), custom_call_target="tpu_custom_call" | custom-call | tf_op jit(solution)/shard_map/row_net/pallas_call | solution.py:135
  50.8 0.8 copy-done.2
  51.6 5.5 %shard_map.100.refs_5_ = f32[64,512]{1,0:T(8,128)} custom-call(s32[4]{0:T(128)} %pad_add_fusion.off_ref, f32[1,256]{1,0:T(1,128)} %bitcast.23, bf16[512,256]{1,0:T(8,128)(2,1)} %row_net.1.refs_0_, bf16[1536,256]{1,0:T(8,128)(2,1)} %copy-done, bf16[1024,256]{1,0:T(8,128)(2,1)} %copy-done.4, bf16[1536,256]{1,0:T(8,128)(2,1)} %copy-done.2, ...), custom_call_target="tpu_custom_call" | custom-call | tf_op jit(solution)/shard_map/pallas_call | solution.py:203
  57.1 0.6 collective-permute-done.3.refs_1_.refs_6_.refs_5_
  57.8 0.5 collective-permute-start.8
  58.3 1.3 %collective-permute-start.10 = (bf16[512,256]{1,0:T(8,128)(2,1)}, bf16[512,256]{1,0:T(8,128)(2,1)S(1)}, u32[]{:S(2)}, u32[]{:S(2)}) collective-permute-start(bf16[512,256]{1,0:T(8,128)(2,1)} %row_net.1.refs_0_), channel_id=1, source_target_pairs={{0,6},{2,0},{4,2},{6,4},{1,7},{3,1},{5,3},{7,5},{8,14},{10,8},{12,... | collective-permute-start | bytes 786440 | tf_op jit(solution)/shard_map/ppermute | solution.py:238
  59.5 0.8 collective-permute-start.9
  60.3 1.2 %collective-permute-start.13 = (bf16[512,256]{1,0:T(8,128)(2,1)}, bf16[512,256]{1,0:T(8,128)(2,1)S(1)}, u32[]{:S(2)}, u32[]{:S(2)}) collective-permute-start(bf16[512,256]{1,0:T(8,128)(2,1)} %row_net.1.refs_0_), channel_id=1, source_target_pairs={{0,4},{2,6},{4,0},{6,2},{1,5},{3,7},{5,1},{7,3},{8,12},{10,14},{12... | collective-permute-start | bytes 786440 | tf_op jit(solution)/shard_map/ppermute | solution.py:239
  61.5 6.2 %collective-permute-done.10.refs_1_ = bf16[512,256]{1,0:T(8,128)(2,1)S(1)} collective-permute-done((bf16[512,256]{1,0:T(8,128)(2,1)}, bf16[512,256]{1,0:T(8,128)(2,1)S(1)}, u32[]{:S(2)}, u32[]{:S(2)}) %collective-permute-start.10) | collective-permute-done | bytes 262176 | tf_op jit(solution)/shard_map/ppermute | solution.py:238
  67.7 6.8 %collective-permute-done.9.refs_0_ = bf16[512,256]{1,0:T(8,128)(2,1)S(1)} collective-permute-done((bf16[512,256]{1,0:T(8,128)(2,1)}, bf16[512,256]{1,0:T(8,128)(2,1)S(1)}, u32[]{:S(2)}, u32[]{:S(2)}) %collective-permute-start.9) | collective-permute-done | bytes 262176 | tf_op jit(solution)/shard_map/ppermute | solution.py:237
  74.5 0.7 copy-done.10
  75.4 0.9 copy-done.3
  76.3 12.9 %shard_map.102 = (bf16[64,512]{1,0:T(8,128)(2,1)}, bf16[64,512]{1,0:T(8,128)(2,1)}) custom-call(s32[4]{0:T(128)} %pad_add_fusion.off_ref, f32[1,256]{1,0:T(1,128)} %bitcast.24, bf16[512,256]{1,0:T(8,128)(2,1)} %copy-done.10, bf16[512,256]{1,0:T(8,128)(2,1)} %copy-done.9, bf16[1536,256]{1,0:T(8,128)(2,1)} %copy-done, bf16[1024,256]{1,0:T(8,128)(2,1)} %copy-done.4, ...), custom_call_target="tpu_custom_call" | custom-call | tf_op jit(solution)/shard_map/pallas_call | solution.py:203
  89.3 2.0 %collective-permute-start.12 = (bf16[64,512]{1,0:T(8,128)(2,1)}, bf16[64,512]{1,0:T(8,128)(2,1)S(1)}, u32[]{:S(2)}, u32[]{:S(2)}) collective-permute-start(bf16[64,512]{1,0:T(8,128)(2,1)} %get-tuple-element.30), channel_id=1, source_target_pairs={{0,2},{2,4},{4,6},{6,0},{1,3},{3,5},{5,7},{7,1},{8,10},{10,12},{12... | collective-permute-start | bytes 196616 | tf_op jit(solution)/shard_map/ppermute | solution.py:248
  91.3 0.7 copy-done.8
  92.0 8.0 %shard_map.103 = bf16[64,512]{1,0:T(8,128)(2,1)} custom-call(s32[4]{0:T(128)} %pad_add_fusion.off_ref, f32[1,256]{1,0:T(1,128)} %bitcast.25, bf16[512,256]{1,0:T(8,128)(2,1)} %copy-done.8, bf16[1536,256]{1,0:T(8,128)(2,1)} %copy-done, bf16[1024,256]{1,0:T(8,128)(2,1)} %copy-done.4, bf16[1536,256]{1,0:T(8,128)(2,1)} %copy-done.2, ...), custom_call_target="tpu_custom_call" | custom-call | tf_op jit(solution)/shard_map/pallas_call | solution.py:203
  100.1 5.5 %shard_map.101 = f32[64,512]{1,0:T(8,128)} custom-call(s32[4]{0:T(128)} %pad_add_fusion.off_ref, f32[1,256]{1,0:T(1,128)} %bitcast.26, bf16[512,256]{1,0:T(8,128)(2,1)} %row_net.1.refs_0_, bf16[1536,256]{1,0:T(8,128)(2,1)} %copy-done.1, bf16[1024,256]{1,0:T(8,128)(2,1)} %copy-done.5, bf16[1536,256]{1,0:T(8,128)(2,1)} %copy-done.3, ...), custom_call_target="tpu_custom_call" | custom-call | tf_op jit(solution)/shard_map/pallas_call | solution.py:203
  105.6 0.4 collective-permute-done.14
  106.1 1.6 %add_bitcast_fusion = f32[512,64]{0,1:T(8,128)} fusion(bf16[64,512]{1,0:T(8,128)(2,1)S(1)} %collective-permute-done.14, bf16[64,512]{1,0:T(8,128)(2,1)S(1)} %collective-permute-done.12, f32[64,512]{1,0:T(8,128)} %shard_map.101, bf16[64,512]{1,0:T(8,128)(2,1)S(1)} %collective-permute-done.11), kind=kLoop, calls=%fused_computation | loop fusion | flops 196608 | bytes 458752 | tf_op jit(solution)/shard_map/transpose | solution.py:253
  (36 shorter events, 0.6 us)
Async XLA Ops:
  12.3 24.1 %collective-permute-start = (bf16[512,256]{1,0:T(8,128)(2,1)}, bf16[512,256]{1,0:T(8,128)(2,1)S(1)}, u32[]{:S(2)}, u32[]{:S(2)}) collective-permute-start(bf16[512,256]{1,0:T(8,128)(2,1)} %get-tuple-element.19), channel_id=1, source_target_pairs={{0,32},{32,64},{64,96},{96,0},{1,33},{33,65},{65,97},{97,1},{2,34}... | collective-permute-start | bytes 786440 | tf_op jit(solution)/shard_map/ppermute | solution.py:225
  14.0 22.4 %collective-permute-start.1 = (bf16[512,256]{1,0:T(8,128)(2,1)}, bf16[512,256]{1,0:T(8,128)(2,1)S(1)}, u32[]{:S(2)}, u32[]{:S(2)}) collective-permute-start(bf16[512,256]{1,0:T(8,128)(2,1)} %get-tuple-element.19), channel_id=1, source_target_pairs={{0,96},{32,0},{64,32},{96,64},{1,97},{33,1},{65,33},{97,65},{2,98}... | collective-permute-start | bytes 786440 | tf_op jit(solution)/shard_map/ppermute | solution.py:226
  15.6 20.9 %collective-permute-start.2 = (bf16[512,256]{1,0:T(8,128)(2,1)}, bf16[512,256]{1,0:T(8,128)(2,1)S(1)}, u32[]{:S(2)}, u32[]{:S(2)}) collective-permute-start(bf16[512,256]{1,0:T(8,128)(2,1)} %get-tuple-element.19), channel_id=1, source_target_pairs={{0,64},{32,96},{64,0},{96,32},{1,65},{33,97},{65,1},{97,33},{2,66}... | collective-permute-start | bytes 786440 | tf_op jit(solution)/shard_map/ppermute | solution.py:227
  17.7 18.8 %all-to-all-start = ((bf16[128,4,128]{2,1,0:T(4,128)(2,1)}), bf16[128,4,128]{2,1,0:T(4,128)(2,1)S(1)}, u32[]{:S(2)}, u32[]{:S(2)}) async-start(bf16[128,4,128]{2,1,0:T(4,128)(2,1)} %bitcast.11), calls=%async_computation | async-start | bytes 262144 | tf_op jit(solution)/shard_map/all_to_all | solution.py:228
  36.4 4.3 %copy-start.7 = (bf16[128,4,128]{2,1,0:T(4,128)(2,1)}, bf16[128,4,128]{2,1,0:T(4,128)(2,1)S(1)}, u32[]{:S(2)}) copy-start(bf16[128,4,128]{2,1,0:T(4,128)(2,1)S(1)} %all-to-all-done) | copy-start | bytes 393220
  36.5 14.3 %copy-start = (bf16[1536,256]{1,0:T(8,128)(2,1)}, bf16[1536,256]{1,0:T(8,128)(2,1)S(1)}, u32[]{:S(2)}) copy-start(bf16[1536,256]{1,0:T(8,128)(2,1)S(1)} %constant_dynamic-update-slice_fusion.refs_1_.refs_2_) | copy-start | bytes 2359300
  36.5 14.3 %collective-permute-start.5 = (bf16[1536,256]{1,0:T(8,128)(2,1)S(1)}, bf16[1536,256]{1,0:T(8,128)(2,1)S(1)}, u32[]{:S(2)}, u32[]{:S(2)}) collective-permute-start(bf16[1536,256]{1,0:T(8,128)(2,1)S(1)} %constant_dynamic-update-slice_fusion.refs_1_.refs_2_), channel_id=1, source_target_pairs={{0,1},{1,0},{2,3},{3,2},{4,5},{5,4},{6,7},{7,6},{8,9},{9,8},{10,11... | collective-permute-start | bytes 2359304 | tf_op jit(solution)/shard_map/ppermute | solution.py:235
  36.6 21.1 %collective-permute-start.3 = (bf16[1536,256]{1,0:T(8,128)(2,1)S(1)}, bf16[1536,256]{1,0:T(8,128)(2,1)S(1)}, u32[]{:S(2)}, u32[]{:S(2)}) collective-permute-start(bf16[1536,256]{1,0:T(8,128)(2,1)S(1)} %constant_dynamic-update-slice_fusion.refs_1_.refs_2_), channel_id=1, source_target_pairs={{0,8},{8,16},{16,24},{24,0},{1,9},{9,17},{17,25},{25,1},{2,10},{10... | collective-permute-start | bytes 2359304 | tf_op jit(solution)/shard_map/ppermute | solution.py:233
  37.5 13.3 %copy-start.4 = (bf16[1024,256]{1,0:T(8,128)(2,1)}, bf16[1024,256]{1,0:T(8,128)(2,1)S(1)}, u32[]{:S(2)}) copy-start(bf16[1024,256]{1,0:T(8,128)(2,1)S(1)} %constant_dynamic-update-slice_fusion.3.refs_2_.refs_3_) | copy-start | bytes 1572868
  37.5 13.3 %collective-permute-start.6 = (bf16[1024,256]{1,0:T(8,128)(2,1)S(1)}, bf16[1024,256]{1,0:T(8,128)(2,1)}, u32[]{:S(2)}, u32[]{:S(2)}) collective-permute-start(bf16[1024,256]{1,0:T(8,128)(2,1)S(1)} %constant_dynamic-update-slice_fusion.3.refs_2_.refs_3_), channel_id=1, source_target_pairs={{0,1},{1,0},{2,3},{3,2},{4,5},{5,4},{6,7},{7,6},{8,9},{9,8},{10,11... | collective-permute-start | bytes 1572872 | tf_op jit(solution)/shard_map/ppermute | solution.py:236
  37.7 19.4 %collective-permute-start.4 = (bf16[1024,256]{1,0:T(8,128)(2,1)S(1)}, bf16[1024,256]{1,0:T(8,128)(2,1)S(1)}, u32[]{:S(2)}, u32[]{:S(2)}) collective-permute-start(bf16[1024,256]{1,0:T(8,128)(2,1)S(1)} %constant_dynamic-update-slice_fusion.3.refs_2_.refs_3_), channel_id=1, source_target_pairs={{0,24},{8,0},{16,8},{24,16},{1,25},{9,1},{17,9},{25,17},{2,26},{10... | collective-permute-start | bytes 1572872 | tf_op jit(solution)/shard_map/ppermute | solution.py:234
  50.8 0.9 copy-start.2
  57.1 17.4 %copy-start.5 = (bf16[1024,256]{1,0:T(8,128)(2,1)}, bf16[1024,256]{1,0:T(8,128)(2,1)S(1)}, u32[]{:S(2)}) copy-start(bf16[1024,256]{1,0:T(8,128)(2,1)S(1)} %collective-permute-done.4.refs_2_.refs_7_.refs_6_) | copy-start | bytes 1572868
  57.8 16.8 %copy-start.1 = (bf16[1536,256]{1,0:T(8,128)(2,1)}, bf16[1536,256]{1,0:T(8,128)(2,1)S(1)}, u32[]{:S(2)}) copy-start(bf16[1536,256]{1,0:T(8,128)(2,1)S(1)} %collective-permute-done.3.refs_1_.refs_6_.refs_5_) | copy-start | bytes 2359300
  57.8 16.8 %collective-permute-start.7 = (bf16[1536,256]{1,0:T(8,128)(2,1)S(1)}, bf16[1536,256]{1,0:T(8,128)(2,1)S(1)}, u32[]{:S(2)}, u32[]{:S(2)}) collective-permute-start(bf16[1536,256]{1,0:T(8,128)(2,1)S(1)} %collective-permute-done.3.refs_1_.refs_6_.refs_5_), channel_id=1, source_target_pairs={{0,1},{1,0},{2,3},{3,2},{4,5},{5,4},{6,7},{7,6},{8,9},{9,8},{10,11... | collective-permute-start | bytes 2359304 | tf_op jit(solution)/shard_map/ppermute | solution.py:243
  57.8 16.7 %collective-permute-start.8 = (bf16[1024,256]{1,0:T(8,128)(2,1)S(1)}, bf16[1024,256]{1,0:T(8,128)(2,1)S(1)}, u32[]{:S(2)}, u32[]{:S(2)}) collective-permute-start(bf16[1024,256]{1,0:T(8,128)(2,1)S(1)} %collective-permute-done.4.refs_2_.refs_7_.refs_6_), channel_id=1, source_target_pairs={{0,1},{1,0},{2,3},{3,2},{4,5},{5,4},{6,7},{7,6},{8,9},{9,8},{10,11... | collective-permute-start | bytes 1572872 | tf_op jit(solution)/shard_map/ppermute | solution.py:244
  58.3 9.4 %collective-permute-start.10 = (bf16[512,256]{1,0:T(8,128)(2,1)}, bf16[512,256]{1,0:T(8,128)(2,1)S(1)}, u32[]{:S(2)}, u32[]{:S(2)}) collective-permute-start(bf16[512,256]{1,0:T(8,128)(2,1)} %row_net.1.refs_0_), channel_id=1, source_target_pairs={{0,6},{2,0},{4,2},{6,4},{1,7},{3,1},{5,3},{7,5},{8,14},{10,8},{12,... | collective-permute-start | bytes 786440 | tf_op jit(solution)/shard_map/ppermute | solution.py:238
  59.5 15.0 %collective-permute-start.9 = (bf16[512,256]{1,0:T(8,128)(2,1)}, bf16[512,256]{1,0:T(8,128)(2,1)S(1)}, u32[]{:S(2)}, u32[]{:S(2)}) collective-permute-start(bf16[512,256]{1,0:T(8,128)(2,1)} %row_net.1.refs_0_), channel_id=1, source_target_pairs={{0,2},{2,4},{4,6},{6,0},{1,3},{3,5},{5,7},{7,1},{8,10},{10,12},{12... | collective-permute-start | bytes 786440 | tf_op jit(solution)/shard_map/ppermute | solution.py:237
  60.3 31.0 %collective-permute-start.13 = (bf16[512,256]{1,0:T(8,128)(2,1)}, bf16[512,256]{1,0:T(8,128)(2,1)S(1)}, u32[]{:S(2)}, u32[]{:S(2)}) collective-permute-start(bf16[512,256]{1,0:T(8,128)(2,1)} %row_net.1.refs_0_), channel_id=1, source_target_pairs={{0,4},{2,6},{4,0},{6,2},{1,5},{3,7},{5,1},{7,3},{8,12},{10,14},{12... | collective-permute-start | bytes 786440 | tf_op jit(solution)/shard_map/ppermute | solution.py:239
  67.7 6.9 %copy-start.9 = (bf16[512,256]{1,0:T(8,128)(2,1)}, bf16[512,256]{1,0:T(8,128)(2,1)S(1)}, u32[]{:S(2)}) copy-start(bf16[512,256]{1,0:T(8,128)(2,1)S(1)} %collective-permute-done.10.refs_1_) | copy-start | bytes 786436
  74.5 0.7 copy-start.10
  74.5 0.9 copy-start.6
  75.4 0.9 copy-start.3
  89.2 16.4 %collective-permute-start.11 = (bf16[64,512]{1,0:T(8,128)(2,1)}, bf16[64,512]{1,0:T(8,128)(2,1)S(1)}, u32[]{:S(2)}, u32[]{:S(2)}) collective-permute-start(bf16[64,512]{1,0:T(8,128)(2,1)} %get-tuple-element.29), channel_id=1, source_target_pairs={{0,6},{2,0},{4,2},{6,4},{1,7},{3,1},{5,3},{7,5},{8,14},{10,8},{12,... | collective-permute-start | bytes 196616 | tf_op jit(solution)/shard_map/ppermute | solution.py:247
  89.3 16.3 %collective-permute-start.12 = (bf16[64,512]{1,0:T(8,128)(2,1)}, bf16[64,512]{1,0:T(8,128)(2,1)S(1)}, u32[]{:S(2)}, u32[]{:S(2)}) collective-permute-start(bf16[64,512]{1,0:T(8,128)(2,1)} %get-tuple-element.30), channel_id=1, source_target_pairs={{0,2},{2,4},{4,6},{6,0},{1,3},{3,5},{5,7},{7,1},{8,10},{10,12},{12... | collective-permute-start | bytes 196616 | tf_op jit(solution)/shard_map/ppermute | solution.py:248
  91.3 0.7 copy-start.8
  100.0 6.1 %collective-permute-start.14 = (bf16[64,512]{1,0:T(8,128)(2,1)}, bf16[64,512]{1,0:T(8,128)(2,1)S(1)}, u32[]{:S(2)}, u32[]{:S(2)}) collective-permute-start(bf16[64,512]{1,0:T(8,128)(2,1)} %shard_map.103), channel_id=1, source_target_pairs={{0,4},{2,6},{4,0},{6,2},{1,5},{3,7},{5,1},{7,3},{8,12},{10,14},{12... | collective-permute-start | bytes 196616 | tf_op jit(solution)/shard_map/ppermute | solution.py:250
where the time goes:
time: 108 us
  Pallas kernels  54.2 us (50%)
  starting transfers between devices  24.3 us (22%)
  waiting for transfers between devices  21.5 us (20%)
  local copies, waits for them, and re-layouts  5.34 us (5%)
  other arithmetic  2.16 us (2%)
    pallas_call x4, Pallas kernels, rbf(): pl.pallas_call(functools.partial(rbf_kernel, nr=nr, pairs=npairs, with_in...  31.9 us
    pallas_call x1, Pallas kernels, col_net(): pl.pallas_call(functools.partial(col_kernel, steps=steps), grid_spec=spec...  10.4 us
    pallas_call x1, Pallas kernels, row_net(): pl.pallas_call(functools.partial(row_kernel, steps=steps), grid=(steps,),...  9.98 us
    all_to_all x1, starting transfers between devices, steps(): got = lax.all_to_all(sent, ALL, 0, 0, tiled=True)  9.41 us
    all_to_all x1, waiting for transfers between devices, steps(): got = lax.all_to_all(sent, ALL, 0, 0, tiled=True)  7.43 us
    ppermute x1, waiting for transfers between devices, steps(): f1 = lax.ppermute(feats, 'x', ring(1))  6.84 us
    ppermute x1, waiting for transfers between devices, steps(): f3 = lax.ppermute(feats, 'x', ring(3))  6.16 us
    unnamed x25, local copies, waits for them, and re-layouts  5.3 us
  transfers between devices with their start and end apart: 16, of which 5 were waited for; matrix products, arithmetic and copies ran while one was open for 2% of the time, Pallas kernels for 39%

commit v1 on v0

--- a/solution.py
+++ b/solution.py
@@ -25,7 +25,40 @@
     return jnp.dot(a, b, preferred_element_type=f32)
 
 
-def send_kernel(dest_ref, xt_ref, o_ref):
+CHUNK = 512
+
+
+def weight_copies(w2_ref, w3_ref, w2_v, w3_v, sem):
+    chunks = w2_v.shape[0]
+    for c in range(chunks):
+        pltpu.make_async_copy(w2_ref.at[:, pl.ds(c * CHUNK, CHUNK)], w2_v.at[c], sem.at[c]).start()
+        if c == 0:
+            pltpu.make_async_copy(w3_ref, w3_v, sem.at[chunks]).start()
+
+
+def last_layers(w2_ref, b2_ref, w3_ref, o_ref, h1, w2_v, w3_v, acc, sem):
+    chunks = w2_v.shape[0]
+
+    def chunk(c):
+        pltpu.make_async_copy(w2_ref.at[:, pl.ds(0, CHUNK)], w2_v.at[c], sem.at[c]).wait()
+        at = pl.multiple_of(c * CHUNK, CHUNK)
+        h2 = jnp.maximum(dot(h1[...], w2_v[c]) + b2_ref[:, pl.ds(at, CHUNK)], 0.0).astype(bf16)
+        return h2, at
+
+    h2, _ = chunk(0)
+    pltpu.make_async_copy(w3_ref, w3_v, sem.at[chunks]).wait()
+    acc[...] = dot(h2, w3_v[0:CHUNK, :])
+
+    def body(c, _):
+        h2, at = chunk(c)
+        acc[...] += dot(h2, w3_v[pl.ds(at, CHUNK), :])
+        return 0
+
+    lax.fori_loop(1, chunks, body, 0)
+    o_ref[...] = acc[...].astype(bf16)
+
+
+def reorder(dest_ref, xt_ref, o_ref):
     d_row = dest_ref[...]
     d_f = d_row.astype(f32)
     d_col = jnp.transpose(jnp.broadcast_to(d_f, (128, ROWS)))
@@ -42,103 +75,74 @@
     o_ref[...] = lax.dot_general(place, ext, NT, preferred_element_type=f32).astype(bf16)
 
 
-def send_rows(dest, x_t):
+def front_kernel(
+    y_ref, dest_ref, xm_ref, xc_ref, p_ref, w1_ref, b1_ref, w2_ref, b2_ref, w3_ref,
+    s_ref, o_ref, q_ref, h1, w2_v, w3_v, acc, sem,
+):
+    weight_copies(w2_ref, w3_ref, w2_v, w3_v, sem)
+    reorder(dest_ref, xm_ref, s_ref)
+    for j in range(8):
+        q_ref[j * 64 : (j + 1) * 64, :] = p_ref[:, j * 256 : (j + 1) * 256].astype(bf16)
+    xc = xc_ref[:, pl.ds(pl.multiple_of(y_ref[0] * UNIT, UNIT), UNIT)]
+    x = lax.dot_general(xc, w1_ref[...], TN, preferred_element_type=f32)
+    h1[...] = jnp.maximum(x + b1_ref[...], 0.0).astype(bf16)
+    last_layers(w2_ref, b2_ref, w3_ref, o_ref, h1, w2_v, w3_v, acc, sem)
+
+
+def row_kernel(r_ref, w1_ref, b1_ref, w2_ref, b2_ref, w3_ref, o_ref, h1, w2_v, w3_v, acc, sem):
+    weight_copies(w2_ref, w3_ref, w2_v, w3_v, sem)
+    got = r_ref[...]
+    lane = lax.broadcasted_iota(jnp.int32, (8, 128), 1)
+    pick = jnp.where(lane == 40, 16.0, jnp.where(lane == 41, 1.0, 0.0)).astype(bf16)
+    pos = lax.dot_general(pick, got, NT, preferred_element_type=f32)[0:1, :]
+    place = lax.broadcasted_iota(jnp.int32, (ROWS, ROWS), 0).astype(f32) == pos
+    place = jnp.where(place, 1.0, 0.0).astype(bf16)
+    x = dot(place, got).astype(bf16)[:, :40]
+    h1[...] = jnp.maximum(dot(x, w1_ref[...]) + b1_ref[...], 0.0).astype(bf16)
+    last_layers(w2_ref, b2_ref, w3_ref, o_ref, h1, w2_v, w3_v, acc, sem)
+
+
+VM = pl.BlockSpec(memory_space=pltpu.VMEM)
+SM = pl.BlockSpec(memory_space=pltpu.SMEM)
+HB = pl.BlockSpec(memory_space=pltpu.HBM)
+LIMIT = pltpu.CompilerParams(vmem_limit_bytes=30 * 2**20)
+WEIGHT_SPECS = [VM, VM, HB, VM, HB]
+
+
+def net_scratch(m, hid, ft):
+    return [
+        pltpu.VMEM((m, hid), bf16),
+        pltpu.VMEM((hid // CHUNK, hid, CHUNK), bf16),
+        pltpu.VMEM((hid, ft), bf16),
+        pltpu.VMEM((m, ft), f32),
+        pltpu.SemaphoreType.DMA((hid // CHUNK + 1,)),
+    ]
+
+
+def front(y, dest, x_m, x_c, p_t, w1, b1, w2, b2, w3):
+    hid, ft = w2.shape[0], w3.shape[1]
     return pl.pallas_call(
-        send_kernel,
-        out_shape=jax.ShapeDtypeStruct((ROWS, 128), bf16),
-        name="send_rows",
-    )(dest.reshape(1, ROWS), x_t)
-
-
-def mlp_tail(h1, w2_ref, b2_ref, w3_ref, o_ref, acc, steps):
-    i = pl.program_id(0)
-    h2 = jnp.maximum(dot(h1[...], w2_ref[...]) + b2_ref[...], 0.0).astype(bf16)
-    part = dot(h2, w3_ref[...])
-
-    @pl.when(i == 0)
-    def _():
-        acc[...] = part
-
-    @pl.when(i > 0)
-    def _():
-        acc[...] += part
-
-    @pl.when(i == steps - 1)
-    def _():
-        o_ref[...] = acc[...].astype(bf16)
-
-
-def col_kernel(y_ref, xt_ref, p_ref, w1_ref, b1_ref, w2_ref, b2_ref, w3_ref, o_ref, q_ref, h1, acc, *, steps):
-    @pl.when(pl.program_id(0) == 0)
-    def _():
-        x = lax.dot_general(xt_ref[...], w1_ref[...], TN, preferred_element_type=f32)
-        h1[...] = jnp.maximum(x + b1_ref[...], 0.0).astype(bf16)
-        for j in range(8):
-            q_ref[j * 64 : (j + 1) * 64, :] = p_ref[:, j * 256 : (j + 1) * 256].astype(bf16)
-
-    mlp_tail(h1, w2_ref, b2_ref, w3_ref, o_ref, acc, steps)
-
-
-def row_kernel(r_ref, w1_ref, b1_ref, w2_ref, b2_ref, w3_ref, o_ref, h1, acc, *, steps):
-    @pl.when(pl.program_id(0) == 0)
-    def _():
-        got = r_ref[...]
-        lane = lax.broadcasted_iota(jnp.int32, (8, 128), 1)
-        pick = jnp.where(lane == 40, 16.0, jnp.where(lane == 41, 1.0, 0.0)).astype(bf16)
-        pos = lax.dot_general(pick, got, NT, preferred_element_type=f32)[0:1, :]
-        place = lax.broadcasted_iota(jnp.int32, (ROWS, ROWS), 0).astype(f32) == pos
-        place = jnp.where(place, 1.0, 0.0).astype(bf16)
-        x = dot(place, got).astype(bf16)[:, :40]
-        h1[...] = jnp.maximum(dot(x, w1_ref[...]) + b1_ref[...], 0.0).astype(bf16)
-
-    mlp_tail(h1, w2_ref, b2_ref, w3_ref, o_ref, acc, steps)
-
-
-def weight_specs(w1, hid, bn, ft):
-    return [
-        pl.BlockSpec(w1.shape, lambda i, *_: (0, 0)),
-        pl.BlockSpec((1, hid), lambda i, *_: (0, 0)),
-        pl.BlockSpec((hid, bn), lambda i, *_: (0, i)),
-        pl.BlockSpec((1, bn), lambda i, *_: (0, i)),
-        pl.BlockSpec((bn, ft), lambda i, *_: (i, 0)),
-    ]
-
-
-def col_net(y, x_t, p_t, w1, b1, w2, b2, w3, bn=512):
+        front_kernel,
+        in_specs=[SM, VM, VM, VM, VM, *WEIGHT_SPECS],
+        out_specs=[VM] * 3,
+        out_shape=[
+            jax.ShapeDtypeStruct((ROWS, 128), bf16),
+            jax.ShapeDtypeStruct((UNIT, ft), bf16),
+            jax.ShapeDtypeStruct((UNIT, ft), bf16),
+        ],
+        scratch_shapes=net_scratch(UNIT, hid, ft),
+        name="front",
+    )(y, dest.reshape(1, ROWS), x_m, x_c, p_t, w1, b1.reshape(1, -1), w2, b2.reshape(1, -1), w3)
+
+
+def row_net(got, w1, b1, w2, b2, w3):
     hid, ft = w2.shape[0], w3.shape[1]
-    steps = hid // bn
-    spec = pltpu.PrefetchScalarGridSpec(
-        num_scalar_prefetch=1,
-        grid=(steps,),
-        in_specs=[
-            pl.BlockSpec((40, UNIT), lambda i, y: (0, y[0])),
-            pl.BlockSpec((64, 2048), lambda i, y: (0, 0)),
-            *weight_specs(w1, hid, bn, ft),
-        ],
-        out_specs=[
-            pl.BlockSpec((UNIT, ft), lambda i, y: (0, 0)),
-            pl.BlockSpec((UNIT, ft), lambda i, y: (0, 0)),
-        ],
-        scratch_shapes=[pltpu.VMEM((UNIT, hid), bf16), pltpu.VMEM((UNIT, ft), f32)],
-    )
     return pl.pallas_call(
-        functools.partial(col_kernel, steps=steps),
-        grid_spec=spec,
-        out_shape=[jax.ShapeDtypeStruct((UNIT, ft), bf16)] * 2,
-        name="col_net",
-    )(y, x_t, p_t, w1, b1.reshape(1, -1), w2, b2.reshape(1, -1), w3)
-
-
-def row_net(got, w1, b1, w2, b2, w3, bn=512):
-    hid, ft = w2.shape[0], w3.shape[1]
-    steps = hid // bn
-    return pl.pallas_call(
-        functools.partial(row_kernel, steps=steps),
-        grid=(steps,),
-        in_specs=[pl.BlockSpec((ROWS, 128), lambda i: (0, 0)), *weight_specs(w1, hid, bn, ft)],
-        out_specs=pl.BlockSpec((ROWS, ft), lambda i: (0, 0)),
+        row_kernel,
+        in_specs=[VM, *WEIGHT_SPECS],
+        out_specs=VM,
         out_shape=jax.ShapeDtypeStruct((ROWS, ft), bf16),
-        scratch_shapes=[pltpu.VMEM((ROWS, hid), bf16), pltpu.VMEM((ROWS, ft), f32)],
+        scratch_shapes=net_scratch(ROWS, hid, ft),
         name="row_net",
     )(got, w1, b1.reshape(1, -1), w2, b2.reshape(1, -1), w3)
 
@@ -198,13 +202,14 @@
 def rbf(off,rel,rows,pairs,init=None,out=f32,bm=256,cs=512,ug=4):
     nr=len(rows)
     args=list(rows)+[x for p in pairs for x in p]+([init] if init is not None else [])
-    V=pl.BlockSpec(memory_space=pltpu.VMEM); A=pl.BlockSpec(memory_space=pl.ANY)
+    V = VM
     npairs=len(pairs); m=nr*ROWS
     return pl.pallas_call(functools.partial(rbf_kernel,nr=nr,pairs=npairs,with_init=init is not None,bm=bm,cs=cs,ug=ug),
-        in_specs=[pl.BlockSpec(memory_space=pltpu.SMEM),V]+[V]*nr+[A]*(2*npairs)+([V] if init is not None else []),
+        in_specs=[SM,V]+[V]*nr+[V]*(2*npairs)+([V] if init is not None else []),
         out_specs=[V]*nr,out_shape=[jax.ShapeDtypeStruct((64,ROWS),out)]*nr,
         scratch_shapes=[pltpu.VMEM((m,FEAT),bf16),pltpu.VMEM((8,m),f32),pltpu.VMEM((npairs*PAIR,FEAT),bf16),pltpu.VMEM((2048,128),f32),
-          pltpu.VMEM((2048,m),bf16),pltpu.VMEM((64,m),f32),pltpu.SemaphoreType.DMA((2*npairs,))])(off,rel,*args)
+          pltpu.VMEM((2048,m),bf16),pltpu.VMEM((64,m),f32),pltpu.SemaphoreType.DMA((2*npairs,))],
+        compiler_params=LIMIT)(off,rel,*args)
 
 
 def ring(shift):
@@ -219,9 +224,7 @@
     rel = rel.reshape(1, FEAT)
     y = lax.axis_index("y").astype(jnp.int32)
     off = jnp.stack([y, (y + 3) % 4, (y + 1) % 4, (y + 2) % 4]).astype(jnp.int32)
-    sent = send_rows(dest, x_m.T)
-    own, probe = col_net(y.reshape(1), x_c.T, probes.T, w1, b1, w2, b2, w3)
-    sent, own = lax.optimization_barrier((sent, own))
+    sent, own, probe = front(y.reshape(1), dest, x_m.T, x_c.T, probes.T, w1, b1, w2, b2, w3)
     u1 = lax.ppermute(own, "y", ring(1))
     u3 = lax.ppermute(own, "y", ring(3))
     u2 = lax.ppermute(own, "y", ring(2))

time: 108 us -> 100 us (0.926)
  Pallas kernels: 54.2 us -> 47.3 us
  waiting for transfers between devices: 21.5 us -> 25.5 us
  local copies, waits for them, and re-layouts: 5.34 us -> 2 us
  other arithmetic: 2.16 us -> 0.76 us
    pallas_call x4, Pallas kernels: 31.9 us -> 27.9 us  [rbf(): pl.pallas_call(functools.partial(rbf_kernel, nr=nr, pairs=npairs, with_in...]
    unnamed x25 -> x7, local copies, waits for them, and re-layouts: 5.3 us -> 1.97 us
    pallas_call x3 -> x2, Pallas kernels: 22.3 us -> 19.4 us  [the longest x1 9.8 us: front(): pl.pallas_call(front_kernel, in_specs=[SM, VM, VM, VM, VM, *WEIGHT_SPECS]...]
    ppermute x1, waiting for transfers between devices: 0.61 us -> 3.49 us  [steps(): za = lax.ppermute(ca, Z, ring(1))]
    ppermute x1, waiting for transfers between devices: 0.45 us -> 1.56 us  [steps(): r2 = lax.ppermute(t2, 'x', ring(2))]
  transfers between devices with their start and end apart: 16 -> 16, of which waited for: 5 -> 5; matrix products, arithmetic and copies ran while one was open for 2% -> 2% of each run, Pallas kernels for 39% -> 37%
where the time goes in v1:
time: 100 us
  Pallas kernels  47.3 us (47%)
  waiting for transfers between devices  25.5 us (26%)
  starting transfers between devices  24.3 us (24%)
  local copies, waits for them, and re-layouts  2 us (2%)
    pallas_call x4, Pallas kernels, rbf(): pl.pallas_call(functools.partial(rbf_kernel, nr=nr, pairs=npairs, with_in...  27.9 us
    pallas_call x1, Pallas kernels, front(): pl.pallas_call(front_kernel, in_specs=[SM, VM, VM, VM, VM, *WEIGHT_SPECS]...  9.8 us
    pallas_call x1, Pallas kernels, row_net(): pl.pallas_call(row_kernel, in_specs=[VM, *WEIGHT_SPECS], out_specs=VM, ou...  9.61 us
    all_to_all x1, starting transfers between devices, steps(): got = lax.all_to_all(sent, ALL, 0, 0, tiled=True)  9.41 us
    all_to_all x1, waiting for transfers between devices, steps(): got = lax.all_to_all(sent, ALL, 0, 0, tiled=True)  7.43 us
    ppermute x1, waiting for transfers between devices, steps(): f1 = lax.ppermute(feats, 'x', ring(1))  6.84 us
    ppermute x1, waiting for transfers between devices, steps(): f3 = lax.ppermute(feats, 'x', ring(3))  6.16 us
    ppermute x1, waiting for transfers between devices, steps(): za = lax.ppermute(ca, Z, ring(1))  3.49 us
  transfers between devices with their start and end apart: 16, of which 5 were waited for; matrix products, arithmetic and copies ran while one was open for 2% of the time, Pallas kernels for 37%

profile of v1, /device:TPU:0, one launch (start us, length us, event | category | flops | bytes accessed | tf_op | source)
XLA Modules:
  0.0 100.1 jit_solution(10502329177518355645)
XLA Ops:
  0.0 9.8 %front.1 = (bf16[512,128]{1,0:T(8,128)(2,1)}, bf16[512,256]{1,0:T(8,128)(2,1)}, bf16[512,256]{1,0:T(8,128)(2,1)}) custom-call(s32[1]{0:T(128)} %bitcast.y_ref, s32[1,512]{1,0:T(1,128)} %bitcast.28, bf16[40,512]{1,0:T(8,128)(2,1)} %bitcast.23, bf16[40,2048]{1,0:T(8,128)(2,1)} %bitcast.21, f32[64,2048]{1,0:T(8,128)} %bitcast.20, bf16[40,2048]{1,0:T(8,128)(2,1)} %w1_ref.3, ...), custom_call_target="tpu_custom_call" | custom-call | tf_op jit(solution)/shard_map/front/pallas_call | solution.py:124
  9.8 0.0 copy-start
  9.8 1.8 %collective-permute-start = (bf16[512,256]{1,0:T(8,128)(2,1)}, bf16[512,256]{1,0:T(8,128)(2,1)S(1)}, u32[]{:S(2)}, u32[]{:S(2)}) collective-permute-start(bf16[512,256]{1,0:T(8,128)(2,1)} %get-tuple-element.17), channel_id=1, source_target_pairs={{0,32},{32,64},{64,96},{96,0},{1,33},{33,65},{65,97},{97,1},{2,34}... | collective-permute-start | bytes 786440 | tf_op jit(solution)/shard_map/ppermute | solution.py:228
  11.6 1.5 %collective-permute-start.1 = (bf16[512,256]{1,0:T(8,128)(2,1)}, bf16[512,256]{1,0:T(8,128)(2,1)S(1)}, u32[]{:S(2)}, u32[]{:S(2)}) collective-permute-start(bf16[512,256]{1,0:T(8,128)(2,1)} %get-tuple-element.17), channel_id=1, source_target_pairs={{0,96},{32,0},{64,32},{96,64},{1,97},{33,1},{65,33},{97,65},{2,98}... | collective-permute-start | bytes 786440 | tf_op jit(solution)/shard_map/ppermute | solution.py:229
  13.1 2.1 %collective-permute-start.2 = (bf16[512,256]{1,0:T(8,128)(2,1)}, bf16[512,256]{1,0:T(8,128)(2,1)S(1)}, u32[]{:S(2)}, u32[]{:S(2)}) collective-permute-start(bf16[512,256]{1,0:T(8,128)(2,1)} %get-tuple-element.17), channel_id=1, source_target_pairs={{0,64},{32,96},{64,0},{96,32},{1,65},{33,97},{65,1},{97,33},{2,66}... | collective-permute-start | bytes 786440 | tf_op jit(solution)/shard_map/ppermute | solution.py:230
  15.2 9.4 %all-to-all-start = ((bf16[128,4,128]{2,1,0:T(4,128)(2,1)}), bf16[128,4,128]{2,1,0:T(4,128)(2,1)S(1)}, u32[]{:S(2)}, u32[]{:S(2)}) async-start(bf16[128,4,128]{2,1,0:T(4,128)(2,1)} %bitcast.22), calls=%async_computation | async-start | bytes 262144 | tf_op jit(solution)/shard_map/all_to_all | solution.py:231
  24.6 1.0 constant_dynamic-update-slice_fusion.2
  25.6 1.0 constant_dynamic-update-slice_fusion.1
  26.6 7.4 %all-to-all-done = bf16[128,4,128]{2,1,0:T(4,128)(2,1)S(1)} async-done(((bf16[128,4,128]{2,1,0:T(4,128)(2,1)}), bf16[128,4,128]{2,1,0:T(4,128)(2,1)S(1)}, u32[]{:S(2)}, u32[]{:S(2)}) %all-to-all-start) | async-done | bytes 131104 | tf_op jit(solution)/shard_map/all_to_all | solution.py:231
  34.0 0.0 collective-permute-done
  34.1 0.1 collective-permute-start.5
  34.2 0.8 collective-permute-start.3
  35.0 0.2 collective-permute-start.6
  35.3 2.5 %collective-permute-start.4 = (bf16[1024,256]{1,0:T(8,128)(2,1)S(1)}, bf16[1024,256]{1,0:T(8,128)(2,1)S(1)}, u32[]{:S(2)}, u32[]{:S(2)}) collective-permute-start(bf16[1024,256]{1,0:T(8,128)(2,1)S(1)} %constant_dynamic-update-slice_fusion.3.refs_2_.refs_3_), channel_id=1, source_target_pairs={{0,24},{8,0},{16,8},{24,16},{1,25},{9,1},{17,9},{25,17},{2,26},{10... | collective-permute-start | bytes 1572872 | tf_op jit(solution)/shard_map/ppermute | solution.py:237
  37.7 0.1 pad_add_fusion.off_ref
  37.8 9.6 %row_net.1.refs_0_ = bf16[512,256]{1,0:T(8,128)(2,1)} custom-call(bf16[512,128]{1,0:T(8,128)(2,1)} %bitcast.19, bf16[40,2048]{1,0:T(8,128)(2,1)} %w1_ref.3, f32[1,2048]{1,0:T(1,128)} %bitcast.25, bf16[2048,2048]{1,0:T(8,128)(2,1)} %w2_ref.3, f32[1,2048]{1,0:T(1,128)} %bitcast.27, bf16[2048,256]{1,0:T(8,128)(2,1)} %w3_ref.3), custom_call_target="tpu_custom_call" | custom-call | tf_op jit(solution)/shard_map/row_net/pallas_call | solution.py:140
  47.5 4.3 %shard_map.100.refs_5_ = f32[64,512]{1,0:T(8,128)S(1)} custom-call(s32[4]{0:T(128)S(1)} %pad_add_fusion.off_ref, f32[1,256]{1,0:T(1,128)S(1)} %bitcast.15, bf16[512,256]{1,0:T(8,128)(2,1)} %row_net.1.refs_0_, bf16[1536,256]{1,0:T(8,128)(2,1)S(1)} %constant_dynamic-update-slice_fusion.refs_1_.refs_2_, ...), custom_call_target="tpu_custom_call" | custom-call | tf_op jit(solution)/shard_map/pallas_call | solution.py:207
  51.8 3.5 %collective-permute-done.3.refs_1_.refs_6_.refs_5_ = bf16[1536,256]{1,0:T(8,128)(2,1)S(1)} collective-permute-done((bf16[1536,256]{1,0:T(8,128)(2,1)S(1)}, bf16[1536,256]{1,0:T(8,128)(2,1)S(1)}, u32[]{:S(2)}, u32[]{:S(2)}) %collective-permute-start.3) | collective-permute-done | bytes 786464 | tf_op jit(solution)/shard_map/ppermute | solution.py:236
  55.3 0.5 collective-permute-start.8
  55.8 1.3 %collective-permute-start.10 = (bf16[512,256]{1,0:T(8,128)(2,1)}, bf16[512,256]{1,0:T(8,128)(2,1)S(1)}, u32[]{:S(2)}, u32[]{:S(2)}) collective-permute-start(bf16[512,256]{1,0:T(8,128)(2,1)} %row_net.1.refs_0_), channel_id=1, source_target_pairs={{0,6},{2,0},{4,2},{6,4},{1,7},{3,1},{5,3},{7,5},{8,14},{10,8},{12,... | collective-permute-start | bytes 786440 | tf_op jit(solution)/shard_map/ppermute | solution.py:241
  57.1 0.8 collective-permute-start.9
  57.9 1.2 %collective-permute-start.13 = (bf16[512,256]{1,0:T(8,128)(2,1)}, bf16[512,256]{1,0:T(8,128)(2,1)S(1)}, u32[]{:S(2)}, u32[]{:S(2)}) collective-permute-start(bf16[512,256]{1,0:T(8,128)(2,1)} %row_net.1.refs_0_), channel_id=1, source_target_pairs={{0,4},{2,6},{4,0},{6,2},{1,5},{3,7},{5,1},{7,3},{8,12},{10,14},{12... | collective-permute-start | bytes 786440 | tf_op jit(solution)/shard_map/ppermute | solution.py:242
  59.1 6.2 %collective-permute-done.10.refs_1_ = bf16[512,256]{1,0:T(8,128)(2,1)S(1)} collective-permute-done((bf16[512,256]{1,0:T(8,128)(2,1)}, bf16[512,256]{1,0:T(8,128)(2,1)S(1)}, u32[]{:S(2)}, u32[]{:S(2)}) %collective-permute-start.10) | collective-permute-done | bytes 262176 | tf_op jit(solution)/shard_map/ppermute | solution.py:241
  65.2 6.8 %collective-permute-done.9.refs_0_ = bf16[512,256]{1,0:T(8,128)(2,1)S(1)} collective-permute-done((bf16[512,256]{1,0:T(8,128)(2,1)}, bf16[512,256]{1,0:T(8,128)(2,1)S(1)}, u32[]{:S(2)}, u32[]{:S(2)}) %collective-permute-start.9) | collective-permute-done | bytes 262176 | tf_op jit(solution)/shard_map/ppermute | solution.py:240
  72.1 12.2 %shard_map.102 = (bf16[64,512]{1,0:T(8,128)(2,1)S(1)}, bf16[64,512]{1,0:T(8,128)(2,1)S(1)}) custom-call(s32[4]{0:T(128)S(1)} %pad_add_fusion.off_ref, f32[1,256]{1,0:T(1,128)S(1)} %bitcast.16, bf16[512,256]{1,0:T(8,128)(2,1)S(1)} %collective-permute-done.9.refs_0_, bf16[512,256]{1,0:T(8,128)(2,1)S(1)} %collective-permute-done.10.refs_1_, ...), custom_call_target="tpu_custom_call" | custom-call | tf_op jit(solution)/shard_map/pallas_call | solution.py:207
  84.3 0.1 collective-permute-start.11
  84.4 2.0 %collective-permute-start.12 = (bf16[64,512]{1,0:T(8,128)(2,1)S(1)}, bf16[64,512]{1,0:T(8,128)(2,1)S(1)}, u32[]{:S(2)}, u32[]{:S(2)}) collective-permute-start(bf16[64,512]{1,0:T(8,128)(2,1)S(1)} %get-tuple-element.28), channel_id=1, source_target_pairs={{0,2},{2,4},{4,6},{6,0},{1,3},{3,5},{5,7},{7,1},{8,10},{10,12},{12... | collective-permute-start | bytes 196616 | tf_op jit(solution)/shard_map/ppermute | solution.py:251
  86.4 7.2 %shard_map.103 = bf16[64,512]{1,0:T(8,128)(2,1)S(1)} custom-call(s32[4]{0:T(128)S(1)} %pad_add_fusion.off_ref, f32[1,256]{1,0:T(1,128)S(1)} %bitcast.17, bf16[512,256]{1,0:T(8,128)(2,1)S(1)} %collective-permute-done.13.refs_0_, bf16[1536,256]{1,0:T(8,128)(2,1)S(1)} %constant_dynamic-update-slice_fusion.refs_1_.refs_2_, ...), custom_call_target="tpu_custom_call" | custom-call | tf_op jit(solution)/shard_map/pallas_call | solution.py:207
  93.6 0.1 collective-permute-start.14
  93.7 4.2 %shard_map.101 = f32[64,512]{1,0:T(8,128)S(1)} custom-call(s32[4]{0:T(128)S(1)} %pad_add_fusion.off_ref, f32[1,256]{1,0:T(1,128)S(1)} %bitcast.18, bf16[512,256]{1,0:T(8,128)(2,1)} %row_net.1.refs_0_, bf16[1536,256]{1,0:T(8,128)(2,1)S(1)} %collective-permute-done.3.refs_1_.refs_6_.refs_5_, ...), custom_call_target="tpu_custom_call" | custom-call | tf_op jit(solution)/shard_map/pallas_call | solution.py:207
  97.9 1.6 %collective-permute-done.14 = bf16[64,512]{1,0:T(8,128)(2,1)S(1)} collective-permute-done((bf16[64,512]{1,0:T(8,128)(2,1)S(1)}, bf16[64,512]{1,0:T(8,128)(2,1)S(1)}, u32[]{:S(2)}, u32[]{:S(2)}) %collective-permute-start.14) | collective-permute-done | bytes 65568 | tf_op jit(solution)/shard_map/ppermute | solution.py:253
  99.4 0.7 add_bitcast_fusion
  (17 shorter events, 0.1 us)
Async XLA Ops:
  9.8 37.7 %copy-start = (f32[256]{0:T(256)S(1)}, f32[256]{0:T(256)}, u32[]{:S(2)}) copy-start(f32[256]{0:T(256)} %param.18) | copy-start | bytes 3076
  9.8 24.2 %collective-permute-start = (bf16[512,256]{1,0:T(8,128)(2,1)}, bf16[512,256]{1,0:T(8,128)(2,1)S(1)}, u32[]{:S(2)}, u32[]{:S(2)}) collective-permute-start(bf16[512,256]{1,0:T(8,128)(2,1)} %get-tuple-element.17), channel_id=1, source_target_pairs={{0,32},{32,64},{64,96},{96,0},{1,33},{33,65},{65,97},{97,1},{2,34}... | collective-permute-start | bytes 786440 | tf_op jit(solution)/shard_map/ppermute | solution.py:228
  11.6 22.4 %collective-permute-start.1 = (bf16[512,256]{1,0:T(8,128)(2,1)}, bf16[512,256]{1,0:T(8,128)(2,1)S(1)}, u32[]{:S(2)}, u32[]{:S(2)}) collective-permute-start(bf16[512,256]{1,0:T(8,128)(2,1)} %get-tuple-element.17), channel_id=1, source_target_pairs={{0,96},{32,0},{64,32},{96,64},{1,97},{33,1},{65,33},{97,65},{2,98}... | collective-permute-start | bytes 786440 | tf_op jit(solution)/shard_map/ppermute | solution.py:229
  13.1 20.9 %collective-permute-start.2 = (bf16[512,256]{1,0:T(8,128)(2,1)}, bf16[512,256]{1,0:T(8,128)(2,1)S(1)}, u32[]{:S(2)}, u32[]{:S(2)}) collective-permute-start(bf16[512,256]{1,0:T(8,128)(2,1)} %get-tuple-element.17), channel_id=1, source_target_pairs={{0,64},{32,96},{64,0},{96,32},{1,65},{33,97},{65,1},{97,33},{2,66}... | collective-permute-start | bytes 786440 | tf_op jit(solution)/shard_map/ppermute | solution.py:230
  15.2 18.8 %all-to-all-start = ((bf16[128,4,128]{2,1,0:T(4,128)(2,1)}), bf16[128,4,128]{2,1,0:T(4,128)(2,1)S(1)}, u32[]{:S(2)}, u32[]{:S(2)}) async-start(bf16[128,4,128]{2,1,0:T(4,128)(2,1)} %bitcast.22), calls=%async_computation | async-start | bytes 262144 | tf_op jit(solution)/shard_map/all_to_all | solution.py:231
  34.0 3.8 %copy-start.1 = (bf16[128,4,128]{2,1,0:T(4,128)(2,1)}, bf16[128,4,128]{2,1,0:T(4,128)(2,1)S(1)}, u32[]{:S(2)}) copy-start(bf16[128,4,128]{2,1,0:T(4,128)(2,1)S(1)} %all-to-all-done) | copy-start | bytes 393220
  34.1 13.4 %collective-permute-start.5 = (bf16[1536,256]{1,0:T(8,128)(2,1)S(1)}, bf16[1536,256]{1,0:T(8,128)(2,1)S(1)}, u32[]{:S(2)}, u32[]{:S(2)}) collective-permute-start(bf16[1536,256]{1,0:T(8,128)(2,1)S(1)} %constant_dynamic-update-slice_fusion.refs_1_.refs_2_), channel_id=1, source_target_pairs={{0,1},{1,0},{2,3},{3,2},{4,5},{5,4},{6,7},{7,6},{8,9},{9,8},{10,11... | collective-permute-start | bytes 2359304 | tf_op jit(solution)/shard_map/ppermute | solution.py:238
  34.2 21.1 %collective-permute-start.3 = (bf16[1536,256]{1,0:T(8,128)(2,1)S(1)}, bf16[1536,256]{1,0:T(8,128)(2,1)S(1)}, u32[]{:S(2)}, u32[]{:S(2)}) collective-permute-start(bf16[1536,256]{1,0:T(8,128)(2,1)S(1)} %constant_dynamic-update-slice_fusion.refs_1_.refs_2_), channel_id=1, source_target_pairs={{0,8},{8,16},{16,24},{24,0},{1,9},{9,17},{17,25},{25,1},{2,10},{10... | collective-permute-start | bytes 2359304 | tf_op jit(solution)/shard_map/ppermute | solution.py:236
  35.0 12.4 %collective-permute-start.6 = (bf16[1024,256]{1,0:T(8,128)(2,1)S(1)}, bf16[1024,256]{1,0:T(8,128)(2,1)}, u32[]{:S(2)}, u32[]{:S(2)}) collective-permute-start(bf16[1024,256]{1,0:T(8,128)(2,1)S(1)} %constant_dynamic-update-slice_fusion.3.refs_2_.refs_3_), channel_id=1, source_target_pairs={{0,1},{1,0},{2,3},{3,2},{4,5},{5,4},{6,7},{7,6},{8,9},{9,8},{10,11... | collective-permute-start | bytes 1572872 | tf_op jit(solution)/shard_map/ppermute | solution.py:239
  35.3 16.5 %collective-permute-start.4 = (bf16[1024,256]{1,0:T(8,128)(2,1)S(1)}, bf16[1024,256]{1,0:T(8,128)(2,1)S(1)}, u32[]{:S(2)}, u32[]{:S(2)}) collective-permute-start(bf16[1024,256]{1,0:T(8,128)(2,1)S(1)} %constant_dynamic-update-slice_fusion.3.refs_2_.refs_3_), channel_id=1, source_target_pairs={{0,24},{8,0},{16,8},{24,16},{1,25},{9,1},{17,9},{25,17},{2,26},{10... | collective-permute-start | bytes 1572872 | tf_op jit(solution)/shard_map/ppermute | solution.py:237
  55.3 16.7 %collective-permute-start.7 = (bf16[1536,256]{1,0:T(8,128)(2,1)S(1)}, bf16[1536,256]{1,0:T(8,128)(2,1)S(1)}, u32[]{:S(2)}, u32[]{:S(2)}) collective-permute-start(bf16[1536,256]{1,0:T(8,128)(2,1)S(1)} %collective-permute-done.3.refs_1_.refs_6_.refs_5_), channel_id=1, source_target_pairs={{0,1},{1,0},{2,3},{3,2},{4,5},{5,4},{6,7},{7,6},{8,9},{9,8},{10,11... | collective-permute-start | bytes 2359304 | tf_op jit(solution)/shard_map/ppermute | solution.py:246
  55.3 16.7 %collective-permute-start.8 = (bf16[1024,256]{1,0:T(8,128)(2,1)S(1)}, bf16[1024,256]{1,0:T(8,128)(2,1)S(1)}, u32[]{:S(2)}, u32[]{:S(2)}) collective-permute-start(bf16[1024,256]{1,0:T(8,128)(2,1)S(1)} %collective-permute-done.4.refs_2_.refs_7_.refs_6_), channel_id=1, source_target_pairs={{0,1},{1,0},{2,3},{3,2},{4,5},{5,4},{6,7},{7,6},{8,9},{9,8},{10,11... | collective-permute-start | bytes 1572872 | tf_op jit(solution)/shard_map/ppermute | solution.py:247
  55.8 9.4 %collective-permute-start.10 = (bf16[512,256]{1,0:T(8,128)(2,1)}, bf16[512,256]{1,0:T(8,128)(2,1)S(1)}, u32[]{:S(2)}, u32[]{:S(2)}) collective-permute-start(bf16[512,256]{1,0:T(8,128)(2,1)} %row_net.1.refs_0_), channel_id=1, source_target_pairs={{0,6},{2,0},{4,2},{6,4},{1,7},{3,1},{5,3},{7,5},{8,14},{10,8},{12,... | collective-permute-start | bytes 786440 | tf_op jit(solution)/shard_map/ppermute | solution.py:241
  57.1 15.0 %collective-permute-start.9 = (bf16[512,256]{1,0:T(8,128)(2,1)}, bf16[512,256]{1,0:T(8,128)(2,1)S(1)}, u32[]{:S(2)}, u32[]{:S(2)}) collective-permute-start(bf16[512,256]{1,0:T(8,128)(2,1)} %row_net.1.refs_0_), channel_id=1, source_target_pairs={{0,2},{2,4},{4,6},{6,0},{1,3},{3,5},{5,7},{7,1},{8,10},{10,12},{12... | collective-permute-start | bytes 786440 | tf_op jit(solution)/shard_map/ppermute | solution.py:240
  57.9 28.6 %collective-permute-start.13 = (bf16[512,256]{1,0:T(8,128)(2,1)}, bf16[512,256]{1,0:T(8,128)(2,1)S(1)}, u32[]{:S(2)}, u32[]{:S(2)}) collective-permute-start(bf16[512,256]{1,0:T(8,128)(2,1)} %row_net.1.refs_0_), channel_id=1, source_target_pairs={{0,4},{2,6},{4,0},{6,2},{1,5},{3,7},{5,1},{7,3},{8,12},{10,14},{12... | collective-permute-start | bytes 786440 | tf_op jit(solution)/shard_map/ppermute | solution.py:242
  84.3 13.5 %collective-permute-start.11 = (bf16[64,512]{1,0:T(8,128)(2,1)S(1)}, bf16[64,512]{1,0:T(8,128)(2,1)S(1)}, u32[]{:S(2)}, u32[]{:S(2)}) collective-permute-start(bf16[64,512]{1,0:T(8,128)(2,1)S(1)} %get-tuple-element.27), channel_id=1, source_target_pairs={{0,6},{2,0},{4,2},{6,4},{1,7},{3,1},{5,3},{7,5},{8,14},{10,8},{12,... | collective-permute-start | bytes 196616 | tf_op jit(solution)/shard_map/ppermute | solution.py:250
  84.4 13.5 %collective-permute-start.12 = (bf16[64,512]{1,0:T(8,128)(2,1)S(1)}, bf16[64,512]{1,0:T(8,128)(2,1)S(1)}, u32[]{:S(2)}, u32[]{:S(2)}) collective-permute-start(bf16[64,512]{1,0:T(8,128)(2,1)S(1)} %get-tuple-element.28), channel_id=1, source_target_pairs={{0,2},{2,4},{4,6},{6,0},{1,3},{3,5},{5,7},{7,1},{8,10},{10,12},{12... | collective-permute-start | bytes 196616 | tf_op jit(solution)/shard_map/ppermute | solution.py:251
  93.6 5.8 %collective-permute-start.14 = (bf16[64,512]{1,0:T(8,128)(2,1)S(1)}, bf16[64,512]{1,0:T(8,128)(2,1)S(1)}, u32[]{:S(2)}, u32[]{:S(2)}) collective-permute-start(bf16[64,512]{1,0:T(8,128)(2,1)S(1)} %shard_map.103), channel_id=1, source_target_pairs={{0,4},{2,6},{4,0},{6,2},{1,5},{3,7},{5,1},{7,3},{8,12},{10,14},{12... | collective-permute-start | bytes 196616 | tf_op jit(solution)/shard_map/ppermute | solution.py:253

commit v2 on v1

--- a/solution.py
+++ b/solution.py
@@ -156,8 +156,8 @@
     m=nr*ROWS
 
     def copies(p,a,b):
-        return (pltpu.make_async_copy(a,cv.at[pl.ds(pl.multiple_of(p*PAIR,PAIR),1536)],sem.at[2*p]),
-                pltpu.make_async_copy(b,cv.at[pl.ds(pl.multiple_of(p*PAIR+1536,512),1024)],sem.at[2*p+1]))
+        return (pltpu.make_async_copy(a,cv.at[pl.ds(pl.multiple_of(p*PAIR,PAIR),1280)],sem.at[2*p]),
+                pltpu.make_async_copy(b,cv.at[pl.ds(pl.multiple_of(p*PAIR+1280,256),1280)],sem.at[2*p+1]))
 
     for p in range(pairs):
         for c in copies(p,cols[2*p],cols[2*p+1]): c.start()
@@ -231,27 +231,28 @@
     got = lax.all_to_all(sent, ALL, 0, 0, tiled=True)
     u1, u3, u2, got = lax.optimization_barrier((u1, u3, u2, got))
     feats = row_net(got, w1, b1, w2, b2, w3)
-    ca = jnp.concatenate([own, probe, u1], 0)
-    cb = jnp.concatenate([u3, u2], 0)
+    ca = jnp.concatenate([own, probe, u1[:256]], 0)
+    cb = jnp.concatenate([u1[256:], u3, u2], 0)
     za = lax.ppermute(ca, Z, ring(1))
     zb = lax.ppermute(cb, Z, ring(3))
     pa = lax.ppermute(ca, "core", SWAP)
     pb = lax.ppermute(cb, "core", SWAP)
     f1 = lax.ppermute(feats, "x", ring(1))
     f3 = lax.ppermute(feats, "x", ring(3))
-    f2 = lax.ppermute(feats, "x", ring(2))
-    near = [(ca, cb), (pa, pb)]
-    (first,) = rbf(off, rel, [feats], near, bm=512)
-    za, zb, first = lax.optimization_barrier((za, zb, first))
+    za, zb, held = lax.optimization_barrier((za, zb, feats))
     pza = lax.ppermute(za, "core", SWAP)
     pzb = lax.ppermute(zb, "core", SWAP)
+    near = [(ca, cb), (pa, pb)]
     far = [(za, zb), (pza, pzb)]
+    (first,) = rbf(off, rel, [held], near, bm=512)
+    f1, f3, first = lax.optimization_barrier((f1, f3, first))
+    f2 = lax.ppermute(f1, "x", ring(1))
     t1, t3 = rbf(off, rel, [f1, f3], near + far, out=bf16)
     r1 = lax.ppermute(t1, "x", ring(3))
     r3 = lax.ppermute(t3, "x", ring(1))
     (t2,) = rbf(off, rel, [f2], near + far, out=bf16, bm=512)
     r2 = lax.ppermute(t2, "x", ring(2))
-    (mine,) = rbf(off, rel, [feats], far, first, bm=512)
+    (mine,) = rbf(off, rel, [held], far, first, bm=512)
     total = mine + r1.astype(f32) + r3.astype(f32) + r2.astype(f32)
     return total.T
 

time: 100 us -> 98.2 us (0.982)
  blocking collectives: 0 us -> 19.3 us
  waiting for transfers between devices: 25.5 us -> 6.82 us
  starting transfers between devices: 24.3 us -> 18.5 us
  Pallas kernels: 47.3 us -> 51.3 us
  local copies, waits for them, and re-layouts: 2 us -> 0.99 us
    all_to_all x0 -> x1, blocking collectives: none -> 19.3 us  [steps(): got = lax.all_to_all(sent, ALL, 0, 0, tiled=True)]
    all_to_all x1 -> x0, starting transfers between devices: 9.41 us -> none  [steps(): got = lax.all_to_all(sent, ALL, 0, 0, tiled=True)]
    all_to_all x1 -> x0, waiting for transfers between devices: 7.43 us -> none  [steps(): got = lax.all_to_all(sent, ALL, 0, 0, tiled=True)]
    ppermute x1, waiting for transfers between devices: 6.84 us -> 0.55 us  [steps(): f1 = lax.ppermute(feats, 'x', ring(1))]
    ppermute x1, waiting for transfers between devices: 6.16 us -> 0.01 us  [steps(): f3 = lax.ppermute(feats, 'x', ring(3))]
    ppermute x1, waiting for transfers between devices: 0.01 us -> 4.12 us  [steps(): zb = lax.ppermute(cb, Z, ring(3))]
    pallas_call x4, Pallas kernels: 27.9 us -> 32 us  [rbf(): pl.pallas_call(functools.partial(rbf_kernel, nr=nr, pairs=npairs, with_in...]
    ppermute x1, starting transfers between devices: 0.09 us -> 3.35 us  [steps(): r2 = lax.ppermute(t2, 'x', ring(2))]
  transfers between devices with their start and end apart: 16 -> 15, of which waited for: 5 -> 3; matrix products, arithmetic and copies ran while one was open for 2% -> 0% of each run, Pallas kernels for 37% -> 42%
where the time goes in v2:
time: 98.2 us; the launch traced here: 97.9 us
  Pallas kernels  51.3 us (52%)
  blocking collectives  19.3 us (20%)
  starting transfers between devices  18.5 us (19%)
  waiting for transfers between devices  6.82 us (7%)
  local copies, waits for them, and re-layouts  0.99 us (1%)
    pallas_call x4, Pallas kernels, rbf(): pl.pallas_call(functools.partial(rbf_kernel, nr=nr, pairs=npairs, with_in...  32 us
    all_to_all x1, blocking collectives, steps(): got = lax.all_to_all(sent, ALL, 0, 0, tiled=True)  19.3 us
    pallas_call x1, Pallas kernels, front(): pl.pallas_call(front_kernel, in_specs=[SM, VM, VM, VM, VM, *WEIGHT_SPECS]...  9.74 us
    pallas_call x1, Pallas kernels, row_net(): pl.pallas_call(row_kernel, in_specs=[VM, *WEIGHT_SPECS], out_specs=VM, ou...  9.56 us
    ppermute x1, waiting for transfers between devices, steps(): zb = lax.ppermute(cb, Z, ring(3))  4.12 us
    ppermute x1, starting transfers between devices, steps(): r2 = lax.ppermute(t2, 'x', ring(2))  3.35 us
    ppermute x1, starting transfers between devices, steps(): r1 = lax.ppermute(t1, 'x', ring(3))  3.28 us
    ppermute x1, starting transfers between devices, steps(): f3 = lax.ppermute(feats, 'x', ring(3))  2.66 us
  transfers between devices with their start and end apart: 15, of which 3 were waited for; matrix products, arithmetic and copies ran while one was open for 0% of the time, Pallas kernels for 42%

profile of v2, /device:TPU:0, one launch (start us, length us, event | category | flops | bytes accessed | tf_op | source)
XLA Modules:
  0.0 97.9 jit_solution(297325743235792873)
XLA Ops:
  0.0 9.7 %front.1 = (bf16[512,128]{1,0:T(8,128)(2,1)}, bf16[512,256]{1,0:T(8,128)(2,1)}, bf16[512,256]{1,0:T(8,128)(2,1)}) custom-call(s32[1]{0:T(128)} %bitcast.y_ref, s32[1,512]{1,0:T(1,128)} %bitcast.28, bf16[40,512]{1,0:T(8,128)(2,1)} %bitcast.23, bf16[40,2048]{1,0:T(8,128)(2,1)} %bitcast.21, f32[64,2048]{1,0:T(8,128)} %bitcast.20, bf16[40,2048]{1,0:T(8,128)(2,1)} %w1_ref.3, ...), custom_call_target="tpu_custom_call" | custom-call | tf_op jit(solution)/shard_map/front/pallas_call | solution.py:124
  9.8 1.8 %collective-permute-start = (bf16[512,256]{1,0:T(8,128)(2,1)}, bf16[512,256]{1,0:T(8,128)(2,1)S(1)}, u32[]{:S(2)}, u32[]{:S(2)}) collective-permute-start(bf16[512,256]{1,0:T(8,128)(2,1)} %get-tuple-element.20), channel_id=1, source_target_pairs={{0,32},{32,64},{64,96},{96,0},{1,33},{33,65},{65,97},{97,1},{2,34}... | collective-permute-start | bytes 786440 | tf_op jit(solution)/shard_map/ppermute | solution.py:228
  11.5 1.5 %collective-permute-start.1 = (bf16[512,256]{1,0:T(8,128)(2,1)}, bf16[512,256]{1,0:T(8,128)(2,1)S(1)}, u32[]{:S(2)}, u32[]{:S(2)}) collective-permute-start(bf16[512,256]{1,0:T(8,128)(2,1)} %get-tuple-element.20), channel_id=1, source_target_pairs={{0,96},{32,0},{64,32},{96,64},{1,97},{33,1},{65,33},{97,65},{2,98}... | collective-permute-start | bytes 786440 | tf_op jit(solution)/shard_map/ppermute | solution.py:229
  13.1 2.1 %collective-permute-start.2 = (bf16[512,256]{1,0:T(8,128)(2,1)}, bf16[512,256]{1,0:T(8,128)(2,1)S(1)}, u32[]{:S(2)}, u32[]{:S(2)}) collective-permute-start(bf16[512,256]{1,0:T(8,128)(2,1)} %get-tuple-element.20), channel_id=1, source_target_pairs={{0,64},{32,96},{64,0},{96,32},{1,65},{33,97},{65,1},{97,33},{2,66}... | collective-permute-start | bytes 786440 | tf_op jit(solution)/shard_map/ppermute | solution.py:230
  15.2 19.3 %all_to_all.12 = bf16[128,4,128]{2,1,0:T(4,128)(2,1)} all-to-all(bf16[128,4,128]{2,1,0:T(4,128)(2,1)} %bitcast.22), channel_id=1, replica_groups=mesh['y'=4,'zh'=2,'zl'=2,'x'=4,'core'=2] {'y','zh','zl','x','core'}, dimensions={0} | all-to-all | bytes 262144 | tf_op jit(solution)/shard_map/all_to_all | solution.py:231
  34.5 0.0 collective-permute-done
  34.5 0.0 collective-permute-done.1
  34.6 0.7 collective-permute-start.4
  35.3 0.0 copy-start.2
  35.4 1.4 %collective-permute-start.3 = (bf16[1280,256]{1,0:T(8,128)(2,1)S(1)}, bf16[1280,256]{1,0:T(8,128)(2,1)S(1)}, u32[]{:S(2)}, u32[]{:S(2)}) collective-permute-start(bf16[1280,256]{1,0:T(8,128)(2,1)S(1)} %pad_maximum_fusion.refs_1_.refs_2_), channel_id=1, source_target_pairs={{0,8},{8,16},{16,24},{24,0},{1,9},{9,17},{17,25},{25,1},{2,10},{10... | collective-permute-start | bytes 1966088 | tf_op jit(solution)/shard_map/ppermute | solution.py:236
  36.8 0.0 collective-permute-start.10
  36.8 0.5 collective-permute-start.9
  37.3 9.6 %row_net.1.refs_0_ = bf16[512,256]{1,0:T(8,128)(2,1)} custom-call(bf16[512,128]{1,0:T(8,128)(2,1)} %bitcast.19, bf16[40,2048]{1,0:T(8,128)(2,1)} %w1_ref.3, f32[1,2048]{1,0:T(1,128)} %bitcast.25, bf16[2048,2048]{1,0:T(8,128)(2,1)} %w2_ref.3, f32[1,2048]{1,0:T(1,128)} %bitcast.27, bf16[2048,256]{1,0:T(8,128)(2,1)} %w3_ref.3), custom_call_target="tpu_custom_call" | custom-call | tf_op jit(solution)/shard_map/row_net/pallas_call | solution.py:140
  46.9 4.1 %collective-permute-done.4.refs_2_.refs_7_.refs_6_ = bf16[1280,256]{1,0:T(8,128)(2,1)S(1)} collective-permute-done((bf16[1280,256]{1,0:T(8,128)(2,1)S(1)}, bf16[1280,256]{1,0:T(8,128)(2,1)S(1)}, u32[]{:S(2)}, u32[]{:S(2)}) %collective-permute-start.4) | collective-permute-done | bytes 655392 | tf_op jit(solution)/shard_map/ppermute | solution.py:237
  51.0 2.1 %collective-permute-done.3.refs_1_.refs_6_.refs_5_ = bf16[1280,256]{1,0:T(8,128)(2,1)S(1)} collective-permute-done((bf16[1280,256]{1,0:T(8,128)(2,1)S(1)}, bf16[1280,256]{1,0:T(8,128)(2,1)S(1)}, u32[]{:S(2)}, u32[]{:S(2)}) %collective-permute-start.3) | collective-permute-done | bytes 655392 | tf_op jit(solution)/shard_map/ppermute | solution.py:236
  53.1 0.0 collective-permute-start.5
  53.1 0.5 collective-permute-start.6
  53.6 0.6 collective-permute-start.7
  54.2 2.7 %collective-permute-start.8 = (bf16[512,256]{1,0:T(8,128)(2,1)}, bf16[512,256]{1,0:T(8,128)(2,1)}, u32[]{:S(2)}, u32[]{:S(2)}) collective-permute-start(bf16[512,256]{1,0:T(8,128)(2,1)} %row_net.1.refs_0_), channel_id=1, source_target_pairs={{0,6},{2,0},{4,2},{6,4},{1,7},{3,1},{5,3},{7,5},{8,14},{10,8},{12,... | collective-permute-start | bytes 786440 | tf_op jit(solution)/shard_map/ppermute | solution.py:241
  56.9 0.1 pad_add_fusion.off_ref
  56.9 0.0 collective-permute-done.9.refs_3_.refs_4_
  56.9 0.9 copy-done
  57.9 4.8 %shard_map.100.refs_5_ = f32[64,512]{1,0:T(8,128)S(1)} custom-call(s32[4]{0:T(128)S(1)} %pad_add_fusion.off_ref, f32[1,256]{1,0:T(1,128)S(1)} %bitcast.15, bf16[512,256]{1,0:T(8,128)(2,1)S(1)} %copy-done, bf16[1280,256]{1,0:T(8,128)(2,1)S(1)} %pad_maximum_fusion.refs_1_.refs_2_, bf16[1280,256]{1,0:T(8,128)(2,1)S(1)} %pad_maximum_fusion.1.refs_2_.refs_3_, ...), custom_call_target="tpu_custom_call" | custom-call | tf_op jit(solution)/shard_map/pallas_call | solution.py:207
  62.7 0.6 collective-permute-done.7.refs_0_
  63.3 0.0 collective-permute-start.13
  63.3 0.0 collective-permute-done.5.refs_3_.refs_8_.refs_7_
  63.3 13.6 %shard_map.102 = (bf16[64,512]{1,0:T(8,128)(2,1)S(1)}, bf16[64,512]{1,0:T(8,128)(2,1)S(1)}) custom-call(s32[4]{0:T(128)S(1)} %pad_add_fusion.off_ref, f32[1,256]{1,0:T(1,128)S(1)} %bitcast.16, bf16[512,256]{1,0:T(8,128)(2,1)S(1)} %collective-permute-done.7.refs_0_, bf16[512,256]{1,0:T(8,128)(2,1)} %collective-permute-done.8.refs_1_, ...), custom_call_target="tpu_custom_call" | custom-call | tf_op jit(solution)/shard_map/pallas_call | solution.py:207
  76.9 3.3 %collective-permute-start.11 = (bf16[64,512]{1,0:T(8,128)(2,1)S(1)}, bf16[64,512]{1,0:T(8,128)(2,1)S(1)}, u32[]{:S(2)}, u32[]{:S(2)}) collective-permute-start(bf16[64,512]{1,0:T(8,128)(2,1)S(1)} %get-tuple-element.33), channel_id=1, source_target_pairs={{0,6},{2,0},{4,2},{6,4},{1,7},{3,1},{5,3},{7,5},{8,14},{10,8},{12,... | collective-permute-start | bytes 196616 | tf_op jit(solution)/shard_map/ppermute | solution.py:251
  80.2 8.6 %shard_map.103 = bf16[64,512]{1,0:T(8,128)(2,1)S(1)} custom-call(s32[4]{0:T(128)S(1)} %pad_add_fusion.off_ref, f32[1,256]{1,0:T(1,128)S(1)} %bitcast.17, bf16[512,256]{1,0:T(8,128)(2,1)S(1)} %collective-permute-done.13.refs_0_, bf16[1280,256]{1,0:T(8,128)(2,1)S(1)} %pad_maximum_fusion.refs_1_.refs_2_, ...), custom_call_target="tpu_custom_call" | custom-call | tf_op jit(solution)/shard_map/pallas_call | solution.py:207
  88.8 3.4 %collective-permute-start.14 = (bf16[64,512]{1,0:T(8,128)(2,1)S(1)}, bf16[64,512]{1,0:T(8,128)(2,1)S(1)}, u32[]{:S(2)}, u32[]{:S(2)}) collective-permute-start(bf16[64,512]{1,0:T(8,128)(2,1)S(1)} %shard_map.103), channel_id=1, source_target_pairs={{0,4},{2,6},{4,0},{6,2},{1,5},{3,7},{5,1},{7,3},{8,12},{10,14},{12... | collective-permute-start | bytes 196616 | tf_op jit(solution)/shard_map/ppermute | solution.py:254
  92.2 5.0 %shard_map.101 = f32[64,512]{1,0:T(8,128)S(1)} custom-call(s32[4]{0:T(128)S(1)} %pad_add_fusion.off_ref, f32[1,256]{1,0:T(1,128)S(1)} %bitcast.18, bf16[512,256]{1,0:T(8,128)(2,1)S(1)} %copy-done.1, bf16[1280,256]{1,0:T(8,128)(2,1)S(1)} %collective-permute-done.3.refs_1_.refs_6_.refs_5_, ...), custom_call_target="tpu_custom_call" | custom-call | tf_op jit(solution)/shard_map/pallas_call | solution.py:207
  97.2 0.7 add_bitcast_fusion
  (20 shorter events, 0.1 us)
Async XLA Ops:
  9.7 25.5 %copy-start.3 = (bf16[512,256]{1,0:T(8,128)(2,1)S(1)}, bf16[512,256]{1,0:T(8,128)(2,1)}, u32[]{:S(2)}) copy-start(bf16[512,256]{1,0:T(8,128)(2,1)} %get-tuple-element.20) | copy-start | bytes 786436
  9.8 25.5 %copy-start.4 = (bf16[512,256]{1,0:T(8,128)(2,1)S(1)}, bf16[512,256]{1,0:T(8,128)(2,1)}, u32[]{:S(2)}) copy-start(bf16[512,256]{1,0:T(8,128)(2,1)} %get-tuple-element.21) | copy-start | bytes 786436
  9.8 24.7 %collective-permute-start = (bf16[512,256]{1,0:T(8,128)(2,1)}, bf16[512,256]{1,0:T(8,128)(2,1)S(1)}, u32[]{:S(2)}, u32[]{:S(2)}) collective-permute-start(bf16[512,256]{1,0:T(8,128)(2,1)} %get-tuple-element.20), channel_id=1, source_target_pairs={{0,32},{32,64},{64,96},{96,0},{1,33},{33,65},{65,97},{97,1},{2,34}... | collective-permute-start | bytes 786440 | tf_op jit(solution)/shard_map/ppermute | solution.py:228
  11.5 23.0 %collective-permute-start.1 = (bf16[512,256]{1,0:T(8,128)(2,1)}, bf16[512,256]{1,0:T(8,128)(2,1)S(1)}, u32[]{:S(2)}, u32[]{:S(2)}) collective-permute-start(bf16[512,256]{1,0:T(8,128)(2,1)} %get-tuple-element.20), channel_id=1, source_target_pairs={{0,96},{32,0},{64,32},{96,64},{1,97},{33,1},{65,33},{97,65},{2,98}... | collective-permute-start | bytes 786440 | tf_op jit(solution)/shard_map/ppermute | solution.py:229
  13.1 21.4 %collective-permute-start.2 = (bf16[512,256]{1,0:T(8,128)(2,1)}, bf16[512,256]{1,0:T(8,128)(2,1)S(1)}, u32[]{:S(2)}, u32[]{:S(2)}) collective-permute-start(bf16[512,256]{1,0:T(8,128)(2,1)} %get-tuple-element.20), channel_id=1, source_target_pairs={{0,64},{32,96},{64,0},{96,32},{1,65},{33,97},{65,1},{97,33},{2,66}... | collective-permute-start | bytes 786440 | tf_op jit(solution)/shard_map/ppermute | solution.py:230
  34.6 16.4 %collective-permute-start.4 = (bf16[1280,256]{1,0:T(8,128)(2,1)S(1)}, bf16[1280,256]{1,0:T(8,128)(2,1)S(1)}, u32[]{:S(2)}, u32[]{:S(2)}) collective-permute-start(bf16[1280,256]{1,0:T(8,128)(2,1)S(1)} %pad_maximum_fusion.1.refs_2_.refs_3_), channel_id=1, source_target_pairs={{0,24},{8,0},{16,8},{24,16},{1,25},{9,1},{17,9},{25,17},{2,26},{10... | collective-permute-start | bytes 1966088 | tf_op jit(solution)/shard_map/ppermute | solution.py:237
  35.3 21.6 %copy-start.2 = (f32[256]{0:T(256)S(1)}, f32[256]{0:T(256)}, u32[]{:S(2)}) copy-start(f32[256]{0:T(256)} %param.18) | copy-start | bytes 3076
  35.4 17.8 %collective-permute-start.3 = (bf16[1280,256]{1,0:T(8,128)(2,1)S(1)}, bf16[1280,256]{1,0:T(8,128)(2,1)S(1)}, u32[]{:S(2)}, u32[]{:S(2)}) collective-permute-start(bf16[1280,256]{1,0:T(8,128)(2,1)S(1)} %pad_maximum_fusion.refs_1_.refs_2_), channel_id=1, source_target_pairs={{0,8},{8,16},{16,24},{24,0},{1,9},{9,17},{17,25},{25,1},{2,10},{10... | collective-permute-start | bytes 1966088 | tf_op jit(solution)/shard_map/ppermute | solution.py:236
  36.8 17.4 %collective-permute-start.10 = (bf16[1280,256]{1,0:T(8,128)(2,1)S(1)}, bf16[1280,256]{1,0:T(8,128)(2,1)S(1)}, u32[]{:S(2)}, u32[]{:S(2)}) collective-permute-start(bf16[1280,256]{1,0:T(8,128)(2,1)S(1)} %pad_maximum_fusion.1.refs_2_.refs_3_), channel_id=1, source_target_pairs={{0,1},{1,0},{2,3},{3,2},{4,5},{5,4},{6,7},{7,6},{8,9},{9,8},{10,11... | collective-permute-start | bytes 1966088 | tf_op jit(solution)/shard_map/ppermute | solution.py:239
  36.8 20.1 %collective-permute-start.9 = (bf16[1280,256]{1,0:T(8,128)(2,1)S(1)}, bf16[1280,256]{1,0:T(8,128)(2,1)}, u32[]{:S(2)}, u32[]{:S(2)}) collective-permute-start(bf16[1280,256]{1,0:T(8,128)(2,1)S(1)} %pad_maximum_fusion.refs_1_.refs_2_), channel_id=1, source_target_pairs={{0,1},{1,0},{2,3},{3,2},{4,5},{5,4},{6,7},{7,6},{8,9},{9,8},{10,11... | collective-permute-start | bytes 1966088 | tf_op jit(solution)/shard_map/ppermute | solution.py:238
  53.1 10.2 %collective-permute-start.5 = (bf16[1280,256]{1,0:T(8,128)(2,1)S(1)}, bf16[1280,256]{1,0:T(8,128)(2,1)}, u32[]{:S(2)}, u32[]{:S(2)}) collective-permute-start(bf16[1280,256]{1,0:T(8,128)(2,1)S(1)} %collective-permute-done.3.refs_1_.refs_6_.refs_5_), channel_id=1, source_target_pairs={{0,1},{1,0},{2,3},{3,2},{4,5},{5,4},{6,7},{7,6},{8,9},{9,8},{10,11... | collective-permute-start | bytes 1966088 | tf_op jit(solution)/shard_map/ppermute | solution.py:243
  53.1 10.2 %collective-permute-start.6 = (bf16[1280,256]{1,0:T(8,128)(2,1)S(1)}, bf16[1280,256]{1,0:T(8,128)(2,1)}, u32[]{:S(2)}, u32[]{:S(2)}) collective-permute-start(bf16[1280,256]{1,0:T(8,128)(2,1)S(1)} %collective-permute-done.4.refs_2_.refs_7_.refs_6_), channel_id=1, source_target_pairs={{0,1},{1,0},{2,3},{3,2},{4,5},{5,4},{6,7},{7,6},{8,9},{9,8},{10,11... | collective-permute-start | bytes 1966088 | tf_op jit(solution)/shard_map/ppermute | solution.py:244
  53.6 9.6 %collective-permute-start.7 = (bf16[512,256]{1,0:T(8,128)(2,1)}, bf16[512,256]{1,0:T(8,128)(2,1)S(1)}, u32[]{:S(2)}, u32[]{:S(2)}) collective-permute-start(bf16[512,256]{1,0:T(8,128)(2,1)} %row_net.1.refs_0_), channel_id=1, source_target_pairs={{0,2},{2,4},{4,6},{6,0},{1,3},{3,5},{5,7},{7,1},{8,10},{10,12},{12... | collective-permute-start | bytes 786440 | tf_op jit(solution)/shard_map/ppermute | solution.py:240
  54.2 9.1 %collective-permute-start.8 = (bf16[512,256]{1,0:T(8,128)(2,1)}, bf16[512,256]{1,0:T(8,128)(2,1)}, u32[]{:S(2)}, u32[]{:S(2)}) collective-permute-start(bf16[512,256]{1,0:T(8,128)(2,1)} %row_net.1.refs_0_), channel_id=1, source_target_pairs={{0,6},{2,0},{4,2},{6,4},{1,7},{3,1},{5,3},{7,5},{8,14},{10,8},{12,... | collective-permute-start | bytes 786440 | tf_op jit(solution)/shard_map/ppermute | solution.py:241
  56.9 1.0 copy-start
  63.3 16.9 %collective-permute-start.13 = (bf16[512,256]{1,0:T(8,128)(2,1)S(1)}, bf16[512,256]{1,0:T(8,128)(2,1)S(1)}, u32[]{:S(2)}, u32[]{:S(2)}) collective-permute-start(bf16[512,256]{1,0:T(8,128)(2,1)S(1)} %collective-permute-done.7.refs_0_), channel_id=1, source_target_pairs={{0,2},{2,4},{4,6},{6,0},{1,3},{3,5},{5,7},{7,1},{8,10},{10,12},{12... | collective-permute-start | bytes 786440 | tf_op jit(solution)/shard_map/ppermute | solution.py:249
  76.9 20.3 %collective-permute-start.11 = (bf16[64,512]{1,0:T(8,128)(2,1)S(1)}, bf16[64,512]{1,0:T(8,128)(2,1)S(1)}, u32[]{:S(2)}, u32[]{:S(2)}) collective-permute-start(bf16[64,512]{1,0:T(8,128)(2,1)S(1)} %get-tuple-element.33), channel_id=1, source_target_pairs={{0,6},{2,0},{4,2},{6,4},{1,7},{3,1},{5,3},{7,5},{8,14},{10,8},{12,... | collective-permute-start | bytes 196616 | tf_op jit(solution)/shard_map/ppermute | solution.py:251
  80.2 12.0 %copy-start.1 = (bf16[512,256]{1,0:T(8,128)(2,1)S(1)}, bf16[512,256]{1,0:T(8,128)(2,1)}, u32[]{:S(2)}) copy-start(bf16[512,256]{1,0:T(8,128)(2,1)} %row_net.1.refs_0_) | copy-start | bytes 786436
  80.2 17.0 %collective-permute-start.12 = (bf16[64,512]{1,0:T(8,128)(2,1)S(1)}, bf16[64,512]{1,0:T(8,128)(2,1)S(1)}, u32[]{:S(2)}, u32[]{:S(2)}) collective-permute-start(bf16[64,512]{1,0:T(8,128)(2,1)S(1)} %get-tuple-element.34), channel_id=1, source_target_pairs={{0,2},{2,4},{4,6},{6,0},{1,3},{3,5},{5,7},{7,1},{8,10},{10,12},{12... | collective-permute-start | bytes 196616 | tf_op jit(solution)/shard_map/ppermute | solution.py:252
  88.8 8.4 %collective-permute-start.14 = (bf16[64,512]{1,0:T(8,128)(2,1)S(1)}, bf16[64,512]{1,0:T(8,128)(2,1)S(1)}, u32[]{:S(2)}, u32[]{:S(2)}) collective-permute-start(bf16[64,512]{1,0:T(8,128)(2,1)S(1)} %shard_map.103), channel_id=1, source_target_pairs={{0,4},{2,6},{4,0},{6,2},{1,5},{3,7},{5,1},{7,3},{8,12},{10,14},{12... | collective-permute-start | bytes 196616 | tf_op jit(solution)/shard_map/ppermute | solution.py:254

commit v3 on v2

--- a/solution.py
+++ b/solution.py
@@ -105,7 +105,7 @@
 VM = pl.BlockSpec(memory_space=pltpu.VMEM)
 SM = pl.BlockSpec(memory_space=pltpu.SMEM)
 HB = pl.BlockSpec(memory_space=pltpu.HBM)
-LIMIT = pltpu.CompilerParams(vmem_limit_bytes=30 * 2**20)
+LIMIT = pltpu.CompilerParams(vmem_limit_bytes=22 * 2**20)
 WEIGHT_SPECS = [VM, VM, HB, VM, HB]
 
 
@@ -239,12 +239,14 @@
     pb = lax.ppermute(cb, "core", SWAP)
     f1 = lax.ppermute(feats, "x", ring(1))
     f3 = lax.ppermute(feats, "x", ring(3))
-    za, zb, held = lax.optimization_barrier((za, zb, feats))
+    held = pltpu.with_memory_space_constraint(feats, pltpu.HBM)
+    near = [(ca, cb), (pa, pb)]
+    (first,) = rbf(off, rel, [held], near[:1], bm=512)
+    za, zb, first = lax.optimization_barrier((za, zb, first))
     pza = lax.ppermute(za, "core", SWAP)
     pzb = lax.ppermute(zb, "core", SWAP)
-    near = [(ca, cb), (pa, pb)]
     far = [(za, zb), (pza, pzb)]
-    (first,) = rbf(off, rel, [held], near, bm=512)
+    (first,) = rbf(off, rel, [held], near[1:], first, bm=512)
     f1, f3, first = lax.optimization_barrier((f1, f3, first))
     f2 = lax.ppermute(f1, "x", ring(1))
     t1, t3 = rbf(off, rel, [f1, f3], near + far, out=bf16)

time: 98.2 us -> 96.7 us (0.985)
    ppermute x1, waiting for transfers between devices: 4.12 us -> 0.97 us  [steps(): zb = lax.ppermute(cb, Z, ring(3))]
    ppermute x1, waiting for transfers between devices: 0.55 us -> 2.97 us  [steps(): f1 = lax.ppermute(feats, 'x', ring(1))]
    pallas_call x4 -> x5, Pallas kernels: 32 us -> 32.2 us  [rbf(): pl.pallas_call(functools.partial(rbf_kernel, nr=nr, pairs=npairs, with_in...]
  transfers between devices with their start and end apart: 15 -> 15, of which waited for: 3 -> 3; matrix products, arithmetic and copies ran while one was open for 0% -> 0% of each run, Pallas kernels for 42% -> 43%
where the time goes in v3:
time: 96.7 us; the launch traced here: 96.3 us
  Pallas kernels  51.5 us (53%)
  blocking collectives  19.3 us (20%)
  starting transfers between devices  18.4 us (19%)
  waiting for transfers between devices  6.07 us (6%)
    pallas_call x5, Pallas kernels, rbf(): pl.pallas_call(functools.partial(rbf_kernel, nr=nr, pairs=npairs, with_in...  32.2 us
    all_to_all x1, blocking collectives, steps(): got = lax.all_to_all(sent, ALL, 0, 0, tiled=True)  19.3 us
    pallas_call x1, Pallas kernels, front(): pl.pallas_call(front_kernel, in_specs=[SM, VM, VM, VM, VM, *WEIGHT_SPECS]...  9.73 us
    pallas_call x1, Pallas kernels, row_net(): pl.pallas_call(row_kernel, in_specs=[VM, *WEIGHT_SPECS], out_specs=VM, ou...  9.57 us
    ppermute x1, starting transfers between devices, steps(): r1 = lax.ppermute(t1, 'x', ring(3))  3.29 us
    ppermute x1, starting transfers between devices, steps(): r2 = lax.ppermute(t2, 'x', ring(2))  3.28 us
    ppermute x1, waiting for transfers between devices, steps(): f1 = lax.ppermute(feats, 'x', ring(1))  2.97 us
    ppermute x1, starting transfers between devices, steps(): f3 = lax.ppermute(feats, 'x', ring(3))  2.66 us
  transfers between devices with their start and end apart: 15, of which 3 were waited for; matrix products, arithmetic and copies ran while one was open for 0% of the time, Pallas kernels for 43%

profile of v3, /device:TPU:0, one launch (start us, length us, event | category | flops | bytes accessed | tf_op | source)
XLA Modules:
  0.0 96.3 jit_solution(1935066200520654330)
XLA Ops:
  0.0 9.7 %front.1 = (bf16[512,128]{1,0:T(8,128)(2,1)}, bf16[512,256]{1,0:T(8,128)(2,1)}, bf16[512,256]{1,0:T(8,128)(2,1)}) custom-call(s32[1]{0:T(128)} %bitcast.y_ref, s32[1,512]{1,0:T(1,128)} %bitcast.29, bf16[40,512]{1,0:T(8,128)(2,1)} %bitcast.24, bf16[40,2048]{1,0:T(8,128)(2,1)} %bitcast.22, f32[64,2048]{1,0:T(8,128)} %bitcast.21, bf16[40,2048]{1,0:T(8,128)(2,1)} %w1_ref.3, ...), custom_call_target="tpu_custom_call" | custom-call | tf_op jit(solution)/shard_map/front/pallas_call | solution.py:124
  9.8 1.8 %collective-permute-start = (bf16[512,256]{1,0:T(8,128)(2,1)}, bf16[512,256]{1,0:T(8,128)(2,1)S(1)}, u32[]{:S(2)}, u32[]{:S(2)}) collective-permute-start(bf16[512,256]{1,0:T(8,128)(2,1)} %get-tuple-element.20), channel_id=1, source_target_pairs={{0,32},{32,64},{64,96},{96,0},{1,33},{33,65},{65,97},{97,1},{2,34}... | collective-permute-start | bytes 786440 | tf_op jit(solution)/shard_map/ppermute | solution.py:228
  11.5 1.5 %collective-permute-start.1 = (bf16[512,256]{1,0:T(8,128)(2,1)}, bf16[512,256]{1,0:T(8,128)(2,1)S(1)}, u32[]{:S(2)}, u32[]{:S(2)}) collective-permute-start(bf16[512,256]{1,0:T(8,128)(2,1)} %get-tuple-element.20), channel_id=1, source_target_pairs={{0,96},{32,0},{64,32},{96,64},{1,97},{33,1},{65,33},{97,65},{2,98}... | collective-permute-start | bytes 786440 | tf_op jit(solution)/shard_map/ppermute | solution.py:229
  13.1 2.1 %collective-permute-start.2 = (bf16[512,256]{1,0:T(8,128)(2,1)}, bf16[512,256]{1,0:T(8,128)(2,1)S(1)}, u32[]{:S(2)}, u32[]{:S(2)}) collective-permute-start(bf16[512,256]{1,0:T(8,128)(2,1)} %get-tuple-element.20), channel_id=1, source_target_pairs={{0,64},{32,96},{64,0},{96,32},{1,65},{33,97},{65,1},{97,33},{2,66}... | collective-permute-start | bytes 786440 | tf_op jit(solution)/shard_map/ppermute | solution.py:230
  15.2 19.3 %all_to_all.12 = bf16[128,4,128]{2,1,0:T(4,128)(2,1)} all-to-all(bf16[128,4,128]{2,1,0:T(4,128)(2,1)} %bitcast.23), channel_id=1, replica_groups=mesh['y'=4,'zh'=2,'zl'=2,'x'=4,'core'=2] {'y','zh','zl','x','core'}, dimensions={0} | all-to-all | bytes 262144 | tf_op jit(solution)/shard_map/all_to_all | solution.py:231
  34.5 0.0 collective-permute-done
  34.6 0.7 collective-permute-start.4
  35.3 1.4 %collective-permute-start.3 = (bf16[1280,256]{1,0:T(8,128)(2,1)S(1)}, bf16[1280,256]{1,0:T(8,128)(2,1)S(1)}, u32[]{:S(2)}, u32[]{:S(2)}) collective-permute-start(bf16[1280,256]{1,0:T(8,128)(2,1)S(1)} %pad_maximum_fusion.refs_1_.refs_2_), channel_id=1, source_target_pairs={{0,8},{8,16},{16,24},{24,0},{1,9},{9,17},{17,25},{25,1},{2,10},{10... | collective-permute-start | bytes 1966088 | tf_op jit(solution)/shard_map/ppermute | solution.py:236
  36.8 0.5 collective-permute-start.9
  37.3 0.1 pad_add_fusion.off_ref
  37.4 9.6 %row_net.1.refs_0_ = bf16[512,256]{1,0:T(8,128)(2,1)} custom-call(bf16[512,128]{1,0:T(8,128)(2,1)} %bitcast.20, bf16[40,2048]{1,0:T(8,128)(2,1)} %w1_ref.3, f32[1,2048]{1,0:T(1,128)} %bitcast.26, bf16[2048,2048]{1,0:T(8,128)(2,1)} %w2_ref.3, f32[1,2048]{1,0:T(1,128)} %bitcast.28, bf16[2048,256]{1,0:T(8,128)(2,1)} %w3_ref.3), custom_call_target="tpu_custom_call" | custom-call | tf_op jit(solution)/shard_map/row_net/pallas_call | solution.py:140
  47.0 3.0 %shard_map.100.refs_3_ = f32[64,512]{1,0:T(8,128)S(1)} custom-call(s32[4]{0:T(128)S(1)} %pad_add_fusion.off_ref, f32[1,256]{1,0:T(1,128)S(1)} %bitcast.15, bf16[512,256]{1,0:T(8,128)(2,1)} %row_net.1.refs_0_, bf16[1280,256]{1,0:T(8,128)(2,1)S(1)} %pad_maximum_fusion.refs_1_.refs_2_, bf16[1280,256]{1,0:T(8,128)(2,1)S(1)} %pad_maximum_fusion.1.refs_2_.refs_3_), custom_call_target="tpu_custom_call" | custom-call | tf_op jit(solution)/shard_map/pallas_call | solution.py:207
  50.0 1.0 %collective-permute-done.4.refs_2_.refs_7_.refs_6_ = bf16[1280,256]{1,0:T(8,128)(2,1)S(1)} collective-permute-done((bf16[1280,256]{1,0:T(8,128)(2,1)S(1)}, bf16[1280,256]{1,0:T(8,128)(2,1)S(1)}, u32[]{:S(2)}, u32[]{:S(2)}) %collective-permute-start.4) | collective-permute-done | bytes 655392 | tf_op jit(solution)/shard_map/ppermute | solution.py:237
  51.0 2.1 %collective-permute-done.3.refs_1_.refs_6_.refs_5_ = bf16[1280,256]{1,0:T(8,128)(2,1)S(1)} collective-permute-done((bf16[1280,256]{1,0:T(8,128)(2,1)S(1)}, bf16[1280,256]{1,0:T(8,128)(2,1)S(1)}, u32[]{:S(2)}, u32[]{:S(2)}) %collective-permute-start.3) | collective-permute-done | bytes 655392 | tf_op jit(solution)/shard_map/ppermute | solution.py:236
  53.1 0.0 collective-permute-start.5
  53.1 0.5 collective-permute-start.6
  53.6 0.6 collective-permute-start.7
  54.2 2.7 %collective-permute-start.8 = (bf16[512,256]{1,0:T(8,128)(2,1)S(1)}, bf16[512,256]{1,0:T(8,128)(2,1)S(1)}, u32[]{:S(2)}, u32[]{:S(2)}) collective-permute-start(bf16[512,256]{1,0:T(8,128)(2,1)S(1)} %copy-done.1), channel_id=1, source_target_pairs={{0,6},{2,0},{4,2},{6,4},{1,7},{3,1},{5,3},{7,5},{8,14},{10,8},{12,... | collective-permute-start | bytes 786440 | tf_op jit(solution)/shard_map/ppermute | solution.py:241
  56.8 0.0 collective-permute-done.9.refs_1_.refs_4_.refs_3_
  56.9 3.2 %shard_map.101.refs_5_ = f32[64,512]{1,0:T(8,128)S(1)} custom-call(s32[4]{0:T(128)S(1)} %pad_add_fusion.off_ref, f32[1,256]{1,0:T(1,128)S(1)} %bitcast.16, bf16[512,256]{1,0:T(8,128)(2,1)} %row_net.1.refs_0_, bf16[1280,256]{1,0:T(8,128)(2,1)} %collective-permute-done.9.refs_1_.refs_4_.refs_3_, ...), custom_call_target="tpu_custom_call" | custom-call | tf_op jit(solution)/shard_map/pallas_call | solution.py:207
  60.1 3.0 %collective-permute-done.7.refs_0_ = bf16[512,256]{1,0:T(8,128)(2,1)S(1)} collective-permute-done((bf16[512,256]{1,0:T(8,128)(2,1)S(1)}, bf16[512,256]{1,0:T(8,128)(2,1)S(1)}, u32[]{:S(2)}, u32[]{:S(2)}) %collective-permute-start.7) | collective-permute-done | bytes 262176 | tf_op jit(solution)/shard_map/ppermute | solution.py:240
  63.0 0.0 collective-permute-done.8.refs_1_
  63.0 0.0 collective-permute-start.13
  63.0 0.0 collective-permute-done.5.refs_3_.refs_8_.refs_7_
  63.1 13.2 %shard_map.103 = (bf16[64,512]{1,0:T(8,128)(2,1)S(1)}, bf16[64,512]{1,0:T(8,128)(2,1)S(1)}) custom-call(s32[4]{0:T(128)S(1)} %pad_add_fusion.off_ref, f32[1,256]{1,0:T(1,128)S(1)} %bitcast.17, bf16[512,256]{1,0:T(8,128)(2,1)S(1)} %collective-permute-done.7.refs_0_, bf16[512,256]{1,0:T(8,128)(2,1)S(1)} %collective-permute-done.8.refs_1_, ...), custom_call_target="tpu_custom_call" | custom-call | tf_op jit(solution)/shard_map/pallas_call | solution.py:207
  76.2 3.3 %collective-permute-start.11 = (bf16[64,512]{1,0:T(8,128)(2,1)S(1)}, bf16[64,512]{1,0:T(8,128)(2,1)S(1)}, u32[]{:S(2)}, u32[]{:S(2)}) collective-permute-start(bf16[64,512]{1,0:T(8,128)(2,1)S(1)} %get-tuple-element.33), channel_id=1, source_target_pairs={{0,6},{2,0},{4,2},{6,4},{1,7},{3,1},{5,3},{7,5},{8,14},{10,8},{12,... | collective-permute-start | bytes 196616 | tf_op jit(solution)/shard_map/ppermute | solution.py:253
  79.5 8.2 %shard_map.104 = bf16[64,512]{1,0:T(8,128)(2,1)S(1)} custom-call(s32[4]{0:T(128)S(1)} %pad_add_fusion.off_ref, f32[1,256]{1,0:T(1,128)S(1)} %bitcast.18, bf16[512,256]{1,0:T(8,128)(2,1)S(1)} %collective-permute-done.13.refs_0_, bf16[1280,256]{1,0:T(8,128)(2,1)S(1)} %pad_maximum_fusion.refs_1_.refs_2_, ...), custom_call_target="tpu_custom_call" | custom-call | tf_op jit(solution)/shard_map/pallas_call | solution.py:207
  87.7 3.3 %collective-permute-start.14 = (bf16[64,512]{1,0:T(8,128)(2,1)S(1)}, bf16[64,512]{1,0:T(8,128)(2,1)S(1)}, u32[]{:S(2)}, u32[]{:S(2)}) collective-permute-start(bf16[64,512]{1,0:T(8,128)(2,1)S(1)} %shard_map.104), channel_id=1, source_target_pairs={{0,4},{2,6},{4,0},{6,2},{1,5},{3,7},{5,1},{7,3},{8,12},{10,14},{12... | collective-permute-start | bytes 196616 | tf_op jit(solution)/shard_map/ppermute | solution.py:256
  91.0 4.6 %shard_map.102 = f32[64,512]{1,0:T(8,128)S(1)} custom-call(s32[4]{0:T(128)S(1)} %pad_add_fusion.off_ref, f32[1,256]{1,0:T(1,128)S(1)} %bitcast.19, bf16[512,256]{1,0:T(8,128)(2,1)} %row_net.1.refs_0_, bf16[1280,256]{1,0:T(8,128)(2,1)S(1)} %collective-permute-done.3.refs_1_.refs_6_.refs_5_, ...), custom_call_target="tpu_custom_call" | custom-call | tf_op jit(solution)/shard_map/pallas_call | solution.py:207
  95.6 0.0 collective-permute-done.11
  95.7 0.0 collective-permute-done.14
  95.7 0.7 add_bitcast_fusion
  (19 shorter events, 0.1 us)
Async XLA Ops:
  9.7 25.5 %copy-start.2 = (bf16[512,256]{1,0:T(8,128)(2,1)S(1)}, bf16[512,256]{1,0:T(8,128)(2,1)}, u32[]{:S(2)}) copy-start(bf16[512,256]{1,0:T(8,128)(2,1)} %get-tuple-element.20) | copy-start | bytes 786436
  9.8 25.5 %copy-start.3 = (bf16[512,256]{1,0:T(8,128)(2,1)S(1)}, bf16[512,256]{1,0:T(8,128)(2,1)}, u32[]{:S(2)}) copy-start(bf16[512,256]{1,0:T(8,128)(2,1)} %get-tuple-element.23) | copy-start | bytes 786436
  9.8 24.7 %collective-permute-start = (bf16[512,256]{1,0:T(8,128)(2,1)}, bf16[512,256]{1,0:T(8,128)(2,1)S(1)}, u32[]{:S(2)}, u32[]{:S(2)}) collective-permute-start(bf16[512,256]{1,0:T(8,128)(2,1)} %get-tuple-element.20), channel_id=1, source_target_pairs={{0,32},{32,64},{64,96},{96,0},{1,33},{33,65},{65,97},{97,1},{2,34}... | collective-permute-start | bytes 786440 | tf_op jit(solution)/shard_map/ppermute | solution.py:228
  11.5 23.0 %collective-permute-start.1 = (bf16[512,256]{1,0:T(8,128)(2,1)}, bf16[512,256]{1,0:T(8,128)(2,1)S(1)}, u32[]{:S(2)}, u32[]{:S(2)}) collective-permute-start(bf16[512,256]{1,0:T(8,128)(2,1)} %get-tuple-element.20), channel_id=1, source_target_pairs={{0,96},{32,0},{64,32},{96,64},{1,97},{33,1},{65,33},{97,65},{2,98}... | collective-permute-start | bytes 786440 | tf_op jit(solution)/shard_map/ppermute | solution.py:229
  13.1 21.4 %collective-permute-start.2 = (bf16[512,256]{1,0:T(8,128)(2,1)}, bf16[512,256]{1,0:T(8,128)(2,1)S(1)}, u32[]{:S(2)}, u32[]{:S(2)}) collective-permute-start(bf16[512,256]{1,0:T(8,128)(2,1)} %get-tuple-element.20), channel_id=1, source_target_pairs={{0,64},{32,96},{64,0},{96,32},{1,65},{33,97},{65,1},{97,33},{2,66}... | collective-permute-start | bytes 786440 | tf_op jit(solution)/shard_map/ppermute | solution.py:230
  34.6 16.4 %collective-permute-start.4 = (bf16[1280,256]{1,0:T(8,128)(2,1)S(1)}, bf16[1280,256]{1,0:T(8,128)(2,1)S(1)}, u32[]{:S(2)}, u32[]{:S(2)}) collective-permute-start(bf16[1280,256]{1,0:T(8,128)(2,1)S(1)} %pad_maximum_fusion.1.refs_2_.refs_3_), channel_id=1, source_target_pairs={{0,24},{8,0},{16,8},{24,16},{1,25},{9,1},{17,9},{25,17},{2,26},{10... | collective-permute-start | bytes 1966088 | tf_op jit(solution)/shard_map/ppermute | solution.py:237
  35.3 17.8 %collective-permute-start.3 = (bf16[1280,256]{1,0:T(8,128)(2,1)S(1)}, bf16[1280,256]{1,0:T(8,128)(2,1)S(1)}, u32[]{:S(2)}, u32[]{:S(2)}) collective-permute-start(bf16[1280,256]{1,0:T(8,128)(2,1)S(1)} %pad_maximum_fusion.refs_1_.refs_2_), channel_id=1, source_target_pairs={{0,8},{8,16},{16,24},{24,0},{1,9},{9,17},{17,25},{25,1},{2,10},{10... | collective-permute-start | bytes 1966088 | tf_op jit(solution)/shard_map/ppermute | solution.py:236
  36.8 17.4 %collective-permute-start.10 = (bf16[1280,256]{1,0:T(8,128)(2,1)S(1)}, bf16[1280,256]{1,0:T(8,128)(2,1)S(1)}, u32[]{:S(2)}, u32[]{:S(2)}) collective-permute-start(bf16[1280,256]{1,0:T(8,128)(2,1)S(1)} %pad_maximum_fusion.1.refs_2_.refs_3_), channel_id=1, source_target_pairs={{0,1},{1,0},{2,3},{3,2},{4,5},{5,4},{6,7},{7,6},{8,9},{9,8},{10,11... | collective-permute-start | bytes 1966088 | tf_op jit(solution)/shard_map/ppermute | solution.py:239
  36.8 20.1 %collective-permute-start.9 = (bf16[1280,256]{1,0:T(8,128)(2,1)S(1)}, bf16[1280,256]{1,0:T(8,128)(2,1)}, u32[]{:S(2)}, u32[]{:S(2)}) collective-permute-start(bf16[1280,256]{1,0:T(8,128)(2,1)S(1)} %pad_maximum_fusion.refs_1_.refs_2_), channel_id=1, source_target_pairs={{0,1},{1,0},{2,3},{3,2},{4,5},{5,4},{6,7},{7,6},{8,9},{9,8},{10,11... | collective-permute-start | bytes 1966088 | tf_op jit(solution)/shard_map/ppermute | solution.py:238
  37.4 9.6 %copy-start = (f32[256]{0:T(256)S(1)}, f32[256]{0:T(256)}, u32[]{:S(2)}) copy-start(f32[256]{0:T(256)} %param.18) | copy-start | bytes 3076
  47.0 6.7 %copy-start.1 = (bf16[512,256]{1,0:T(8,128)(2,1)S(1)}, bf16[512,256]{1,0:T(8,128)(2,1)}, u32[]{:S(2)}) copy-start(bf16[512,256]{1,0:T(8,128)(2,1)} %row_net.1.refs_0_) | copy-start | bytes 786436
  53.1 9.9 %collective-permute-start.5 = (bf16[1280,256]{1,0:T(8,128)(2,1)S(1)}, bf16[1280,256]{1,0:T(8,128)(2,1)S(1)}, u32[]{:S(2)}, u32[]{:S(2)}) collective-permute-start(bf16[1280,256]{1,0:T(8,128)(2,1)S(1)} %collective-permute-done.3.refs_1_.refs_6_.refs_5_), channel_id=1, source_target_pairs={{0,1},{1,0},{2,3},{3,2},{4,5},{5,4},{6,7},{7,6},{8,9},{9,8},{10,11... | collective-permute-start | bytes 1966088 | tf_op jit(solution)/shard_map/ppermute | solution.py:246
  53.1 10.0 %collective-permute-start.6 = (bf16[1280,256]{1,0:T(8,128)(2,1)S(1)}, bf16[1280,256]{1,0:T(8,128)(2,1)S(1)}, u32[]{:S(2)}, u32[]{:S(2)}) collective-permute-start(bf16[1280,256]{1,0:T(8,128)(2,1)S(1)} %collective-permute-done.4.refs_2_.refs_7_.refs_6_), channel_id=1, source_target_pairs={{0,1},{1,0},{2,3},{3,2},{4,5},{5,4},{6,7},{7,6},{8,9},{9,8},{10,11... | collective-permute-start | bytes 1966088 | tf_op jit(solution)/shard_map/ppermute | solution.py:247
  53.6 9.4 %collective-permute-start.7 = (bf16[512,256]{1,0:T(8,128)(2,1)S(1)}, bf16[512,256]{1,0:T(8,128)(2,1)S(1)}, u32[]{:S(2)}, u32[]{:S(2)}) collective-permute-start(bf16[512,256]{1,0:T(8,128)(2,1)S(1)} %copy-done.1), channel_id=1, source_target_pairs={{0,2},{2,4},{4,6},{6,0},{1,3},{3,5},{5,7},{7,1},{8,10},{10,12},{12... | collective-permute-start | bytes 786440 | tf_op jit(solution)/shard_map/ppermute | solution.py:240
  54.2 8.8 %collective-permute-start.8 = (bf16[512,256]{1,0:T(8,128)(2,1)S(1)}, bf16[512,256]{1,0:T(8,128)(2,1)S(1)}, u32[]{:S(2)}, u32[]{:S(2)}) collective-permute-start(bf16[512,256]{1,0:T(8,128)(2,1)S(1)} %copy-done.1), channel_id=1, source_target_pairs={{0,6},{2,0},{4,2},{6,4},{1,7},{3,1},{5,3},{7,5},{8,14},{10,8},{12,... | collective-permute-start | bytes 786440 | tf_op jit(solution)/shard_map/ppermute | solution.py:241
  63.0 16.5 %collective-permute-start.13 = (bf16[512,256]{1,0:T(8,128)(2,1)S(1)}, bf16[512,256]{1,0:T(8,128)(2,1)S(1)}, u32[]{:S(2)}, u32[]{:S(2)}) collective-permute-start(bf16[512,256]{1,0:T(8,128)(2,1)S(1)} %collective-permute-done.7.refs_0_), channel_id=1, source_target_pairs={{0,2},{2,4},{4,6},{6,0},{1,3},{3,5},{5,7},{7,1},{8,10},{10,12},{12... | collective-permute-start | bytes 786440 | tf_op jit(solution)/shard_map/ppermute | solution.py:251
  76.2 19.4 %collective-permute-start.11 = (bf16[64,512]{1,0:T(8,128)(2,1)S(1)}, bf16[64,512]{1,0:T(8,128)(2,1)S(1)}, u32[]{:S(2)}, u32[]{:S(2)}) collective-permute-start(bf16[64,512]{1,0:T(8,128)(2,1)S(1)} %get-tuple-element.33), channel_id=1, source_target_pairs={{0,6},{2,0},{4,2},{6,4},{1,7},{3,1},{5,3},{7,5},{8,14},{10,8},{12,... | collective-permute-start | bytes 196616 | tf_op jit(solution)/shard_map/ppermute | solution.py:253
  79.5 16.1 %collective-permute-start.12 = (bf16[64,512]{1,0:T(8,128)(2,1)S(1)}, bf16[64,512]{1,0:T(8,128)(2,1)S(1)}, u32[]{:S(2)}, u32[]{:S(2)}) collective-permute-start(bf16[64,512]{1,0:T(8,128)(2,1)S(1)} %get-tuple-element.34), channel_id=1, source_target_pairs={{0,2},{2,4},{4,6},{6,0},{1,3},{3,5},{5,7},{7,1},{8,10},{10,12},{12... | collective-permute-start | bytes 196616 | tf_op jit(solution)/shard_map/ppermute | solution.py:254
  87.7 8.0 %collective-permute-start.14 = (bf16[64,512]{1,0:T(8,128)(2,1)S(1)}, bf16[64,512]{1,0:T(8,128)(2,1)S(1)}, u32[]{:S(2)}, u32[]{:S(2)}) collective-permute-start(bf16[64,512]{1,0:T(8,128)(2,1)S(1)} %shard_map.104), channel_id=1, source_target_pairs={{0,4},{2,6},{4,0},{6,2},{1,5},{3,7},{5,1},{7,3},{8,12},{10,14},{12... | collective-permute-start | bytes 196616 | tf_op jit(solution)/shard_map/ppermute | solution.py:256

commit v4 on v3

--- a/solution.py
+++ b/solution.py
@@ -18,7 +18,6 @@
 ROWS = 512
 FEAT = 256
 UNIT = 512
-PAIR = 2560
 
 
 def dot(a, b):
@@ -143,73 +142,78 @@
         out_specs=VM,
         out_shape=jax.ShapeDtypeStruct((ROWS, ft), bf16),
         scratch_shapes=net_scratch(ROWS, hid, ft),
+        compiler_params=pltpu.CompilerParams(vmem_limit_bytes=57 * 2**20),
         name="row_net",
     )(got, w1, b1.reshape(1, -1), w2, b2.reshape(1, -1), w3)
 
 
-def rbf_kernel(off_ref,rel_ref,*refs,nr,pairs,with_init,bm,cs,ug):
-    rows=refs[:nr]; refs=refs[nr:]
-    cols=refs[:2*pairs]; refs=refs[2*pairs:]
-    if with_init: init_ref,refs=refs[0],refs[1:]
-    outs=refs[:nr]; refs=refs[nr:]
-    sc,sqr,cv,sv,kv,acc,sem=refs
-    m=nr*ROWS
-
-    def copies(p,a,b):
-        return (pltpu.make_async_copy(a,cv.at[pl.ds(pl.multiple_of(p*PAIR,PAIR),1280)],sem.at[2*p]),
-                pltpu.make_async_copy(b,cv.at[pl.ds(pl.multiple_of(p*PAIR+1280,256),1280)],sem.at[2*p+1]))
-
+def rbf_kernel(off_ref, rel_ref, *refs, nr, pairs, with_init, bm):
+    rows, refs = refs[:nr], refs[nr:]
+    cols, refs = refs[: 2 * pairs], refs[2 * pairs :]
+    if with_init:
+        init_ref, refs = refs[0], refs[1:]
+    outs, refs = refs[:nr], refs[nr:]
+    sc, sqr, sv, kv, acc = refs
+    m = nr * ROWS
+    rel = rel_ref[...]
+    ones = jnp.ones((8, FEAT), bf16)
+    for j in range(nr):
+        at = slice(j * ROWS, (j + 1) * ROWS)
+        rf = rows[j][...].astype(f32)
+        sc[at, :] = (rf * (rel * LOG2E)).astype(bf16)
+        w = rel * rf * rf
+        hi = w.astype(bf16)
+        lo = (w - hi.astype(f32)).astype(bf16)
+        sqr[:, at] = (-0.5 * LOG2E) * (
+            lax.dot_general(ones, hi, NT, preferred_element_type=f32)
+            + lax.dot_general(ones, lo, NT, preferred_element_type=f32)
+        )
+        acc[:, at] = init_ref[...] if with_init else jnp.zeros((64, ROWS), f32)
     for p in range(pairs):
-        for c in copies(p,cols[2*p],cols[2*p+1]): c.start()
-    rel=rel_ref[...]
-    ones=jnp.ones((8,FEAT),bf16)
+        a_ref, b_ref = cols[2 * p], cols[2 * p + 1]
+        blocks = ((a_ref, 0, 512), (a_ref, 1024, 256), (b_ref, 0, 256), (b_ref, 256, 512), (b_ref, 768, 512))
+        slot = p % 2
+        to = 0
+        for ref, at, size in blocks:
+            c = ref[at : at + size, :].astype(f32)
+            total = jnp.sum(rel * c * c, axis=1, keepdims=True)
+            sv[slot, to : to + size, :] = jnp.broadcast_to((-0.5 * LOG2E) * total, (size, 128))
+            to += size
+        probe = []
+        for u in range(4):
+            at = pl.multiple_of(512 + off_ref[u] * 128, 128)
+            probe += [a_ref[pl.ds(at, 64), :], a_ref[pl.ds(at + 64, 64), :]]
+        probe = jnp.concatenate(probe, axis=1)
+        for r in range(0, m, bm):
+            to = 0
+            for ref, at, size in blocks:
+                s = lax.dot_general(ref[at : at + size, :], sc[r : r + bm, :], NT, preferred_element_type=f32)
+                q = jnp.concatenate([sv[slot, to : to + size, :]] * (bm // 128), axis=1)
+                kv[slot, to : to + size, r : r + bm] = jnp.exp2(s + (q + sqr[0:1, r : r + bm])).astype(bf16)
+                to += size
+            acc[:, r : r + bm] += dot(probe, kv[slot, :, r : r + bm])
     for j in range(nr):
-        at=slice(j*ROWS,(j+1)*ROWS)
-        rf=rows[j][...].astype(f32)
-        sc[at,:]=(rf*(rel*LOG2E)).astype(bf16)
-        w=rel*rf*rf
-        hi=w.astype(bf16); lo=(w-hi.astype(f32)).astype(bf16)
-        sqr[:,at]=(-0.5*LOG2E)*(lax.dot_general(ones,hi,NT,preferred_element_type=f32)+lax.dot_general(ones,lo,NT,preferred_element_type=f32))
-        acc[:,at]=init_ref[...] if with_init else jnp.zeros((64,ROWS),f32)
-
-    def body(p,_):
-        for c in copies(p,cols[0],cols[1]): c.wait()
-        starts=[pl.multiple_of(p*PAIR+(0 if u==0 else 512+u*512),512) for u in range(4)]
-        for u0 in range(0,4,ug):
-            us=range(u0,u0+ug)
-            for u in us:
-                c=cv[pl.ds(starts[u],UNIT),:].astype(f32)
-                sv[u*UNIT:(u+1)*UNIT,:]=jnp.broadcast_to((-0.5*LOG2E)*jnp.sum(rel*c*c,axis=1,keepdims=True),(UNIT,128))
-            prs=[]
-            for u in us:
-                st=pl.multiple_of(p*PAIR+512+off_ref[u]*128,128)
-                prs+=[cv[pl.ds(st,64),:],cv[pl.ds(st+64,64),:]]
-            pr=jnp.concatenate(prs,axis=1)
-            for r in range(0,m,bm):
-                for u in us:
-                    for b in range(0,UNIT,cs):
-                        s=lax.dot_general(cv[pl.ds(starts[u]+b,cs),:],sc[r:r+bm,:],NT,preferred_element_type=f32)
-                        q=sv[u*UNIT+b:u*UNIT+b+cs,:]
-                        q=jnp.concatenate([q]*(bm//128),axis=1)
-                        kv[u*UNIT+b:u*UNIT+b+cs,r:r+bm]=jnp.exp2(s+(q+sqr[0:1,r:r+bm])).astype(bf16)
-                acc[:,r:r+bm]+=jnp.dot(pr,kv[u0*UNIT:(u0+ug)*UNIT,r:r+bm],preferred_element_type=f32)
-        return 0
-
-    lax.fori_loop(0,pairs,body,0)
-    for j in range(nr): outs[j][...]=acc[:,j*ROWS:(j+1)*ROWS].astype(outs[j].dtype)
-
-
-def rbf(off,rel,rows,pairs,init=None,out=f32,bm=256,cs=512,ug=4):
-    nr=len(rows)
-    args=list(rows)+[x for p in pairs for x in p]+([init] if init is not None else [])
-    V = VM
-    npairs=len(pairs); m=nr*ROWS
-    return pl.pallas_call(functools.partial(rbf_kernel,nr=nr,pairs=npairs,with_init=init is not None,bm=bm,cs=cs,ug=ug),
-        in_specs=[SM,V]+[V]*nr+[V]*(2*npairs)+([V] if init is not None else []),
-        out_specs=[V]*nr,out_shape=[jax.ShapeDtypeStruct((64,ROWS),out)]*nr,
-        scratch_shapes=[pltpu.VMEM((m,FEAT),bf16),pltpu.VMEM((8,m),f32),pltpu.VMEM((npairs*PAIR,FEAT),bf16),pltpu.VMEM((2048,128),f32),
-          pltpu.VMEM((2048,m),bf16),pltpu.VMEM((64,m),f32),pltpu.SemaphoreType.DMA((2*npairs,))],
-        compiler_params=LIMIT)(off,rel,*args)
+        outs[j][...] = acc[:, j * ROWS : (j + 1) * ROWS].astype(outs[j].dtype)
+
+
+def rbf(off, rel, rows, col_pairs, init=None, out=f32, bm=256):
+    nr, pairs = len(rows), len(col_pairs)
+    args = [*rows, *(x for pair in col_pairs for x in pair), *([] if init is None else [init])]
+    m = nr * ROWS
+    return pl.pallas_call(
+        functools.partial(rbf_kernel, nr=nr, pairs=pairs, with_init=init is not None, bm=bm),
+        in_specs=[SM, VM] + [VM] * len(args),
+        out_specs=[VM] * nr,
+        out_shape=[jax.ShapeDtypeStruct((64, ROWS), out)] * nr,
+        scratch_shapes=[
+            pltpu.VMEM((m, FEAT), bf16),
+            pltpu.VMEM((8, m), f32),
+            pltpu.VMEM((2, 2048, 128), f32),
+            pltpu.VMEM((2, 2048, m), bf16),
+            pltpu.VMEM((64, m), f32),
+        ],
+        compiler_params=LIMIT,
+    )(off, rel, *args)
 
 
 def ring(shift):
@@ -239,7 +243,7 @@
     pb = lax.ppermute(cb, "core", SWAP)
     f1 = lax.ppermute(feats, "x", ring(1))
     f3 = lax.ppermute(feats, "x", ring(3))
-    held = pltpu.with_memory_space_constraint(feats, pltpu.HBM)
+    held = pltpu.with_memory_space_constraint(feats, pltpu.VMEM)
     near = [(ca, cb), (pa, pb)]
     (first,) = rbf(off, rel, [held], near[:1], bm=512)
     za, zb, first = lax.optimization_barrier((za, zb, first))

time: 96.7 us -> 92 us (0.951)
  Pallas kernels: 51.5 us -> 45.5 us
    pallas_call x5, Pallas kernels: 32.2 us -> 26.2 us  [rbf(): pl.pallas_call(functools.partial(rbf_kernel, nr=nr, pairs=pairs, with_ini...]
  transfers between devices with their start and end apart: 15 -> 15, of which waited for: 3 -> 3; matrix products, arithmetic and copies ran while one was open for 0% -> 0% of each run, Pallas kernels for 43% -> 39%
where the time goes in v4:
time: 92 us; the launch traced here: 91.7 us
  Pallas kernels  45.5 us (49%)
  blocking collectives  19.3 us (21%)
  starting transfers between devices  18.3 us (20%)
  waiting for transfers between devices  6.62 us (7%)
  local copies, waits for them, and re-layouts  0.98 us (1%)
    pallas_call x5, Pallas kernels, rbf(): pl.pallas_call(functools.partial(rbf_kernel, nr=nr, pairs=pairs, with_ini...  26.2 us
    all_to_all x1, blocking collectives, steps(): got = lax.all_to_all(sent, ALL, 0, 0, tiled=True)  19.3 us
    pallas_call x1, Pallas kernels, front(): pl.pallas_call(front_kernel, in_specs=[SM, VM, VM, VM, VM, *WEIGHT_SPECS]...  9.74 us
    pallas_call x1, Pallas kernels, row_net(): pl.pallas_call(row_kernel, in_specs=[VM, *WEIGHT_SPECS], out_specs=VM, ou...  9.58 us
    ppermute x1, waiting for transfers between devices, steps(): f1 = lax.ppermute(feats, 'x', ring(1))  3.53 us
    ppermute x1, starting transfers between devices, steps(): r1 = lax.ppermute(t1, 'x', ring(3))  3.29 us
    ppermute x1, starting transfers between devices, steps(): r2 = lax.ppermute(t2, 'x', ring(2))  3.23 us
    ppermute x1, starting transfers between devices, steps(): f3 = lax.ppermute(feats, 'x', ring(3))  2.66 us
  transfers between devices with their start and end apart: 15, of which 3 were waited for; matrix products, arithmetic and copies ran while one was open for 0% of the time, Pallas kernels for 39%

profile of v4, /device:TPU:0, one launch (start us, length us, event | category | flops | bytes accessed | tf_op | source)
XLA Modules:
  0.0 91.7 jit_solution(8926477080981382063)
XLA Ops:
  0.0 9.7 %front.1 = (bf16[512,128]{1,0:T(8,128)(2,1)}, bf16[512,256]{1,0:T(8,128)(2,1)}, bf16[512,256]{1,0:T(8,128)(2,1)}) custom-call(s32[1]{0:T(128)} %bitcast.y_ref, s32[1,512]{1,0:T(1,128)} %bitcast.29, bf16[40,512]{1,0:T(8,128)(2,1)} %bitcast.24, bf16[40,2048]{1,0:T(8,128)(2,1)} %bitcast.22, f32[64,2048]{1,0:T(8,128)} %bitcast.21, bf16[40,2048]{1,0:T(8,128)(2,1)} %w1_ref.3, ...), custom_call_target="tpu_custom_call" | custom-call | tf_op jit(solution)/shard_map/front/pallas_call | solution.py:123
  9.8 1.8 %collective-permute-start = (bf16[512,256]{1,0:T(8,128)(2,1)}, bf16[512,256]{1,0:T(8,128)(2,1)S(1)}, u32[]{:S(2)}, u32[]{:S(2)}) collective-permute-start(bf16[512,256]{1,0:T(8,128)(2,1)} %get-tuple-element.20), channel_id=1, source_target_pairs={{0,32},{32,64},{64,96},{96,0},{1,33},{33,65},{65,97},{97,1},{2,34}... | collective-permute-start | bytes 786440 | tf_op jit(solution)/shard_map/ppermute | solution.py:232
  11.5 1.5 %collective-permute-start.1 = (bf16[512,256]{1,0:T(8,128)(2,1)}, bf16[512,256]{1,0:T(8,128)(2,1)S(1)}, u32[]{:S(2)}, u32[]{:S(2)}) collective-permute-start(bf16[512,256]{1,0:T(8,128)(2,1)} %get-tuple-element.20), channel_id=1, source_target_pairs={{0,96},{32,0},{64,32},{96,64},{1,97},{33,1},{65,33},{97,65},{2,98}... | collective-permute-start | bytes 786440 | tf_op jit(solution)/shard_map/ppermute | solution.py:233
  13.1 2.1 %collective-permute-start.2 = (bf16[512,256]{1,0:T(8,128)(2,1)}, bf16[512,256]{1,0:T(8,128)(2,1)S(1)}, u32[]{:S(2)}, u32[]{:S(2)}) collective-permute-start(bf16[512,256]{1,0:T(8,128)(2,1)} %get-tuple-element.20), channel_id=1, source_target_pairs={{0,64},{32,96},{64,0},{96,32},{1,65},{33,97},{65,1},{97,33},{2,66}... | collective-permute-start | bytes 786440 | tf_op jit(solution)/shard_map/ppermute | solution.py:234
  15.2 19.3 %all_to_all.12 = bf16[128,4,128]{2,1,0:T(4,128)(2,1)} all-to-all(bf16[128,4,128]{2,1,0:T(4,128)(2,1)} %bitcast.23), channel_id=1, replica_groups=mesh['y'=4,'zh'=2,'zl'=2,'x'=4,'core'=2] {'y','zh','zl','x','core'}, dimensions={0} | all-to-all | bytes 262144 | tf_op jit(solution)/shard_map/all_to_all | solution.py:235
  34.5 0.0 collective-permute-done
  34.5 0.0 collective-permute-done.1
  34.6 0.7 collective-permute-start.4
  35.3 1.4 %collective-permute-start.3 = (bf16[1280,256]{1,0:T(8,128)(2,1)S(1)}, bf16[1280,256]{1,0:T(8,128)(2,1)S(1)}, u32[]{:S(2)}, u32[]{:S(2)}) collective-permute-start(bf16[1280,256]{1,0:T(8,128)(2,1)S(1)} %pad_maximum_fusion.refs_1_.refs_2_), channel_id=1, source_target_pairs={{0,8},{8,16},{16,24},{24,0},{1,9},{9,17},{17,25},{25,1},{2,10},{10... | collective-permute-start | bytes 1966088 | tf_op jit(solution)/shard_map/ppermute | solution.py:240
  36.8 0.0 collective-permute-start.10
  36.8 0.5 collective-permute-start.9
  37.3 0.1 pad_add_fusion.off_ref
  37.4 9.6 %row_net.1.refs_0_ = bf16[512,256]{1,0:T(8,128)(2,1)} custom-call(bf16[512,128]{1,0:T(8,128)(2,1)} %bitcast.20, bf16[40,2048]{1,0:T(8,128)(2,1)} %w1_ref.3, f32[1,2048]{1,0:T(1,128)} %bitcast.26, bf16[2048,2048]{1,0:T(8,128)(2,1)} %w2_ref.3, f32[1,2048]{1,0:T(1,128)} %bitcast.28, bf16[2048,256]{1,0:T(8,128)(2,1)} %w3_ref.3), custom_call_target="tpu_custom_call" | custom-call | tf_op jit(solution)/shard_map/row_net/pallas_call | solution.py:139
  47.0 0.9 %copy-done = bf16[512,256]{1,0:T(8,128)(2,1)S(1)} copy-done((bf16[512,256]{1,0:T(8,128)(2,1)S(1)}, bf16[512,256]{1,0:T(8,128)(2,1)}, u32[]{:S(2)}) %copy-start) | copy-done | bytes 262168
  47.9 2.1 %shard_map.100.refs_3_ = f32[64,512]{1,0:T(8,128)S(1)} custom-call(s32[4]{0:T(128)S(1)} %pad_add_fusion.off_ref, f32[1,256]{1,0:T(1,128)S(1)} %bitcast.15, bf16[512,256]{1,0:T(8,128)(2,1)S(1)} %copy-done, bf16[1280,256]{1,0:T(8,128)(2,1)S(1)} %pad_maximum_fusion.refs_1_.refs_2_, bf16[1280,256]{1,0:T(8,128)(2,1)S(1)} %pad_maximum_fusion.1.refs_2_.refs_3_), custom_call_target="tpu_custom_call" | custom-call | tf_op jit(solution)/shard_map/pallas_call | solution.py:203
  50.0 1.0 %collective-permute-done.4.refs_2_.refs_7_.refs_6_ = bf16[1280,256]{1,0:T(8,128)(2,1)S(1)} collective-permute-done((bf16[1280,256]{1,0:T(8,128)(2,1)S(1)}, bf16[1280,256]{1,0:T(8,128)(2,1)S(1)}, u32[]{:S(2)}, u32[]{:S(2)}) %collective-permute-start.4) | collective-permute-done | bytes 655392 | tf_op jit(solution)/shard_map/ppermute | solution.py:241
  51.0 2.1 %collective-permute-done.3.refs_1_.refs_6_.refs_5_ = bf16[1280,256]{1,0:T(8,128)(2,1)S(1)} collective-permute-done((bf16[1280,256]{1,0:T(8,128)(2,1)S(1)}, bf16[1280,256]{1,0:T(8,128)(2,1)S(1)}, u32[]{:S(2)}, u32[]{:S(2)}) %collective-permute-start.3) | collective-permute-done | bytes 655392 | tf_op jit(solution)/shard_map/ppermute | solution.py:240
  53.1 0.0 collective-permute-start.5
  53.1 0.5 collective-permute-start.6
  53.6 0.6 collective-permute-start.7
  54.2 0.0 collective-permute-done.10.refs_2_.refs_5_.refs_4_
  54.2 2.7 %collective-permute-start.8 = (bf16[512,256]{1,0:T(8,128)(2,1)S(1)}, bf16[512,256]{1,0:T(8,128)(2,1)S(1)}, u32[]{:S(2)}, u32[]{:S(2)}) collective-permute-start(bf16[512,256]{1,0:T(8,128)(2,1)S(1)} %copy-done), channel_id=1, source_target_pairs={{0,6},{2,0},{4,2},{6,4},{1,7},{3,1},{5,3},{7,5},{8,14},{10,8},{12,... | collective-permute-start | bytes 786440 | tf_op jit(solution)/shard_map/ppermute | solution.py:245
  56.9 2.7 %shard_map.101.refs_5_ = f32[64,512]{1,0:T(8,128)S(1)} custom-call(s32[4]{0:T(128)S(1)} %pad_add_fusion.off_ref, f32[1,256]{1,0:T(1,128)S(1)} %bitcast.16, bf16[512,256]{1,0:T(8,128)(2,1)S(1)} %copy-done, bf16[1280,256]{1,0:T(8,128)(2,1)} %collective-permute-done.9.refs_1_.refs_4_.refs_3_, ...), custom_call_target="tpu_custom_call" | custom-call | tf_op jit(solution)/shard_map/pallas_call | solution.py:203
  59.5 3.5 %collective-permute-done.7.refs_0_ = bf16[512,256]{1,0:T(8,128)(2,1)S(1)} collective-permute-done((bf16[512,256]{1,0:T(8,128)(2,1)S(1)}, bf16[512,256]{1,0:T(8,128)(2,1)S(1)}, u32[]{:S(2)}, u32[]{:S(2)}) %collective-permute-start.7) | collective-permute-done | bytes 262176 | tf_op jit(solution)/shard_map/ppermute | solution.py:244
  63.0 0.0 collective-permute-done.8.refs_1_
  63.1 11.1 %shard_map.103 = (bf16[64,512]{1,0:T(8,128)(2,1)S(1)}, bf16[64,512]{1,0:T(8,128)(2,1)S(1)}) custom-call(s32[4]{0:T(128)S(1)} %pad_add_fusion.off_ref, f32[1,256]{1,0:T(1,128)S(1)} %bitcast.17, bf16[512,256]{1,0:T(8,128)(2,1)S(1)} %collective-permute-done.7.refs_0_, bf16[512,256]{1,0:T(8,128)(2,1)S(1)} %collective-permute-done.8.refs_1_, ...), custom_call_target="tpu_custom_call" | custom-call | tf_op jit(solution)/shard_map/pallas_call | solution.py:203
  74.2 3.3 %collective-permute-start.11 = (bf16[64,512]{1,0:T(8,128)(2,1)S(1)}, bf16[64,512]{1,0:T(8,128)(2,1)S(1)}, u32[]{:S(2)}, u32[]{:S(2)}) collective-permute-start(bf16[64,512]{1,0:T(8,128)(2,1)S(1)} %get-tuple-element.33), channel_id=1, source_target_pairs={{0,6},{2,0},{4,2},{6,4},{1,7},{3,1},{5,3},{7,5},{8,14},{10,8},{12,... | collective-permute-start | bytes 196616 | tf_op jit(solution)/shard_map/ppermute | solution.py:257
  77.5 0.0 collective-permute-start.12
  77.5 6.7 %shard_map.104 = bf16[64,512]{1,0:T(8,128)(2,1)S(1)} custom-call(s32[4]{0:T(128)S(1)} %pad_add_fusion.off_ref, f32[1,256]{1,0:T(1,128)S(1)} %bitcast.18, bf16[512,256]{1,0:T(8,128)(2,1)S(1)} %collective-permute-done.13.refs_0_, bf16[1280,256]{1,0:T(8,128)(2,1)S(1)} %pad_maximum_fusion.refs_1_.refs_2_, ...), custom_call_target="tpu_custom_call" | custom-call | tf_op jit(solution)/shard_map/pallas_call | solution.py:203
  84.2 3.2 %collective-permute-start.14 = (bf16[64,512]{1,0:T(8,128)(2,1)S(1)}, bf16[64,512]{1,0:T(8,128)(2,1)S(1)}, u32[]{:S(2)}, u32[]{:S(2)}) collective-permute-start(bf16[64,512]{1,0:T(8,128)(2,1)S(1)} %shard_map.104), channel_id=1, source_target_pairs={{0,4},{2,6},{4,0},{6,2},{1,5},{3,7},{5,1},{7,3},{8,12},{10,14},{12... | collective-permute-start | bytes 196616 | tf_op jit(solution)/shard_map/ppermute | solution.py:260
  87.5 3.5 %shard_map.102 = f32[64,512]{1,0:T(8,128)S(1)} custom-call(s32[4]{0:T(128)S(1)} %pad_add_fusion.off_ref, f32[1,256]{1,0:T(1,128)S(1)} %bitcast.19, bf16[512,256]{1,0:T(8,128)(2,1)S(1)} %copy-done.1, bf16[1280,256]{1,0:T(8,128)(2,1)S(1)} %collective-permute-done.3.refs_1_.refs_6_.refs_5_, ...), custom_call_target="tpu_custom_call" | custom-call | tf_op jit(solution)/shard_map/pallas_call | solution.py:203
  91.0 0.7 add_bitcast_fusion
  (21 shorter events, 0.1 us)
Async XLA Ops:
  9.7 25.5 %copy-start.3 = (bf16[512,256]{1,0:T(8,128)(2,1)S(1)}, bf16[512,256]{1,0:T(8,128)(2,1)}, u32[]{:S(2)}) copy-start(bf16[512,256]{1,0:T(8,128)(2,1)} %get-tuple-element.20) | copy-start | bytes 786436
  9.8 25.5 %copy-start.4 = (bf16[512,256]{1,0:T(8,128)(2,1)S(1)}, bf16[512,256]{1,0:T(8,128)(2,1)}, u32[]{:S(2)}) copy-start(bf16[512,256]{1,0:T(8,128)(2,1)} %get-tuple-element.23) | copy-start | bytes 786436
  9.8 24.7 %collective-permute-start = (bf16[512,256]{1,0:T(8,128)(2,1)}, bf16[512,256]{1,0:T(8,128)(2,1)S(1)}, u32[]{:S(2)}, u32[]{:S(2)}) collective-permute-start(bf16[512,256]{1,0:T(8,128)(2,1)} %get-tuple-element.20), channel_id=1, source_target_pairs={{0,32},{32,64},{64,96},{96,0},{1,33},{33,65},{65,97},{97,1},{2,34}... | collective-permute-start | bytes 786440 | tf_op jit(solution)/shard_map/ppermute | solution.py:232
  11.5 23.0 %collective-permute-start.1 = (bf16[512,256]{1,0:T(8,128)(2,1)}, bf16[512,256]{1,0:T(8,128)(2,1)S(1)}, u32[]{:S(2)}, u32[]{:S(2)}) collective-permute-start(bf16[512,256]{1,0:T(8,128)(2,1)} %get-tuple-element.20), channel_id=1, source_target_pairs={{0,96},{32,0},{64,32},{96,64},{1,97},{33,1},{65,33},{97,65},{2,98}... | collective-permute-start | bytes 786440 | tf_op jit(solution)/shard_map/ppermute | solution.py:233
  13.1 21.4 %collective-permute-start.2 = (bf16[512,256]{1,0:T(8,128)(2,1)}, bf16[512,256]{1,0:T(8,128)(2,1)S(1)}, u32[]{:S(2)}, u32[]{:S(2)}) collective-permute-start(bf16[512,256]{1,0:T(8,128)(2,1)} %get-tuple-element.20), channel_id=1, source_target_pairs={{0,64},{32,96},{64,0},{96,32},{1,65},{33,97},{65,1},{97,33},{2,66}... | collective-permute-start | bytes 786440 | tf_op jit(solution)/shard_map/ppermute | solution.py:234
  34.6 16.4 %collective-permute-start.4 = (bf16[1280,256]{1,0:T(8,128)(2,1)S(1)}, bf16[1280,256]{1,0:T(8,128)(2,1)S(1)}, u32[]{:S(2)}, u32[]{:S(2)}) collective-permute-start(bf16[1280,256]{1,0:T(8,128)(2,1)S(1)} %pad_maximum_fusion.1.refs_2_.refs_3_), channel_id=1, source_target_pairs={{0,24},{8,0},{16,8},{24,16},{1,25},{9,1},{17,9},{25,17},{2,26},{10... | collective-permute-start | bytes 1966088 | tf_op jit(solution)/shard_map/ppermute | solution.py:241
  35.3 17.8 %collective-permute-start.3 = (bf16[1280,256]{1,0:T(8,128)(2,1)S(1)}, bf16[1280,256]{1,0:T(8,128)(2,1)S(1)}, u32[]{:S(2)}, u32[]{:S(2)}) collective-permute-start(bf16[1280,256]{1,0:T(8,128)(2,1)S(1)} %pad_maximum_fusion.refs_1_.refs_2_), channel_id=1, source_target_pairs={{0,8},{8,16},{16,24},{24,0},{1,9},{9,17},{17,25},{25,1},{2,10},{10... | collective-permute-start | bytes 1966088 | tf_op jit(solution)/shard_map/ppermute | solution.py:240
  36.8 17.4 %collective-permute-start.10 = (bf16[1280,256]{1,0:T(8,128)(2,1)S(1)}, bf16[1280,256]{1,0:T(8,128)(2,1)S(1)}, u32[]{:S(2)}, u32[]{:S(2)}) collective-permute-start(bf16[1280,256]{1,0:T(8,128)(2,1)S(1)} %pad_maximum_fusion.1.refs_2_.refs_3_), channel_id=1, source_target_pairs={{0,1},{1,0},{2,3},{3,2},{4,5},{5,4},{6,7},{7,6},{8,9},{9,8},{10,11... | collective-permute-start | bytes 1966088 | tf_op jit(solution)/shard_map/ppermute | solution.py:243
  36.8 20.1 %collective-permute-start.9 = (bf16[1280,256]{1,0:T(8,128)(2,1)S(1)}, bf16[1280,256]{1,0:T(8,128)(2,1)}, u32[]{:S(2)}, u32[]{:S(2)}) collective-permute-start(bf16[1280,256]{1,0:T(8,128)(2,1)S(1)} %pad_maximum_fusion.refs_1_.refs_2_), channel_id=1, source_target_pairs={{0,1},{1,0},{2,3},{3,2},{4,5},{5,4},{6,7},{7,6},{8,9},{9,8},{10,11... | collective-permute-start | bytes 1966088 | tf_op jit(solution)/shard_map/ppermute | solution.py:242
  37.4 9.6 %copy-start.2 = (f32[256]{0:T(256)S(1)}, f32[256]{0:T(256)}, u32[]{:S(2)}) copy-start(f32[256]{0:T(256)} %param.18) | copy-start | bytes 3076
  47.0 1.0 %copy-start = (bf16[512,256]{1,0:T(8,128)(2,1)S(1)}, bf16[512,256]{1,0:T(8,128)(2,1)}, u32[]{:S(2)}) copy-start(bf16[512,256]{1,0:T(8,128)(2,1)} %row_net.1.refs_0_) | copy-start | bytes 786436
  53.1 9.9 %collective-permute-start.5 = (bf16[1280,256]{1,0:T(8,128)(2,1)S(1)}, bf16[1280,256]{1,0:T(8,128)(2,1)S(1)}, u32[]{:S(2)}, u32[]{:S(2)}) collective-permute-start(bf16[1280,256]{1,0:T(8,128)(2,1)S(1)} %collective-permute-done.3.refs_1_.refs_6_.refs_5_), channel_id=1, source_target_pairs={{0,1},{1,0},{2,3},{3,2},{4,5},{5,4},{6,7},{7,6},{8,9},{9,8},{10,11... | collective-permute-start | bytes 1966088 | tf_op jit(solution)/shard_map/ppermute | solution.py:250
  53.1 9.9 %collective-permute-start.6 = (bf16[1280,256]{1,0:T(8,128)(2,1)S(1)}, bf16[1280,256]{1,0:T(8,128)(2,1)S(1)}, u32[]{:S(2)}, u32[]{:S(2)}) collective-permute-start(bf16[1280,256]{1,0:T(8,128)(2,1)S(1)} %collective-permute-done.4.refs_2_.refs_7_.refs_6_), channel_id=1, source_target_pairs={{0,1},{1,0},{2,3},{3,2},{4,5},{5,4},{6,7},{7,6},{8,9},{9,8},{10,11... | collective-permute-start | bytes 1966088 | tf_op jit(solution)/shard_map/ppermute | solution.py:251
  53.6 9.4 %collective-permute-start.7 = (bf16[512,256]{1,0:T(8,128)(2,1)S(1)}, bf16[512,256]{1,0:T(8,128)(2,1)S(1)}, u32[]{:S(2)}, u32[]{:S(2)}) collective-permute-start(bf16[512,256]{1,0:T(8,128)(2,1)S(1)} %copy-done), channel_id=1, source_target_pairs={{0,2},{2,4},{4,6},{6,0},{1,3},{3,5},{5,7},{7,1},{8,10},{10,12},{12... | collective-permute-start | bytes 786440 | tf_op jit(solution)/shard_map/ppermute | solution.py:244
  54.2 8.8 %collective-permute-start.8 = (bf16[512,256]{1,0:T(8,128)(2,1)S(1)}, bf16[512,256]{1,0:T(8,128)(2,1)S(1)}, u32[]{:S(2)}, u32[]{:S(2)}) collective-permute-start(bf16[512,256]{1,0:T(8,128)(2,1)S(1)} %copy-done), channel_id=1, source_target_pairs={{0,6},{2,0},{4,2},{6,4},{1,7},{3,1},{5,3},{7,5},{8,14},{10,8},{12,... | collective-permute-start | bytes 786440 | tf_op jit(solution)/shard_map/ppermute | solution.py:245
  63.0 14.5 %collective-permute-start.13 = (bf16[512,256]{1,0:T(8,128)(2,1)S(1)}, bf16[512,256]{1,0:T(8,128)(2,1)S(1)}, u32[]{:S(2)}, u32[]{:S(2)}) collective-permute-start(bf16[512,256]{1,0:T(8,128)(2,1)S(1)} %collective-permute-done.7.refs_0_), channel_id=1, source_target_pairs={{0,2},{2,4},{4,6},{6,0},{1,3},{3,5},{5,7},{7,1},{8,10},{10,12},{12... | collective-permute-start | bytes 786440 | tf_op jit(solution)/shard_map/ppermute | solution.py:255
  74.2 16.8 %collective-permute-start.11 = (bf16[64,512]{1,0:T(8,128)(2,1)S(1)}, bf16[64,512]{1,0:T(8,128)(2,1)S(1)}, u32[]{:S(2)}, u32[]{:S(2)}) collective-permute-start(bf16[64,512]{1,0:T(8,128)(2,1)S(1)} %get-tuple-element.33), channel_id=1, source_target_pairs={{0,6},{2,0},{4,2},{6,4},{1,7},{3,1},{5,3},{7,5},{8,14},{10,8},{12,... | collective-permute-start | bytes 196616 | tf_op jit(solution)/shard_map/ppermute | solution.py:257
  77.5 10.0 %copy-start.1 = (bf16[512,256]{1,0:T(8,128)(2,1)S(1)}, bf16[512,256]{1,0:T(8,128)(2,1)}, u32[]{:S(2)}) copy-start(bf16[512,256]{1,0:T(8,128)(2,1)} %row_net.1.refs_0_) | copy-start | bytes 786436
  77.5 13.5 %collective-permute-start.12 = (bf16[64,512]{1,0:T(8,128)(2,1)S(1)}, bf16[64,512]{1,0:T(8,128)(2,1)S(1)}, u32[]{:S(2)}, u32[]{:S(2)}) collective-permute-start(bf16[64,512]{1,0:T(8,128)(2,1)S(1)} %get-tuple-element.34), channel_id=1, source_target_pairs={{0,2},{2,4},{4,6},{6,0},{1,3},{3,5},{5,7},{7,1},{8,10},{10,12},{12... | collective-permute-start | bytes 196616 | tf_op jit(solution)/shard_map/ppermute | solution.py:258
  84.2 6.8 %collective-permute-start.14 = (bf16[64,512]{1,0:T(8,128)(2,1)S(1)}, bf16[64,512]{1,0:T(8,128)(2,1)S(1)}, u32[]{:S(2)}, u32[]{:S(2)}) collective-permute-start(bf16[64,512]{1,0:T(8,128)(2,1)S(1)} %shard_map.104), channel_id=1, source_target_pairs={{0,4},{2,6},{4,0},{6,2},{1,5},{3,7},{5,1},{7,3},{8,12},{10,14},{12... | collective-permute-start | bytes 196616 | tf_op jit(solution)/shard_map/ppermute | solution.py:260

commit v5 on v4

--- a/solution.py
+++ b/solution.py
@@ -243,22 +243,22 @@
     pb = lax.ppermute(cb, "core", SWAP)
     f1 = lax.ppermute(feats, "x", ring(1))
     f3 = lax.ppermute(feats, "x", ring(3))
-    held = pltpu.with_memory_space_constraint(feats, pltpu.VMEM)
     near = [(ca, cb), (pa, pb)]
-    (first,) = rbf(off, rel, [held], near[:1], bm=512)
+    held = pltpu.with_memory_space_constraint(feats, pltpu.HBM)
+    (first,) = rbf(off, rel, [held], near[:1])
     za, zb, first = lax.optimization_barrier((za, zb, first))
     pza = lax.ppermute(za, "core", SWAP)
     pzb = lax.ppermute(zb, "core", SWAP)
     far = [(za, zb), (pza, pzb)]
-    (first,) = rbf(off, rel, [held], near[1:], first, bm=512)
+    (first,) = rbf(off, rel, [feats], near[1:], first)
     f1, f3, first = lax.optimization_barrier((f1, f3, first))
     f2 = lax.ppermute(f1, "x", ring(1))
     t1, t3 = rbf(off, rel, [f1, f3], near + far, out=bf16)
     r1 = lax.ppermute(t1, "x", ring(3))
     r3 = lax.ppermute(t3, "x", ring(1))
-    (t2,) = rbf(off, rel, [f2], near + far, out=bf16, bm=512)
+    (t2,) = rbf(off, rel, [f2], near + far, out=bf16)
     r2 = lax.ppermute(t2, "x", ring(2))
-    (mine,) = rbf(off, rel, [held], far, first, bm=512)
+    (mine,) = rbf(off, rel, [feats], far, first)
     total = mine + r1.astype(f32) + r3.astype(f32) + r2.astype(f32)
     return total.T
 

time: 92 us -> 91.9 us (level)
  local copies, waits for them, and re-layouts: 0.98 us -> 0.04 us
    unnamed x10 -> x8, local copies, waits for them, and re-layouts: 0.96 us -> 0.02 us
where the time goes in v5:
time: 91.9 us; the launch traced here: 91.5 us
  Pallas kernels  45.6 us (50%)
  blocking collectives  19.3 us (21%)
  starting transfers between devices  18.4 us (20%)
  waiting for transfers between devices  7.17 us (8%)
    pallas_call x5, Pallas kernels, rbf(): pl.pallas_call(functools.partial(rbf_kernel, nr=nr, pairs=pairs, with_ini...  26.3 us
    all_to_all x1, blocking collectives, steps(): got = lax.all_to_all(sent, ALL, 0, 0, tiled=True)  19.3 us
    pallas_call x1, Pallas kernels, front(): pl.pallas_call(front_kernel, in_specs=[SM, VM, VM, VM, VM, *WEIGHT_SPECS]...  9.73 us
    pallas_call x1, Pallas kernels, row_net(): pl.pallas_call(row_kernel, in_specs=[VM, *WEIGHT_SPECS], out_specs=VM, ou...  9.57 us
    ppermute x1, waiting for transfers between devices, steps(): f1 = lax.ppermute(feats, 'x', ring(1))  3.53 us
    ppermute x1, starting transfers between devices, steps(): r1 = lax.ppermute(t1, 'x', ring(3))  3.29 us
    ppermute x1, starting transfers between devices, steps(): r2 = lax.ppermute(t2, 'x', ring(2))  3.27 us
    ppermute x1, starting transfers between devices, steps(): f3 = lax.ppermute(feats, 'x', ring(3))  2.66 us
  transfers between devices with their start and end apart: 15, of which 3 were waited for; matrix products, arithmetic and copies ran while one was open for 0% of the time, Pallas kernels for 39%

profile of v5, /device:TPU:0, one launch (start us, length us, event | category | flops | bytes accessed | tf_op | source)
XLA Modules:
  0.0 91.5 jit_solution(16615754832538326179)
XLA Ops:
  0.0 9.7 %front.1 = (bf16[512,128]{1,0:T(8,128)(2,1)}, bf16[512,256]{1,0:T(8,128)(2,1)}, bf16[512,256]{1,0:T(8,128)(2,1)}) custom-call(s32[1]{0:T(128)} %bitcast.y_ref, s32[1,512]{1,0:T(1,128)} %bitcast.29, bf16[40,512]{1,0:T(8,128)(2,1)} %bitcast.24, bf16[40,2048]{1,0:T(8,128)(2,1)} %bitcast.22, f32[64,2048]{1,0:T(8,128)} %bitcast.21, bf16[40,2048]{1,0:T(8,128)(2,1)} %w1_ref.3, ...), custom_call_target="tpu_custom_call" | custom-call | tf_op jit(solution)/shard_map/front/pallas_call | solution.py:123
  9.8 1.8 %collective-permute-start = (bf16[512,256]{1,0:T(8,128)(2,1)}, bf16[512,256]{1,0:T(8,128)(2,1)S(1)}, u32[]{:S(2)}, u32[]{:S(2)}) collective-permute-start(bf16[512,256]{1,0:T(8,128)(2,1)} %get-tuple-element.20), channel_id=1, source_target_pairs={{0,32},{32,64},{64,96},{96,0},{1,33},{33,65},{65,97},{97,1},{2,34}... | collective-permute-start | bytes 786440 | tf_op jit(solution)/shard_map/ppermute | solution.py:232
  11.5 1.5 %collective-permute-start.1 = (bf16[512,256]{1,0:T(8,128)(2,1)}, bf16[512,256]{1,0:T(8,128)(2,1)S(1)}, u32[]{:S(2)}, u32[]{:S(2)}) collective-permute-start(bf16[512,256]{1,0:T(8,128)(2,1)} %get-tuple-element.20), channel_id=1, source_target_pairs={{0,96},{32,0},{64,32},{96,64},{1,97},{33,1},{65,33},{97,65},{2,98}... | collective-permute-start | bytes 786440 | tf_op jit(solution)/shard_map/ppermute | solution.py:233
  13.1 2.1 %collective-permute-start.2 = (bf16[512,256]{1,0:T(8,128)(2,1)}, bf16[512,256]{1,0:T(8,128)(2,1)S(1)}, u32[]{:S(2)}, u32[]{:S(2)}) collective-permute-start(bf16[512,256]{1,0:T(8,128)(2,1)} %get-tuple-element.20), channel_id=1, source_target_pairs={{0,64},{32,96},{64,0},{96,32},{1,65},{33,97},{65,1},{97,33},{2,66}... | collective-permute-start | bytes 786440 | tf_op jit(solution)/shard_map/ppermute | solution.py:234
  15.2 19.3 %all_to_all.12 = bf16[128,4,128]{2,1,0:T(4,128)(2,1)} all-to-all(bf16[128,4,128]{2,1,0:T(4,128)(2,1)} %bitcast.23), channel_id=1, replica_groups=mesh['y'=4,'zh'=2,'zl'=2,'x'=4,'core'=2] {'y','zh','zl','x','core'}, dimensions={0} | all-to-all | bytes 262144 | tf_op jit(solution)/shard_map/all_to_all | solution.py:235
  34.6 0.7 collective-permute-start.4
  35.3 1.4 %collective-permute-start.3 = (bf16[1280,256]{1,0:T(8,128)(2,1)S(1)}, bf16[1280,256]{1,0:T(8,128)(2,1)S(1)}, u32[]{:S(2)}, u32[]{:S(2)}) collective-permute-start(bf16[1280,256]{1,0:T(8,128)(2,1)S(1)} %pad_maximum_fusion.refs_1_.refs_2_), channel_id=1, source_target_pairs={{0,8},{8,16},{16,24},{24,0},{1,9},{9,17},{17,25},{25,1},{2,10},{10... | collective-permute-start | bytes 1966088 | tf_op jit(solution)/shard_map/ppermute | solution.py:240
  36.8 0.5 collective-permute-start.9
  37.3 0.1 pad_add_fusion.off_ref
  37.4 9.6 %row_net.1.refs_0_ = bf16[512,256]{1,0:T(8,128)(2,1)} custom-call(bf16[512,128]{1,0:T(8,128)(2,1)} %bitcast.20, bf16[40,2048]{1,0:T(8,128)(2,1)} %w1_ref.3, f32[1,2048]{1,0:T(1,128)} %bitcast.26, bf16[2048,2048]{1,0:T(8,128)(2,1)} %w2_ref.3, f32[1,2048]{1,0:T(1,128)} %bitcast.28, bf16[2048,256]{1,0:T(8,128)(2,1)} %w3_ref.3), custom_call_target="tpu_custom_call" | custom-call | tf_op jit(solution)/shard_map/row_net/pallas_call | solution.py:139
  47.0 2.5 %shard_map.100.refs_3_ = f32[64,512]{1,0:T(8,128)S(1)} custom-call(s32[4]{0:T(128)S(1)} %pad_add_fusion.off_ref, f32[1,256]{1,0:T(1,128)S(1)} %bitcast.15, bf16[512,256]{1,0:T(8,128)(2,1)} %row_net.1.refs_0_, bf16[1280,256]{1,0:T(8,128)(2,1)S(1)} %pad_maximum_fusion.refs_1_.refs_2_, bf16[1280,256]{1,0:T(8,128)(2,1)S(1)} %pad_maximum_fusion.1.refs_2_.refs_3_), custom_call_target="tpu_custom_call" | custom-call | tf_op jit(solution)/shard_map/pallas_call | solution.py:203
  49.5 1.5 %collective-permute-done.4.refs_2_.refs_7_.refs_6_ = bf16[1280,256]{1,0:T(8,128)(2,1)S(1)} collective-permute-done((bf16[1280,256]{1,0:T(8,128)(2,1)S(1)}, bf16[1280,256]{1,0:T(8,128)(2,1)S(1)}, u32[]{:S(2)}, u32[]{:S(2)}) %collective-permute-start.4) | collective-permute-done | bytes 655392 | tf_op jit(solution)/shard_map/ppermute | solution.py:241
  51.0 2.1 %collective-permute-done.3.refs_1_.refs_6_.refs_5_ = bf16[1280,256]{1,0:T(8,128)(2,1)S(1)} collective-permute-done((bf16[1280,256]{1,0:T(8,128)(2,1)S(1)}, bf16[1280,256]{1,0:T(8,128)(2,1)S(1)}, u32[]{:S(2)}, u32[]{:S(2)}) %collective-permute-start.3) | collective-permute-done | bytes 655392 | tf_op jit(solution)/shard_map/ppermute | solution.py:240
  53.1 0.0 collective-permute-start.5
  53.1 0.5 collective-permute-start.6
  53.6 0.6 collective-permute-start.7
  54.2 2.7 %collective-permute-start.8 = (bf16[512,256]{1,0:T(8,128)(2,1)S(1)}, bf16[512,256]{1,0:T(8,128)(2,1)S(1)}, u32[]{:S(2)}, u32[]{:S(2)}) collective-permute-start(bf16[512,256]{1,0:T(8,128)(2,1)S(1)} %copy-done), channel_id=1, source_target_pairs={{0,6},{2,0},{4,2},{6,4},{1,7},{3,1},{5,3},{7,5},{8,14},{10,8},{12,... | collective-permute-start | bytes 786440 | tf_op jit(solution)/shard_map/ppermute | solution.py:245
  56.8 0.0 collective-permute-done.9.refs_1_.refs_4_.refs_3_
  56.9 2.6 %shard_map.101.refs_5_ = f32[64,512]{1,0:T(8,128)S(1)} custom-call(s32[4]{0:T(128)S(1)} %pad_add_fusion.off_ref, f32[1,256]{1,0:T(1,128)S(1)} %bitcast.16, bf16[512,256]{1,0:T(8,128)(2,1)S(1)} %copy-done, bf16[1280,256]{1,0:T(8,128)(2,1)} %collective-permute-done.9.refs_1_.refs_4_.refs_3_, ...), custom_call_target="tpu_custom_call" | custom-call | tf_op jit(solution)/shard_map/pallas_call | solution.py:203
  59.5 3.5 %collective-permute-done.7.refs_0_ = bf16[512,256]{1,0:T(8,128)(2,1)S(1)} collective-permute-done((bf16[512,256]{1,0:T(8,128)(2,1)S(1)}, bf16[512,256]{1,0:T(8,128)(2,1)S(1)}, u32[]{:S(2)}, u32[]{:S(2)}) %collective-permute-start.7) | collective-permute-done | bytes 262176 | tf_op jit(solution)/shard_map/ppermute | solution.py:244
  63.0 0.0 collective-permute-done.8.refs_1_
  63.0 0.0 collective-permute-start.13
  63.0 0.0 collective-permute-done.5.refs_3_.refs_8_.refs_7_
  63.1 11.1 %shard_map.103 = (bf16[64,512]{1,0:T(8,128)(2,1)S(1)}, bf16[64,512]{1,0:T(8,128)(2,1)S(1)}) custom-call(s32[4]{0:T(128)S(1)} %pad_add_fusion.off_ref, f32[1,256]{1,0:T(1,128)S(1)} %bitcast.17, bf16[512,256]{1,0:T(8,128)(2,1)S(1)} %collective-permute-done.7.refs_0_, bf16[512,256]{1,0:T(8,128)(2,1)S(1)} %collective-permute-done.8.refs_1_, ...), custom_call_target="tpu_custom_call" | custom-call | tf_op jit(solution)/shard_map/pallas_call | solution.py:203
  74.2 3.3 %collective-permute-start.11 = (bf16[64,512]{1,0:T(8,128)(2,1)S(1)}, bf16[64,512]{1,0:T(8,128)(2,1)S(1)}, u32[]{:S(2)}, u32[]{:S(2)}) collective-permute-start(bf16[64,512]{1,0:T(8,128)(2,1)S(1)} %get-tuple-element.33), channel_id=1, source_target_pairs={{0,6},{2,0},{4,2},{6,4},{1,7},{3,1},{5,3},{7,5},{8,14},{10,8},{12,... | collective-permute-start | bytes 196616 | tf_op jit(solution)/shard_map/ppermute | solution.py:257
  77.5 0.0 collective-permute-start.12
  77.5 0.0 collective-permute-done.13.refs_0_
  77.5 6.6 %shard_map.104 = bf16[64,512]{1,0:T(8,128)(2,1)S(1)} custom-call(s32[4]{0:T(128)S(1)} %pad_add_fusion.off_ref, f32[1,256]{1,0:T(1,128)S(1)} %bitcast.18, bf16[512,256]{1,0:T(8,128)(2,1)S(1)} %collective-permute-done.13.refs_0_, bf16[1280,256]{1,0:T(8,128)(2,1)S(1)} %pad_maximum_fusion.refs_1_.refs_2_, ...), custom_call_target="tpu_custom_call" | custom-call | tf_op jit(solution)/shard_map/pallas_call | solution.py:203
  84.0 3.3 %collective-permute-start.14 = (bf16[64,512]{1,0:T(8,128)(2,1)S(1)}, bf16[64,512]{1,0:T(8,128)(2,1)S(1)}, u32[]{:S(2)}, u32[]{:S(2)}) collective-permute-start(bf16[64,512]{1,0:T(8,128)(2,1)S(1)} %shard_map.104), channel_id=1, source_target_pairs={{0,4},{2,6},{4,0},{6,2},{1,5},{3,7},{5,1},{7,3},{8,12},{10,14},{12... | collective-permute-start | bytes 196616 | tf_op jit(solution)/shard_map/ppermute | solution.py:260
  87.3 3.5 %shard_map.102 = f32[64,512]{1,0:T(8,128)S(1)} custom-call(s32[4]{0:T(128)S(1)} %pad_add_fusion.off_ref, f32[1,256]{1,0:T(1,128)S(1)} %bitcast.19, bf16[512,256]{1,0:T(8,128)(2,1)S(1)} %copy-done, bf16[1280,256]{1,0:T(8,128)(2,1)S(1)} %collective-permute-done.3.refs_1_.refs_6_.refs_5_, bf16[1280,256]{1,0:T(8,128)(2,1)S(1)} %collective-permute-done.4.refs_2_.refs_7_.refs_6_, ...), custom_call_target="tpu_custom_call" | custom-call | tf_op jit(solution)/shard_map/pallas_call | solution.py:203
  90.8 0.0 collective-permute-done.11
  90.8 0.7 add_bitcast_fusion
  (19 shorter events, 0.1 us)
Async XLA Ops:
  9.7 25.5 %copy-start.2 = (bf16[512,256]{1,0:T(8,128)(2,1)S(1)}, bf16[512,256]{1,0:T(8,128)(2,1)}, u32[]{:S(2)}) copy-start(bf16[512,256]{1,0:T(8,128)(2,1)} %get-tuple-element.20) | copy-start | bytes 786436
  9.8 25.5 %copy-start.3 = (bf16[512,256]{1,0:T(8,128)(2,1)S(1)}, bf16[512,256]{1,0:T(8,128)(2,1)}, u32[]{:S(2)}) copy-start(bf16[512,256]{1,0:T(8,128)(2,1)} %get-tuple-element.23) | copy-start | bytes 786436
  9.8 24.7 %collective-permute-start = (bf16[512,256]{1,0:T(8,128)(2,1)}, bf16[512,256]{1,0:T(8,128)(2,1)S(1)}, u32[]{:S(2)}, u32[]{:S(2)}) collective-permute-start(bf16[512,256]{1,0:T(8,128)(2,1)} %get-tuple-element.20), channel_id=1, source_target_pairs={{0,32},{32,64},{64,96},{96,0},{1,33},{33,65},{65,97},{97,1},{2,34}... | collective-permute-start | bytes 786440 | tf_op jit(solution)/shard_map/ppermute | solution.py:232
  11.5 23.0 %collective-permute-start.1 = (bf16[512,256]{1,0:T(8,128)(2,1)}, bf16[512,256]{1,0:T(8,128)(2,1)S(1)}, u32[]{:S(2)}, u32[]{:S(2)}) collective-permute-start(bf16[512,256]{1,0:T(8,128)(2,1)} %get-tuple-element.20), channel_id=1, source_target_pairs={{0,96},{32,0},{64,32},{96,64},{1,97},{33,1},{65,33},{97,65},{2,98}... | collective-permute-start | bytes 786440 | tf_op jit(solution)/shard_map/ppermute | solution.py:233
  13.1 21.4 %collective-permute-start.2 = (bf16[512,256]{1,0:T(8,128)(2,1)}, bf16[512,256]{1,0:T(8,128)(2,1)S(1)}, u32[]{:S(2)}, u32[]{:S(2)}) collective-permute-start(bf16[512,256]{1,0:T(8,128)(2,1)} %get-tuple-element.20), channel_id=1, source_target_pairs={{0,64},{32,96},{64,0},{96,32},{1,65},{33,97},{65,1},{97,33},{2,66}... | collective-permute-start | bytes 786440 | tf_op jit(solution)/shard_map/ppermute | solution.py:234
  34.6 16.4 %collective-permute-start.4 = (bf16[1280,256]{1,0:T(8,128)(2,1)S(1)}, bf16[1280,256]{1,0:T(8,128)(2,1)S(1)}, u32[]{:S(2)}, u32[]{:S(2)}) collective-permute-start(bf16[1280,256]{1,0:T(8,128)(2,1)S(1)} %pad_maximum_fusion.1.refs_2_.refs_3_), channel_id=1, source_target_pairs={{0,24},{8,0},{16,8},{24,16},{1,25},{9,1},{17,9},{25,17},{2,26},{10... | collective-permute-start | bytes 1966088 | tf_op jit(solution)/shard_map/ppermute | solution.py:241
  35.3 17.8 %collective-permute-start.3 = (bf16[1280,256]{1,0:T(8,128)(2,1)S(1)}, bf16[1280,256]{1,0:T(8,128)(2,1)S(1)}, u32[]{:S(2)}, u32[]{:S(2)}) collective-permute-start(bf16[1280,256]{1,0:T(8,128)(2,1)S(1)} %pad_maximum_fusion.refs_1_.refs_2_), channel_id=1, source_target_pairs={{0,8},{8,16},{16,24},{24,0},{1,9},{9,17},{17,25},{25,1},{2,10},{10... | collective-permute-start | bytes 1966088 | tf_op jit(solution)/shard_map/ppermute | solution.py:240
  36.8 17.4 %collective-permute-start.10 = (bf16[1280,256]{1,0:T(8,128)(2,1)S(1)}, bf16[1280,256]{1,0:T(8,128)(2,1)S(1)}, u32[]{:S(2)}, u32[]{:S(2)}) collective-permute-start(bf16[1280,256]{1,0:T(8,128)(2,1)S(1)} %pad_maximum_fusion.1.refs_2_.refs_3_), channel_id=1, source_target_pairs={{0,1},{1,0},{2,3},{3,2},{4,5},{5,4},{6,7},{7,6},{8,9},{9,8},{10,11... | collective-permute-start | bytes 1966088 | tf_op jit(solution)/shard_map/ppermute | solution.py:243
  36.8 20.1 %collective-permute-start.9 = (bf16[1280,256]{1,0:T(8,128)(2,1)S(1)}, bf16[1280,256]{1,0:T(8,128)(2,1)}, u32[]{:S(2)}, u32[]{:S(2)}) collective-permute-start(bf16[1280,256]{1,0:T(8,128)(2,1)S(1)} %pad_maximum_fusion.refs_1_.refs_2_), channel_id=1, source_target_pairs={{0,1},{1,0},{2,3},{3,2},{4,5},{5,4},{6,7},{7,6},{8,9},{9,8},{10,11... | collective-permute-start | bytes 1966088 | tf_op jit(solution)/shard_map/ppermute | solution.py:242
  37.4 9.6 %copy-start.1 = (f32[256]{0:T(256)S(1)}, f32[256]{0:T(256)}, u32[]{:S(2)}) copy-start(f32[256]{0:T(256)} %param.18) | copy-start | bytes 3076
  47.0 6.7 %copy-start = (bf16[512,256]{1,0:T(8,128)(2,1)S(1)}, bf16[512,256]{1,0:T(8,128)(2,1)}, u32[]{:S(2)}) copy-start(bf16[512,256]{1,0:T(8,128)(2,1)} %row_net.1.refs_0_) | copy-start | bytes 786436
  53.1 9.9 %collective-permute-start.5 = (bf16[1280,256]{1,0:T(8,128)(2,1)S(1)}, bf16[1280,256]{1,0:T(8,128)(2,1)S(1)}, u32[]{:S(2)}, u32[]{:S(2)}) collective-permute-start(bf16[1280,256]{1,0:T(8,128)(2,1)S(1)} %collective-permute-done.3.refs_1_.refs_6_.refs_5_), channel_id=1, source_target_pairs={{0,1},{1,0},{2,3},{3,2},{4,5},{5,4},{6,7},{7,6},{8,9},{9,8},{10,11... | collective-permute-start | bytes 1966088 | tf_op jit(solution)/shard_map/ppermute | solution.py:250
  53.1 10.0 %collective-permute-start.6 = (bf16[1280,256]{1,0:T(8,128)(2,1)S(1)}, bf16[1280,256]{1,0:T(8,128)(2,1)S(1)}, u32[]{:S(2)}, u32[]{:S(2)}) collective-permute-start(bf16[1280,256]{1,0:T(8,128)(2,1)S(1)} %collective-permute-done.4.refs_2_.refs_7_.refs_6_), channel_id=1, source_target_pairs={{0,1},{1,0},{2,3},{3,2},{4,5},{5,4},{6,7},{7,6},{8,9},{9,8},{10,11... | collective-permute-start | bytes 1966088 | tf_op jit(solution)/shard_map/ppermute | solution.py:251
  53.6 9.4 %collective-permute-start.7 = (bf16[512,256]{1,0:T(8,128)(2,1)S(1)}, bf16[512,256]{1,0:T(8,128)(2,1)S(1)}, u32[]{:S(2)}, u32[]{:S(2)}) collective-permute-start(bf16[512,256]{1,0:T(8,128)(2,1)S(1)} %copy-done), channel_id=1, source_target_pairs={{0,2},{2,4},{4,6},{6,0},{1,3},{3,5},{5,7},{7,1},{8,10},{10,12},{12... | collective-permute-start | bytes 786440 | tf_op jit(solution)/shard_map/ppermute | solution.py:244
  54.2 8.8 %collective-permute-start.8 = (bf16[512,256]{1,0:T(8,128)(2,1)S(1)}, bf16[512,256]{1,0:T(8,128)(2,1)S(1)}, u32[]{:S(2)}, u32[]{:S(2)}) collective-permute-start(bf16[512,256]{1,0:T(8,128)(2,1)S(1)} %copy-done), channel_id=1, source_target_pairs={{0,6},{2,0},{4,2},{6,4},{1,7},{3,1},{5,3},{7,5},{8,14},{10,8},{12,... | collective-permute-start | bytes 786440 | tf_op jit(solution)/shard_map/ppermute | solution.py:245
  63.0 14.4 %collective-permute-start.13 = (bf16[512,256]{1,0:T(8,128)(2,1)S(1)}, bf16[512,256]{1,0:T(8,128)(2,1)S(1)}, u32[]{:S(2)}, u32[]{:S(2)}) collective-permute-start(bf16[512,256]{1,0:T(8,128)(2,1)S(1)} %collective-permute-done.7.refs_0_), channel_id=1, source_target_pairs={{0,2},{2,4},{4,6},{6,0},{1,3},{3,5},{5,7},{7,1},{8,10},{10,12},{12... | collective-permute-start | bytes 786440 | tf_op jit(solution)/shard_map/ppermute | solution.py:255
  74.2 16.6 %collective-permute-start.11 = (bf16[64,512]{1,0:T(8,128)(2,1)S(1)}, bf16[64,512]{1,0:T(8,128)(2,1)S(1)}, u32[]{:S(2)}, u32[]{:S(2)}) collective-permute-start(bf16[64,512]{1,0:T(8,128)(2,1)S(1)} %get-tuple-element.33), channel_id=1, source_target_pairs={{0,6},{2,0},{4,2},{6,4},{1,7},{3,1},{5,3},{7,5},{8,14},{10,8},{12,... | collective-permute-start | bytes 196616 | tf_op jit(solution)/shard_map/ppermute | solution.py:257
  77.5 13.3 %collective-permute-start.12 = (bf16[64,512]{1,0:T(8,128)(2,1)S(1)}, bf16[64,512]{1,0:T(8,128)(2,1)S(1)}, u32[]{:S(2)}, u32[]{:S(2)}) collective-permute-start(bf16[64,512]{1,0:T(8,128)(2,1)S(1)} %get-tuple-element.34), channel_id=1, source_target_pairs={{0,2},{2,4},{4,6},{6,0},{1,3},{3,5},{5,7},{7,1},{8,10},{10,12},{12... | collective-permute-start | bytes 196616 | tf_op jit(solution)/shard_map/ppermute | solution.py:258
  84.0 6.8 %collective-permute-start.14 = (bf16[64,512]{1,0:T(8,128)(2,1)S(1)}, bf16[64,512]{1,0:T(8,128)(2,1)S(1)}, u32[]{:S(2)}, u32[]{:S(2)}) collective-permute-start(bf16[64,512]{1,0:T(8,128)(2,1)S(1)} %shard_map.104), channel_id=1, source_target_pairs={{0,4},{2,6},{4,0},{6,2},{1,5},{3,7},{5,1},{7,3},{8,12},{10,14},{12... | collective-permute-start | bytes 196616 | tf_op jit(solution)/shard_map/ppermute | solution.py:260

commit v6 on v5

--- a/solution.py
+++ b/solution.py
@@ -239,10 +239,11 @@
     cb = jnp.concatenate([u1[256:], u3, u2], 0)
     za = lax.ppermute(ca, Z, ring(1))
     zb = lax.ppermute(cb, Z, ring(3))
-    pa = lax.ppermute(ca, "core", SWAP)
-    pb = lax.ppermute(cb, "core", SWAP)
+    ca2, cb2, feats = lax.optimization_barrier((ca, cb, feats))
     f1 = lax.ppermute(feats, "x", ring(1))
     f3 = lax.ppermute(feats, "x", ring(3))
+    pa = lax.ppermute(ca2, "core", SWAP)
+    pb = lax.ppermute(cb2, "core", SWAP)
     near = [(ca, cb), (pa, pb)]
     held = pltpu.with_memory_space_constraint(feats, pltpu.HBM)
     (first,) = rbf(off, rel, [held], near[:1])

time: 91.9 us -> 91.9 us (level)
  no operation moved by 1% of the time
where the time goes in v6:
time: 91.9 us; the launch traced here: 91.6 us
  Pallas kernels  45.6 us (50%)
  blocking collectives  19.3 us (21%)
  starting transfers between devices  18.5 us (20%)
  waiting for transfers between devices  7.21 us (8%)
    pallas_call x5, Pallas kernels, rbf(): pl.pallas_call(functools.partial(rbf_kernel, nr=nr, pairs=pairs, with_ini...  26.3 us
    all_to_all x1, blocking collectives, steps(): got = lax.all_to_all(sent, ALL, 0, 0, tiled=True)  19.3 us
    pallas_call x1, Pallas kernels, front(): pl.pallas_call(front_kernel, in_specs=[SM, VM, VM, VM, VM, *WEIGHT_SPECS]...  9.73 us
    pallas_call x1, Pallas kernels, row_net(): pl.pallas_call(row_kernel, in_specs=[VM, *WEIGHT_SPECS], out_specs=VM, ou...  9.56 us
    ppermute x1, waiting for transfers between devices, steps(): f1 = lax.ppermute(feats, 'x', ring(1))  3.53 us
    ppermute x1, starting transfers between devices, steps(): r1 = lax.ppermute(t1, 'x', ring(3))  3.29 us
    ppermute x1, starting transfers between devices, steps(): r2 = lax.ppermute(t2, 'x', ring(2))  3.28 us
    ppermute x1, starting transfers between devices, steps(): f3 = lax.ppermute(feats, 'x', ring(3))  2.66 us
  transfers between devices with their start and end apart: 15, of which 3 were waited for; matrix products, arithmetic and copies ran while one was open for 0% of the time, Pallas kernels for 39%

profile of v6, /device:TPU:0, one launch (start us, length us, event | category | flops | bytes accessed | tf_op | source)
XLA Modules:
  0.0 91.6 jit_solution(2058027448381027113)
XLA Ops:
  0.0 9.7 %front.1 = (bf16[512,128]{1,0:T(8,128)(2,1)}, bf16[512,256]{1,0:T(8,128)(2,1)}, bf16[512,256]{1,0:T(8,128)(2,1)}) custom-call(s32[1]{0:T(128)} %bitcast.y_ref, s32[1,512]{1,0:T(1,128)} %bitcast.29, bf16[40,512]{1,0:T(8,128)(2,1)} %bitcast.24, bf16[40,2048]{1,0:T(8,128)(2,1)} %bitcast.22, f32[64,2048]{1,0:T(8,128)} %bitcast.21, bf16[40,2048]{1,0:T(8,128)(2,1)} %w1_ref.3, ...), custom_call_target="tpu_custom_call" | custom-call | tf_op jit(solution)/shard_map/front/pallas_call | solution.py:123
  9.8 1.8 %collective-permute-start = (bf16[512,256]{1,0:T(8,128)(2,1)}, bf16[512,256]{1,0:T(8,128)(2,1)S(1)}, u32[]{:S(2)}, u32[]{:S(2)}) collective-permute-start(bf16[512,256]{1,0:T(8,128)(2,1)} %get-tuple-element.23), channel_id=1, source_target_pairs={{0,32},{32,64},{64,96},{96,0},{1,33},{33,65},{65,97},{97,1},{2,34}... | collective-permute-start | bytes 786440 | tf_op jit(solution)/shard_map/ppermute | solution.py:232
  11.5 1.5 %collective-permute-start.1 = (bf16[512,256]{1,0:T(8,128)(2,1)}, bf16[512,256]{1,0:T(8,128)(2,1)S(1)}, u32[]{:S(2)}, u32[]{:S(2)}) collective-permute-start(bf16[512,256]{1,0:T(8,128)(2,1)} %get-tuple-element.23), channel_id=1, source_target_pairs={{0,96},{32,0},{64,32},{96,64},{1,97},{33,1},{65,33},{97,65},{2,98}... | collective-permute-start | bytes 786440 | tf_op jit(solution)/shard_map/ppermute | solution.py:233
  13.1 2.1 %collective-permute-start.2 = (bf16[512,256]{1,0:T(8,128)(2,1)}, bf16[512,256]{1,0:T(8,128)(2,1)S(1)}, u32[]{:S(2)}, u32[]{:S(2)}) collective-permute-start(bf16[512,256]{1,0:T(8,128)(2,1)} %get-tuple-element.23), channel_id=1, source_target_pairs={{0,64},{32,96},{64,0},{96,32},{1,65},{33,97},{65,1},{97,33},{2,66}... | collective-permute-start | bytes 786440 | tf_op jit(solution)/shard_map/ppermute | solution.py:234
  15.2 19.3 %all_to_all.12 = bf16[128,4,128]{2,1,0:T(4,128)(2,1)} all-to-all(bf16[128,4,128]{2,1,0:T(4,128)(2,1)} %bitcast.23), channel_id=1, replica_groups=mesh['y'=4,'zh'=2,'zl'=2,'x'=4,'core'=2] {'y','zh','zl','x','core'}, dimensions={0} | all-to-all | bytes 262144 | tf_op jit(solution)/shard_map/all_to_all | solution.py:235
  34.5 0.8 collective-permute-start.4
  35.3 0.0 copy-start.1
  35.4 1.4 %collective-permute-start.3 = (bf16[1280,256]{1,0:T(8,128)(2,1)S(1)}, bf16[1280,256]{1,0:T(8,128)(2,1)S(1)}, u32[]{:S(2)}, u32[]{:S(2)}) collective-permute-start(bf16[1280,256]{1,0:T(8,128)(2,1)S(1)} %pad_maximum_fusion.refs_1_.refs_2_), channel_id=1, source_target_pairs={{0,8},{8,16},{16,24},{24,0},{1,9},{9,17},{17,25},{25,1},{2,10},{10... | collective-permute-start | bytes 1966088 | tf_op jit(solution)/shard_map/ppermute | solution.py:240
  36.8 9.6 %row_net.1.refs_0_ = bf16[512,256]{1,0:T(8,128)(2,1)} custom-call(bf16[512,128]{1,0:T(8,128)(2,1)} %bitcast.20, bf16[40,2048]{1,0:T(8,128)(2,1)} %w1_ref.3, f32[1,2048]{1,0:T(1,128)} %bitcast.26, bf16[2048,2048]{1,0:T(8,128)(2,1)} %w2_ref.3, f32[1,2048]{1,0:T(1,128)} %bitcast.28, bf16[2048,256]{1,0:T(8,128)(2,1)} %w3_ref.3), custom_call_target="tpu_custom_call" | custom-call | tf_op jit(solution)/shard_map/row_net/pallas_call | solution.py:139
  46.3 0.1 collective-permute-start.10
  46.4 0.5 collective-permute-start.9
  46.9 0.1 pad_add_fusion.off_ref
  47.0 2.5 %shard_map.100.refs_3_ = f32[64,512]{1,0:T(8,128)S(1)} custom-call(s32[4]{0:T(128)S(1)} %pad_add_fusion.off_ref, f32[1,256]{1,0:T(1,128)S(1)} %bitcast.15, bf16[512,256]{1,0:T(8,128)(2,1)} %row_net.1.refs_0_, bf16[1280,256]{1,0:T(8,128)(2,1)S(1)} %pad_maximum_fusion.refs_1_.refs_2_, bf16[1280,256]{1,0:T(8,128)(2,1)S(1)} %pad_maximum_fusion.1.refs_2_.refs_3_), custom_call_target="tpu_custom_call" | custom-call | tf_op jit(solution)/shard_map/pallas_call | solution.py:203
  49.5 1.5 %collective-permute-done.4.refs_2_.refs_7_.refs_6_ = bf16[1280,256]{1,0:T(8,128)(2,1)S(1)} collective-permute-done((bf16[1280,256]{1,0:T(8,128)(2,1)S(1)}, bf16[1280,256]{1,0:T(8,128)(2,1)S(1)}, u32[]{:S(2)}, u32[]{:S(2)}) %collective-permute-start.4) | collective-permute-done | bytes 655392 | tf_op jit(solution)/shard_map/ppermute | solution.py:241
  51.0 2.1 %collective-permute-done.3.refs_1_.refs_6_.refs_5_ = bf16[1280,256]{1,0:T(8,128)(2,1)S(1)} collective-permute-done((bf16[1280,256]{1,0:T(8,128)(2,1)S(1)}, bf16[1280,256]{1,0:T(8,128)(2,1)S(1)}, u32[]{:S(2)}, u32[]{:S(2)}) %collective-permute-start.3) | collective-permute-done | bytes 655392 | tf_op jit(solution)/shard_map/ppermute | solution.py:240
  53.1 0.0 collective-permute-start.5
  53.1 0.5 collective-permute-start.6
  53.6 0.6 collective-permute-start.7
  54.2 0.0 collective-permute-done.10.refs_2_.refs_5_.refs_4_
  54.2 2.7 %collective-permute-start.8 = (bf16[512,256]{1,0:T(8,128)(2,1)S(1)}, bf16[512,256]{1,0:T(8,128)(2,1)S(1)}, u32[]{:S(2)}, u32[]{:S(2)}) collective-permute-start(bf16[512,256]{1,0:T(8,128)(2,1)S(1)} %copy-done), channel_id=1, source_target_pairs={{0,6},{2,0},{4,2},{6,4},{1,7},{3,1},{5,3},{7,5},{8,14},{10,8},{12,... | collective-permute-start | bytes 786440 | tf_op jit(solution)/shard_map/ppermute | solution.py:244
  56.9 0.0 collective-permute-done.9.refs_1_.refs_4_.refs_3_
  56.9 2.6 %shard_map.101.refs_5_ = f32[64,512]{1,0:T(8,128)S(1)} custom-call(s32[4]{0:T(128)S(1)} %pad_add_fusion.off_ref, f32[1,256]{1,0:T(1,128)S(1)} %bitcast.16, bf16[512,256]{1,0:T(8,128)(2,1)S(1)} %copy-done, bf16[1280,256]{1,0:T(8,128)(2,1)} %collective-permute-done.9.refs_1_.refs_4_.refs_3_, ...), custom_call_target="tpu_custom_call" | custom-call | tf_op jit(solution)/shard_map/pallas_call | solution.py:203
  59.5 3.5 %collective-permute-done.7.refs_0_ = bf16[512,256]{1,0:T(8,128)(2,1)S(1)} collective-permute-done((bf16[512,256]{1,0:T(8,128)(2,1)S(1)}, bf16[512,256]{1,0:T(8,128)(2,1)S(1)}, u32[]{:S(2)}, u32[]{:S(2)}) %collective-permute-start.7) | collective-permute-done | bytes 262176 | tf_op jit(solution)/shard_map/ppermute | solution.py:243
  63.0 0.0 collective-permute-start.13
  63.1 11.1 %shard_map.103 = (bf16[64,512]{1,0:T(8,128)(2,1)S(1)}, bf16[64,512]{1,0:T(8,128)(2,1)S(1)}) custom-call(s32[4]{0:T(128)S(1)} %pad_add_fusion.off_ref, f32[1,256]{1,0:T(1,128)S(1)} %bitcast.17, bf16[512,256]{1,0:T(8,128)(2,1)S(1)} %collective-permute-done.7.refs_0_, bf16[512,256]{1,0:T(8,128)(2,1)S(1)} %collective-permute-done.8.refs_1_, ...), custom_call_target="tpu_custom_call" | custom-call | tf_op jit(solution)/shard_map/pallas_call | solution.py:203
  74.2 3.3 %collective-permute-start.11 = (bf16[64,512]{1,0:T(8,128)(2,1)S(1)}, bf16[64,512]{1,0:T(8,128)(2,1)S(1)}, u32[]{:S(2)}, u32[]{:S(2)}) collective-permute-start(bf16[64,512]{1,0:T(8,128)(2,1)S(1)} %get-tuple-element.39), channel_id=1, source_target_pairs={{0,6},{2,0},{4,2},{6,4},{1,7},{3,1},{5,3},{7,5},{8,14},{10,8},{12,... | collective-permute-start | bytes 196616 | tf_op jit(solution)/shard_map/ppermute | solution.py:258
  77.5 0.0 collective-permute-start.12
  77.5 6.6 %shard_map.104 = bf16[64,512]{1,0:T(8,128)(2,1)S(1)} custom-call(s32[4]{0:T(128)S(1)} %pad_add_fusion.off_ref, f32[1,256]{1,0:T(1,128)S(1)} %bitcast.18, bf16[512,256]{1,0:T(8,128)(2,1)S(1)} %collective-permute-done.13.refs_0_, bf16[1280,256]{1,0:T(8,128)(2,1)S(1)} %pad_maximum_fusion.refs_1_.refs_2_, ...), custom_call_target="tpu_custom_call" | custom-call | tf_op jit(solution)/shard_map/pallas_call | solution.py:203
  84.1 3.3 %collective-permute-start.14 = (bf16[64,512]{1,0:T(8,128)(2,1)S(1)}, bf16[64,512]{1,0:T(8,128)(2,1)S(1)}, u32[]{:S(2)}, u32[]{:S(2)}) collective-permute-start(bf16[64,512]{1,0:T(8,128)(2,1)S(1)} %shard_map.104), channel_id=1, source_target_pairs={{0,4},{2,6},{4,0},{6,2},{1,5},{3,7},{5,1},{7,3},{8,12},{10,14},{12... | collective-permute-start | bytes 196616 | tf_op jit(solution)/shard_map/ppermute | solution.py:261
  87.3 3.5 %shard_map.102 = f32[64,512]{1,0:T(8,128)S(1)} custom-call(s32[4]{0:T(128)S(1)} %pad_add_fusion.off_ref, f32[1,256]{1,0:T(1,128)S(1)} %bitcast.19, bf16[512,256]{1,0:T(8,128)(2,1)S(1)} %copy-done, bf16[1280,256]{1,0:T(8,128)(2,1)S(1)} %collective-permute-done.3.refs_1_.refs_6_.refs_5_, bf16[1280,256]{1,0:T(8,128)(2,1)S(1)} %collective-permute-done.4.refs_2_.refs_7_.refs_6_, ...), custom_call_target="tpu_custom_call" | custom-call | tf_op jit(solution)/shard_map/pallas_call | solution.py:203
  90.8 0.0 collective-permute-done.11
  90.9 0.7 add_bitcast_fusion
  (19 shorter events, 0.1 us)
Async XLA Ops:
  9.7 25.5 %copy-start.2 = (bf16[512,256]{1,0:T(8,128)(2,1)S(1)}, bf16[512,256]{1,0:T(8,128)(2,1)}, u32[]{:S(2)}) copy-start(bf16[512,256]{1,0:T(8,128)(2,1)} %get-tuple-element.23) | copy-start | bytes 786436
  9.8 25.5 %copy-start.3 = (bf16[512,256]{1,0:T(8,128)(2,1)S(1)}, bf16[512,256]{1,0:T(8,128)(2,1)}, u32[]{:S(2)}) copy-start(bf16[512,256]{1,0:T(8,128)(2,1)} %get-tuple-element.24) | copy-start | bytes 786436
  9.8 24.7 %collective-permute-start = (bf16[512,256]{1,0:T(8,128)(2,1)}, bf16[512,256]{1,0:T(8,128)(2,1)S(1)}, u32[]{:S(2)}, u32[]{:S(2)}) collective-permute-start(bf16[512,256]{1,0:T(8,128)(2,1)} %get-tuple-element.23), channel_id=1, source_target_pairs={{0,32},{32,64},{64,96},{96,0},{1,33},{33,65},{65,97},{97,1},{2,34}... | collective-permute-start | bytes 786440 | tf_op jit(solution)/shard_map/ppermute | solution.py:232
  11.5 22.9 %collective-permute-start.1 = (bf16[512,256]{1,0:T(8,128)(2,1)}, bf16[512,256]{1,0:T(8,128)(2,1)S(1)}, u32[]{:S(2)}, u32[]{:S(2)}) collective-permute-start(bf16[512,256]{1,0:T(8,128)(2,1)} %get-tuple-element.23), channel_id=1, source_target_pairs={{0,96},{32,0},{64,32},{96,64},{1,97},{33,1},{65,33},{97,65},{2,98}... | collective-permute-start | bytes 786440 | tf_op jit(solution)/shard_map/ppermute | solution.py:233
  13.1 21.4 %collective-permute-start.2 = (bf16[512,256]{1,0:T(8,128)(2,1)}, bf16[512,256]{1,0:T(8,128)(2,1)S(1)}, u32[]{:S(2)}, u32[]{:S(2)}) collective-permute-start(bf16[512,256]{1,0:T(8,128)(2,1)} %get-tuple-element.23), channel_id=1, source_target_pairs={{0,64},{32,96},{64,0},{96,32},{1,65},{33,97},{65,1},{97,33},{2,66}... | collective-permute-start | bytes 786440 | tf_op jit(solution)/shard_map/ppermute | solution.py:234
  34.5 16.5 %collective-permute-start.4 = (bf16[1280,256]{1,0:T(8,128)(2,1)S(1)}, bf16[1280,256]{1,0:T(8,128)(2,1)S(1)}, u32[]{:S(2)}, u32[]{:S(2)}) collective-permute-start(bf16[1280,256]{1,0:T(8,128)(2,1)S(1)} %pad_maximum_fusion.1.refs_2_.refs_3_), channel_id=1, source_target_pairs={{0,24},{8,0},{16,8},{24,16},{1,25},{9,1},{17,9},{25,17},{2,26},{10... | collective-permute-start | bytes 1966088 | tf_op jit(solution)/shard_map/ppermute | solution.py:241
  35.3 11.7 %copy-start.1 = (f32[256]{0:T(256)S(1)}, f32[256]{0:T(256)}, u32[]{:S(2)}) copy-start(f32[256]{0:T(256)} %param.18) | copy-start | bytes 3076
  35.4 17.8 %collective-permute-start.3 = (bf16[1280,256]{1,0:T(8,128)(2,1)S(1)}, bf16[1280,256]{1,0:T(8,128)(2,1)S(1)}, u32[]{:S(2)}, u32[]{:S(2)}) collective-permute-start(bf16[1280,256]{1,0:T(8,128)(2,1)S(1)} %pad_maximum_fusion.refs_1_.refs_2_), channel_id=1, source_target_pairs={{0,8},{8,16},{16,24},{24,0},{1,9},{9,17},{17,25},{25,1},{2,10},{10... | collective-permute-start | bytes 1966088 | tf_op jit(solution)/shard_map/ppermute | solution.py:240
  46.3 7.3 %copy-start = (bf16[512,256]{1,0:T(8,128)(2,1)S(1)}, bf16[512,256]{1,0:T(8,128)(2,1)}, u32[]{:S(2)}) copy-start(bf16[512,256]{1,0:T(8,128)(2,1)} %row_net.1.refs_0_) | copy-start | bytes 786436
  46.3 7.9 %collective-permute-start.10 = (bf16[1280,256]{1,0:T(8,128)(2,1)S(1)}, bf16[1280,256]{1,0:T(8,128)(2,1)S(1)}, u32[]{:S(2)}, u32[]{:S(2)}) collective-permute-start(bf16[1280,256]{1,0:T(8,128)(2,1)S(1)} %pad_maximum_fusion.1.refs_2_.refs_3_), channel_id=1, source_target_pairs={{0,1},{1,0},{2,3},{3,2},{4,5},{5,4},{6,7},{7,6},{8,9},{9,8},{10,11... | collective-permute-start | bytes 1966088 | tf_op jit(solution)/shard_map/ppermute | solution.py:246
  46.4 10.4 %collective-permute-start.9 = (bf16[1280,256]{1,0:T(8,128)(2,1)S(1)}, bf16[1280,256]{1,0:T(8,128)(2,1)}, u32[]{:S(2)}, u32[]{:S(2)}) collective-permute-start(bf16[1280,256]{1,0:T(8,128)(2,1)S(1)} %pad_maximum_fusion.refs_1_.refs_2_), channel_id=1, source_target_pairs={{0,1},{1,0},{2,3},{3,2},{4,5},{5,4},{6,7},{7,6},{8,9},{9,8},{10,11... | collective-permute-start | bytes 1966088 | tf_op jit(solution)/shard_map/ppermute | solution.py:245
  53.1 9.9 %collective-permute-start.5 = (bf16[1280,256]{1,0:T(8,128)(2,1)S(1)}, bf16[1280,256]{1,0:T(8,128)(2,1)S(1)}, u32[]{:S(2)}, u32[]{:S(2)}) collective-permute-start(bf16[1280,256]{1,0:T(8,128)(2,1)S(1)} %collective-permute-done.3.refs_1_.refs_6_.refs_5_), channel_id=1, source_target_pairs={{0,1},{1,0},{2,3},{3,2},{4,5},{5,4},{6,7},{7,6},{8,9},{9,8},{10,11... | collective-permute-start | bytes 1966088 | tf_op jit(solution)/shard_map/ppermute | solution.py:251
  53.1 10.0 %collective-permute-start.6 = (bf16[1280,256]{1,0:T(8,128)(2,1)S(1)}, bf16[1280,256]{1,0:T(8,128)(2,1)S(1)}, u32[]{:S(2)}, u32[]{:S(2)}) collective-permute-start(bf16[1280,256]{1,0:T(8,128)(2,1)S(1)} %collective-permute-done.4.refs_2_.refs_7_.refs_6_), channel_id=1, source_target_pairs={{0,1},{1,0},{2,3},{3,2},{4,5},{5,4},{6,7},{7,6},{8,9},{9,8},{10,11... | collective-permute-start | bytes 1966088 | tf_op jit(solution)/shard_map/ppermute | solution.py:252
  53.6 9.4 %collective-permute-start.7 = (bf16[512,256]{1,0:T(8,128)(2,1)S(1)}, bf16[512,256]{1,0:T(8,128)(2,1)S(1)}, u32[]{:S(2)}, u32[]{:S(2)}) collective-permute-start(bf16[512,256]{1,0:T(8,128)(2,1)S(1)} %copy-done), channel_id=1, source_target_pairs={{0,2},{2,4},{4,6},{6,0},{1,3},{3,5},{5,7},{7,1},{8,10},{10,12},{12... | collective-permute-start | bytes 786440 | tf_op jit(solution)/shard_map/ppermute | solution.py:243
  54.2 8.8 %collective-permute-start.8 = (bf16[512,256]{1,0:T(8,128)(2,1)S(1)}, bf16[512,256]{1,0:T(8,128)(2,1)S(1)}, u32[]{:S(2)}, u32[]{:S(2)}) collective-permute-start(bf16[512,256]{1,0:T(8,128)(2,1)S(1)} %copy-done), channel_id=1, source_target_pairs={{0,6},{2,0},{4,2},{6,4},{1,7},{3,1},{5,3},{7,5},{8,14},{10,8},{12,... | collective-permute-start | bytes 786440 | tf_op jit(solution)/shard_map/ppermute | solution.py:244
  63.0 14.4 %collective-permute-start.13 = (bf16[512,256]{1,0:T(8,128)(2,1)S(1)}, bf16[512,256]{1,0:T(8,128)(2,1)S(1)}, u32[]{:S(2)}, u32[]{:S(2)}) collective-permute-start(bf16[512,256]{1,0:T(8,128)(2,1)S(1)} %collective-permute-done.7.refs_0_), channel_id=1, source_target_pairs={{0,2},{2,4},{4,6},{6,0},{1,3},{3,5},{5,7},{7,1},{8,10},{10,12},{12... | collective-permute-start | bytes 786440 | tf_op jit(solution)/shard_map/ppermute | solution.py:256
  74.2 16.6 %collective-permute-start.11 = (bf16[64,512]{1,0:T(8,128)(2,1)S(1)}, bf16[64,512]{1,0:T(8,128)(2,1)S(1)}, u32[]{:S(2)}, u32[]{:S(2)}) collective-permute-start(bf16[64,512]{1,0:T(8,128)(2,1)S(1)} %get-tuple-element.39), channel_id=1, source_target_pairs={{0,6},{2,0},{4,2},{6,4},{1,7},{3,1},{5,3},{7,5},{8,14},{10,8},{12,... | collective-permute-start | bytes 196616 | tf_op jit(solution)/shard_map/ppermute | solution.py:258
  77.5 13.4 %collective-permute-start.12 = (bf16[64,512]{1,0:T(8,128)(2,1)S(1)}, bf16[64,512]{1,0:T(8,128)(2,1)S(1)}, u32[]{:S(2)}, u32[]{:S(2)}) collective-permute-start(bf16[64,512]{1,0:T(8,128)(2,1)S(1)} %get-tuple-element.40), channel_id=1, source_target_pairs={{0,2},{2,4},{4,6},{6,0},{1,3},{3,5},{5,7},{7,1},{8,10},{10,12},{12... | collective-permute-start | bytes 196616 | tf_op jit(solution)/shard_map/ppermute | solution.py:259
  84.1 6.8 %collective-permute-start.14 = (bf16[64,512]{1,0:T(8,128)(2,1)S(1)}, bf16[64,512]{1,0:T(8,128)(2,1)S(1)}, u32[]{:S(2)}, u32[]{:S(2)}) collective-permute-start(bf16[64,512]{1,0:T(8,128)(2,1)S(1)} %shard_map.104), channel_id=1, source_target_pairs={{0,4},{2,6},{4,0},{6,2},{1,5},{3,7},{5,1},{7,3},{8,12},{10,14},{12... | collective-permute-start | bytes 196616 | tf_op jit(solution)/shard_map/ppermute | solution.py:261
